TPU v7x, 32 devices: a whole 2x2x4 slice. The times are simulated.
32 devices in a mesh: fsdp: 16 (over z, x, core), tp: 2 (over y).
Axes of the slice: x: 2, y: 2, z: 4, core: 2. Of those that a mesh axis runs over, the one named last changes fastest.
Arguments:
- hidden: bfloat16 [16384, 768], P(('fsdp', 'tp')), may hold values from -6 to 6
- prev_logits: float32 [16384, 12], P(('fsdp', 'tp')), may hold values from -4 to 4
- routes: int32 [16384, 2], P(('fsdp', 'tp')), may hold values from 0 to 11, as said below
- slot_rank: int32 [16384, 2], P(('fsdp', 'tp')), may hold values from 0 to 191, as said below
- dropped: int32 [16384, 2], P(('fsdp', 'tp')), may hold values from 0 to 1, as said below
- cotangent: bfloat16 [16384, 768], P(('fsdp', 'tp')), may hold values from -6 to 6
- attn_norm: bfloat16 [768], P(('fsdp', 'tp')), may hold values from 0.5 to 1.5
- ffn_norm: bfloat16 [768], P(('fsdp', 'tp')), may hold values from 0.5 to 1.5
- w_qkv: bfloat16 [768, 3, 768], P('fsdp', None, 'tp'), may hold values from -0.21875 to 0.21875
- w_attn_out: bfloat16 [768, 768], P('fsdp', 'tp'), may hold values from -0.875 to 0.875
- w_router: bfloat16 [768, 12], P(('fsdp', 'tp')), may hold values from -0.109375 to 0.109375
- w_const_gate: bfloat16 [768, 4], P(('fsdp', 'tp')), may hold values from -0.21875 to 0.21875
- w_const_value: bfloat16 [768, 2], P(('fsdp', 'tp')), may hold values from -5 to 5
- w_expert_in: bfloat16 [8, 768, 2, 2048], P(None, 'fsdp', None, 'tp'), may hold values from -0.21875 to 0.21875
- w_expert_out: bfloat16 [8, 768, 2048], P(None, 'fsdp', 'tp'), may hold values from -0.25 to 0.25
Outputs:
- output: bfloat16 [16384, 768], P(('fsdp', 'tp'))
- grad_hidden: float32 [16384, 768], P(('fsdp', 'tp'))
- grad_attn_norm: float32 [768], P(('fsdp', 'tp'))
- grad_ffn_norm: float32 [768], P(('fsdp', 'tp'))
- grad_qkv: float32 [768, 3, 768], P('fsdp', None, 'tp')
- grad_attn_out: float32 [768, 768], P('fsdp', 'tp')
- grad_router: float32 [768, 12], P(('fsdp', 'tp'))
- grad_const_gate: float32 [768, 4], P(('fsdp', 'tp'))
- grad_const_value: float32 [768, 2], P(('fsdp', 'tp'))
- grad_expert_in: float32 [8, 768, 2, 2048], P(None, 'fsdp', None, 'tp')
- grad_expert_out: float32 [8, 768, 2048], P(None, 'fsdp', 'tp')
Inputs may be any that keep to these rules, and one draw needn't show every extreme that they name: `routes`: each token names two different experts; experts 0 to 7 are feed-forward, 8 the zero expert, 9 the copy expert, 10 and 11 the constant ones. `slot_rank`: for a kept pair to a feed-forward expert: the number of earlier pairs of its sequence kept by the same expert (tokens in order, a token's first expert before its second), so that kept pairs of one expert fill slots 0 upward without gaps; 0 for all other pairs. `dropped`: 1 exactly for pairs to a feed-forward expert that come after 192 earlier pairs of their sequence to that expert.
All inputs are finite; a program needn't handle non-finite values.
Results may differ from a plain program's by a relative error of at most 0.018.
Values may be sent and summed in bfloat16 or wider, within the bound.
A program may use at most 256 MiB of HBM per device.

v0:
```python
import jax
import jax.numpy as jnp
from jax import lax
from jax.sharding import PartitionSpec as P

HD = 64
BLOCK = 256


PRECISE = lax.Precision.HIGHEST
EPSILON = 1e-06
MASKED_SCORE = -1e30


def rms_norm(values, gain):
    return values * lax.rsqrt(jnp.mean(values * values, axis=-1, keepdims=True) + EPSILON) * gain


def rotate(heads):
    length, half_dim = (heads.shape[0], heads.shape[2] // 2)
    positions = jnp.arange(length).astype(jnp.float32)
    inverse = jnp.power(10000.0, -jnp.arange(half_dim).astype(jnp.float32) / half_dim)
    angles = positions[:, None] * inverse[None, :]
    cosine = jnp.cos(angles)[:, None, :]
    sine_part = jnp.sin(angles)[:, None, :]
    lower_half, upper_half = (heads[..., :half_dim], heads[..., half_dim:])
    return jnp.concatenate(
        [
            lower_half * cosine - upper_half * sine_part,
            upper_half * cosine + lower_half * sine_part,
        ],
        axis=-1,
    )


def soft_last(scores):
    highest = jnp.max(scores, axis=-1, keepdims=True)
    expanded = jnp.exp(scores - highest)
    return expanded / jnp.sum(expanded, axis=-1, keepdims=True)


def swiglu(gate_part, up_part):
    return gate_part / (1.0 + jnp.exp(-gate_part)) * up_part


def gather_rows(values):
    return lax.all_gather(values, "tp", axis=0, tiled=True)


def sum_rows(values):
    return lax.psum_scatter(
        values.astype(jnp.bfloat16), "tp", scatter_dimension=0, tiled=True
    ).astype(jnp.float32)


def fetch_attention(w_qkv, w_attn_out):
    return (
        lax.all_gather(w_qkv, "fsdp", axis=0, tiled=True),
        lax.all_gather(w_attn_out, "fsdp", axis=0, tiled=True),
    )


def fetch_experts(w_expert_in, w_expert_out):
    return (
        lax.all_gather(w_expert_in, "fsdp", axis=1, tiled=True),
        lax.all_gather(w_expert_out, "fsdp", axis=1, tiled=True),
    )


def query_blocks(length):
    base_rows = BLOCK * max(1, 512 // BLOCK)
    block_count = max(1, min(8, length // base_rows))
    return (block_count, length // block_count)


def allowed_mask(row_start, row_count, key_stop):
    query_block = (row_start + jnp.arange(row_count)) // BLOCK
    key_block = jnp.arange(key_stop) // BLOCK
    return key_block[None, :] <= query_block[:, None]


def logit_grad(gate_pair, gate_grad, route_ids, route_count):
    local_grad = gate_pair * (gate_grad - jnp.sum(gate_pair * gate_grad, axis=-1, keepdims=True))
    columns = jnp.arange(route_count)
    return jnp.sum(
        jnp.where(route_ids[:, :, None] == columns[None, None, :], local_grad[:, :, None], 0.0),
        axis=1,
    )


def special_mix(normed, gate_matrix, value_table, gate_pair, routes, experts):
    const_weights = soft_last(jnp.dot(normed, gate_matrix, precision=PRECISE).reshape(-1, 2, 2))
    constants = (
        const_weights[:, :, 0:1] * normed[:, None, :]
        + const_weights[:, :, 1:2] * value_table.T[None, :, :]
    )
    mixture = jnp.zeros_like(normed)
    for member in range(2):
        route_col = routes[:, member][:, None]
        branch = jnp.where(route_col == experts + 1, normed, 0.0)
        branch = branch + jnp.where(route_col == experts + 2, constants[:, 0], 0.0)
        branch = branch + jnp.where(route_col == experts + 3, constants[:, 1], 0.0)
        mixture = mixture + gate_pair[:, member : member + 1] * branch
    return mixture


def shards(
    hidden,
    prev_logits,
    routes,
    slot_rank,
    dropped,
    cotangent,
    attn_norm,
    ffn_norm,
    w_qkv,
    w_attn_out,
    w_router,
    w_const_gate,
    w_const_value,
    w_expert_in,
    w_expert_out,
):
    own_rows = hidden.shape[0]
    width = hidden.shape[1]
    length = own_rows * lax.axis_size("tp")
    experts = w_expert_in.shape[0]
    route_count = w_router.shape[1]
    capacity = 9 * length // (4 * route_count)
    slot_total = experts * capacity
    scaling = HD ** (-0.5)
    gain_one, gain_two, router, gate_small, value_small = (
        lax.all_gather(attn_norm, ("fsdp", "tp"), axis=0, tiled=True),
        lax.all_gather(ffn_norm, ("fsdp", "tp"), axis=0, tiled=True),
        lax.all_gather(w_router, ("fsdp", "tp"), axis=0, tiled=True),
        lax.all_gather(w_const_gate, ("fsdp", "tp"), axis=0, tiled=True),
        lax.all_gather(w_const_value, ("fsdp", "tp"), axis=0, tiled=True),
    )
    gain_one = gain_one.astype(jnp.float32)
    gain_two = gain_two.astype(jnp.float32)
    router_wide = router.astype(jnp.float32)
    gate_matrix = gate_small.astype(jnp.float32)
    value_table = value_small.astype(jnp.float32)
    hidden_wide = hidden.astype(jnp.float32)
    normed_one, back_one = jax.vjp(rms_norm, hidden_wide, gain_one)
    stream_one = gather_rows(normed_one.astype(jnp.bfloat16))
    qkv_full, attn_full = fetch_attention(w_qkv, w_attn_out)
    local_heads = qkv_full.shape[2] // HD
    projected = jnp.dot(
        stream_one, qkv_full.reshape(width, -1), preferred_element_type=jnp.float32
    ).reshape(length, 3, local_heads, HD)
    query_pre = projected[:, 0]
    key_pre = projected[:, 1]
    values_all = projected[:, 2].astype(jnp.bfloat16)
    queries = rotate(query_pre).astype(jnp.bfloat16)
    keys_rot = rotate(key_pre).astype(jnp.bfloat16)
    block_count, block_rows = query_blocks(length)
    mixed_parts = []
    log_sums = []
    for block_no in range(block_count):
        row_start = block_no * block_rows
        key_stop = row_start + block_rows
        allowed = allowed_mask(row_start, block_rows, key_stop)
        scores = (
            jnp.einsum(
                "qhd,khd->hqk",
                queries[row_start:key_stop],
                keys_rot[:key_stop],
                preferred_element_type=jnp.float32,
            )
            * scaling
        )
        scores = jnp.where(allowed[None], scores, MASKED_SCORE)
        highest = jnp.max(scores, axis=-1, keepdims=True)
        expanded = jnp.exp(scores - highest)
        totals = jnp.sum(expanded, axis=-1, keepdims=True)
        attn_probs = (expanded / totals).astype(jnp.bfloat16)
        mixed_parts.append(
            jnp.einsum(
                "hqk,khd->qhd",
                attn_probs,
                values_all[:key_stop],
                preferred_element_type=jnp.float32,
            ).astype(jnp.bfloat16)
        )
        log_sums.append(highest + jnp.log(totals))
    mixed = jnp.concatenate(mixed_parts, axis=0).reshape(length, -1)
    attended = sum_rows(
        jnp.einsum("tf,df->td", mixed, attn_full, preferred_element_type=jnp.float32)
    )
    residual_mid = hidden_wide + attended
    normed_two, back_two = jax.vjp(rms_norm, residual_mid, gain_two)
    stream_own = normed_two.astype(jnp.bfloat16)
    logits = jnp.dot(stream_own, router, preferred_element_type=jnp.float32) + prev_logits
    gates_own = soft_last(jnp.take_along_axis(logits, routes, axis=1))
    stream_two = gather_rows(stream_own)
    routes_all, rank_all, dropped_all = (
        lax.all_gather(routes, "tp", axis=0, tiled=True),
        lax.all_gather(slot_rank, "tp", axis=0, tiled=True),
        lax.all_gather(dropped, "tp", axis=0, tiled=True),
    )
    gates_all = lax.all_gather(gates_own, "tp", axis=0, tiled=True)
    slot_index = routes_all * capacity + rank_all
    kept_pair = (routes_all < experts) & (dropped_all == 0)
    safe_index = jnp.clip(slot_index, 0, slot_total - 1)
    slot_range = jnp.arange(slot_total)
    slot_hits = [
        (slot_index[:, member][None, :] == slot_range[:, None]) & kept_pair[:, member][None, :]
        for member in range(2)
    ]
    dispatch = (slot_hits[0] | slot_hits[1]).astype(jnp.bfloat16)
    packed = (
        jnp.dot(dispatch, stream_two, preferred_element_type=jnp.float32)
        .astype(jnp.bfloat16)
        .reshape(experts, capacity, width)
    )
    in_full, out_full = fetch_experts(w_expert_in, w_expert_out)
    both_parts = jnp.einsum("ecd,edjf->ecjf", packed, in_full, preferred_element_type=jnp.float32)
    gate_part = both_parts[:, :, 0]
    up_part = both_parts[:, :, 1]
    activated = swiglu(gate_part, up_part).astype(jnp.bfloat16)
    results = jnp.einsum(
        "ecf,edf->ecd", activated, out_full, preferred_element_type=jnp.float32
    ).reshape(slot_total, width)
    picked = [
        jnp.where(
            kept_pair[:, member][:, None], jnp.take(results, safe_index[:, member], axis=0), 0.0
        )
        for member in range(2)
    ]
    ffn_partial = gates_all[:, 0:1] * picked[0] + gates_all[:, 1:2] * picked[1]

    def local_mix(normed, gate_weights, value_weights, gate_pair):
        return special_mix(normed, gate_weights, value_weights, gate_pair, routes, experts)

    special, back_special = jax.vjp(local_mix, normed_two, gate_matrix, value_table, gates_own)
    output = (residual_mid + sum_rows(ffn_partial) + special).astype(jnp.bfloat16)
    qkv_back, attn_back = fetch_attention(w_qkv, w_attn_out)
    in_back, out_back = fetch_experts(w_expert_in, w_expert_out)
    grad_wide = cotangent.astype(jnp.float32)
    grad_mix_all = gather_rows(cotangent)
    grad_mix_wide = grad_mix_all.astype(jnp.float32)
    gate_grad = jnp.stack(
        [jnp.sum(picked[member] * grad_mix_wide, axis=-1) for member in range(2)], axis=1
    )
    slot_gate = jnp.sum(jnp.where(slot_hits[0], gates_all[:, 0][None, :], 0.0), axis=1) + jnp.sum(
        jnp.where(slot_hits[1], gates_all[:, 1][None, :], 0.0), axis=1
    )
    grad_results = (
        (jnp.dot(dispatch, grad_mix_all, preferred_element_type=jnp.float32) * slot_gate[:, None])
        .astype(jnp.bfloat16)
        .reshape(experts, capacity, width)
    )
    glu_back = jax.vjp(swiglu, gate_part, up_part)[1]
    grad_out_exp = jnp.einsum(
        "ecf,ecd->edf", activated, grad_results, preferred_element_type=jnp.float32
    )
    grad_act = jnp.einsum(
        "ecd,edf->ecf", grad_results, out_back, preferred_element_type=jnp.float32
    )
    grad_gate_part, grad_up_part = glu_back(grad_act)
    grad_both = jnp.stack([grad_gate_part, grad_up_part], axis=2).astype(jnp.bfloat16)
    grad_in_exp = jnp.einsum(
        "ecd,ecjf->edjf", packed, grad_both, preferred_element_type=jnp.float32
    )
    grad_packed = jnp.einsum(
        "ecjf,edjf->ecd", grad_both, in_back, preferred_element_type=jnp.float32
    ).reshape(slot_total, width)
    grad_logit_all = logit_grad(gates_all, gate_grad, routes_all, route_count)
    grad_stream_two = jnp.dot(grad_logit_all, router_wide.T, precision=PRECISE)
    for member in range(2):
        grad_stream_two = grad_stream_two + jnp.where(
            kept_pair[:, member][:, None], jnp.take(grad_packed, safe_index[:, member], axis=0), 0.0
        )
    grad_normed_spec, grad_gate_matrix, grad_value_table, grad_gate_spec = back_special(grad_wide)
    grad_logit_own = logit_grad(gates_own, grad_gate_spec, routes, route_count)
    grad_router = jnp.einsum(
        "td,tr->dr", stream_two.astype(jnp.float32), grad_logit_all, precision=PRECISE
    ) + jnp.einsum("td,tr->dr", stream_own.astype(jnp.float32), grad_logit_own, precision=PRECISE)
    grad_normed_two = (
        sum_rows(grad_stream_two)
        + grad_normed_spec
        + jnp.dot(grad_logit_own, router_wide.T, precision=PRECISE)
    )
    grad_mid, grad_gain_two = back_two(grad_normed_two)
    grad_mid = grad_mid + grad_wide
    grad_attended = gather_rows(grad_mid.astype(jnp.bfloat16))
    grad_attn_out = jnp.einsum(
        "td,tf->df", grad_attended, mixed, preferred_element_type=jnp.float32
    )
    grad_mixed = (
        jnp.dot(grad_attended, attn_back, preferred_element_type=jnp.float32)
        .astype(jnp.bfloat16)
        .reshape(length, local_heads, HD)
    )
    grad_values = jnp.zeros((length, local_heads, HD), jnp.float32)
    grad_keys = jnp.zeros((length, local_heads, HD), jnp.float32)
    grad_query_parts = []
    for block_no in range(block_count):
        row_start = block_no * block_rows
        key_stop = row_start + block_rows
        allowed = allowed_mask(row_start, block_rows, key_stop)
        scores = (
            jnp.einsum(
                "qhd,khd->hqk",
                queries[row_start:key_stop],
                keys_rot[:key_stop],
                preferred_element_type=jnp.float32,
            )
            * scaling
        )
        recomputed = jnp.where(allowed[None], jnp.exp(scores - log_sums[block_no]), 0.0)
        grad_block = grad_mixed[row_start:key_stop]
        grad_probs = jnp.einsum(
            "qhd,khd->hqk", grad_block, values_all[:key_stop], preferred_element_type=jnp.float32
        )
        grad_values = grad_values.at[:key_stop].add(
            jnp.einsum(
                "hqk,qhd->khd",
                recomputed.astype(jnp.bfloat16),
                grad_block,
                preferred_element_type=jnp.float32,
            )
        )
        grad_scores = (
            recomputed * (grad_probs - jnp.sum(recomputed * grad_probs, axis=-1, keepdims=True))
        ).astype(jnp.bfloat16)
        grad_query_parts.append(
            jnp.einsum(
                "hqk,khd->qhd", grad_scores, keys_rot[:key_stop], preferred_element_type=jnp.float32
            )
            * scaling
        )
        grad_keys = grad_keys.at[:key_stop].add(
            jnp.einsum(
                "hqk,qhd->khd",
                grad_scores,
                queries[row_start:key_stop],
                preferred_element_type=jnp.float32,
            )
            * scaling
        )
    grad_query_pre = jax.vjp(rotate, query_pre)[1](jnp.concatenate(grad_query_parts, axis=0))[0]
    grad_key_pre = jax.vjp(rotate, key_pre)[1](grad_keys)[0]
    grad_projected = (
        jnp.stack([grad_query_pre, grad_key_pre, grad_values], axis=1)
        .astype(jnp.bfloat16)
        .reshape(length, -1)
    )
    grad_qkv = jnp.einsum(
        "td,tf->df", stream_one, grad_projected, preferred_element_type=jnp.float32
    ).reshape(width, 3, -1)
    grad_stream_one = jnp.einsum(
        "tf,df->td", grad_projected, qkv_back.reshape(width, -1), preferred_element_type=jnp.float32
    )
    grad_hidden_one, grad_gain_one = back_one(sum_rows(grad_stream_one))
    grad_hidden = grad_mid + grad_hidden_one
    grad_qkv, grad_attn_out = (
        lax.psum_scatter(grad_qkv, "fsdp", scatter_dimension=0, tiled=True),
        lax.psum_scatter(grad_attn_out, "fsdp", scatter_dimension=0, tiled=True),
    )
    grad_in_exp, grad_out_exp = (
        lax.psum_scatter(grad_in_exp, "fsdp", scatter_dimension=1, tiled=True),
        lax.psum_scatter(grad_out_exp, "fsdp", scatter_dimension=1, tiled=True),
    )
    grad_gain_one, grad_gain_two, grad_router, grad_gate_matrix, grad_value_table = (
        lax.psum_scatter(grad_gain_one, ("fsdp", "tp"), scatter_dimension=0, tiled=True),
        lax.psum_scatter(grad_gain_two, ("fsdp", "tp"), scatter_dimension=0, tiled=True),
        lax.psum_scatter(grad_router, ("fsdp", "tp"), scatter_dimension=0, tiled=True),
        lax.psum_scatter(grad_gate_matrix, ("fsdp", "tp"), scatter_dimension=0, tiled=True),
        lax.psum_scatter(grad_value_table, ("fsdp", "tp"), scatter_dimension=0, tiled=True),
    )
    return (
        output,
        grad_hidden,
        grad_gain_one,
        grad_gain_two,
        grad_qkv,
        grad_attn_out,
        grad_router,
        grad_gate_matrix,
        grad_value_table,
        grad_in_exp,
        grad_out_exp,
    )


def solution(mesh):
    in_specs = (
        P(("fsdp", "tp"), None),
        P(("fsdp", "tp"), None),
        P(("fsdp", "tp"), None),
        P(("fsdp", "tp"), None),
        P(("fsdp", "tp"), None),
        P(("fsdp", "tp"), None),
        P(("fsdp", "tp")),
        P(("fsdp", "tp")),
        P("fsdp", None, "tp"),
        P("fsdp", "tp"),
        P(("fsdp", "tp"), None),
        P(("fsdp", "tp"), None),
        P(("fsdp", "tp"), None),
        P(None, "fsdp", None, "tp"),
        P(None, "fsdp", "tp"),
    )
    out_specs = (
        P(("fsdp", "tp"), None),
        P(("fsdp", "tp"), None),
        P(("fsdp", "tp")),
        P(("fsdp", "tp")),
        P("fsdp", None, "tp"),
        P("fsdp", "tp"),
        P(("fsdp", "tp"), None),
        P(("fsdp", "tp"), None),
        P(("fsdp", "tp"), None),
        P(None, "fsdp", None, "tp"),
        P(None, "fsdp", "tp"),
    )
    return jax.shard_map(shards, mesh=mesh, in_specs=in_specs, out_specs=out_specs, check_vma=False)
```

profile of v0, /device:TPU:12, one launch (start us, length us, event | category | flops | bytes accessed | tf_op | source)
XLA Modules:
  0.0 1536.9 jit_solution(649618837494953291)
XLA Ops:
  9.7 41.5 %all-reduce.22 = (bf16[768]{0:T(1024)(128)(2,1)S(1)}, bf16[768]{0:T(1024)(128)(2,1)S(1)}) all-reduce(bf16[768]{0:T(1024)(128)(2,1)S(1)} %dynamic-update-slice.10, bf16[768]{0:T(1024)(128)(2,1)S(1)} %dynamic-update-slice.11), channel_id=1, replica_groups=mesh['fsdp'=16,'tp'=2] {'fsdp','tp'}, use_global_device_ids=true, to_apply=%add.14 | all-reduce | flops 1536 | bytes 6144
  53.7 2.3 fusion.36
  57.3 18.9 %all_gather.58 = bf16[768,384]{1,0:T(8,128)(2,1)S(1)} all-gather(bf16[48,384]{1,0:T(8,128)(2,1)S(1)} %copy-done.59), channel_id=1, replica_groups=mesh['fsdp'=16,'tp'=2] {'fsdp'}, dimensions={0}, use_global_device_ids=true | all-gather | bytes 626688 | tf_op jit(solution)/shard_map/all_gather | solution.py:59
  76.2 2.8 copy.140
  79.0 2.5 all-gather.11.cloned.1.call-done
  81.5 3.4 fusion.119
  87.3 2.4 select_reduce_fusion
  93.3 3.8 fusion.2
  97.1 4.0 fusion.67
  102.2 2.2 convolution_convert_fusion.1
  105.0 25.6 %reduce-scatter.12.cloned.1.call-done = bf16[512,768]{1,0:T(8,128)(2,1)} async-done(((bf16[1024,768]{1,0:T(8,128)(2,1)}), bf16[512,768]{1,0:T(8,128)(2,1)}) %reduce-scatter.12.cloned.1.call-update) | async-done | bytes 786448 | tf_op jit(solution)/shard_map/reduce_scatter | solution.py:51
  132.1 2.3 fusion.112
  134.6 3.0 copy.145
  138.4 52.8 %all-gather.2 = bf16[32,24,2]{1,2,0:T(2,128)(2,1)S(1)} all-gather(bf16[1,24,2]{1,2,0:T(2,128)(2,1)S(1)} %bitcast.268), channel_id=1, replica_groups=mesh['fsdp'=16,'tp'=2] {'fsdp','tp'}, dimensions={0}, use_global_device_ids=true | all-gather | bytes 3168 | tf_op jit(solution)/shard_map/all_gather | solution.py:137
  191.5 67.1 %all-gather.1 = bf16[32,24,4]{1,2,0:T(4,128)(2,1)S(1)} all-gather(bf16[1,24,4]{1,2,0:T(4,128)(2,1)S(1)} %bitcast.267), channel_id=1, replica_groups=mesh['fsdp'=16,'tp'=2] {'fsdp','tp'}, dimensions={0}, use_global_device_ids=true | all-gather | bytes 6336 | tf_op jit(solution)/shard_map/all_gather | solution.py:136
  258.7 64.9 %all-gather = bf16[32,24,12]{1,2,0:T(8,128)(2,1)S(1)} all-gather(bf16[1,24,12]{1,2,0:T(8,128)(2,1)S(1)} %bitcast.260), channel_id=1, replica_groups=mesh['fsdp'=16,'tp'=2] {'fsdp','tp'}, dimensions={0}, use_global_device_ids=true | all-gather | bytes 19008 | tf_op jit(solution)/shard_map/all_gather | solution.py:135
  324.2 4.3 all_gather.62
  328.5 4.3 all_gather.64
  332.9 4.3 all_gather.63
  341.9 8.7 gather_fusion
  351.8 2.5 fusion.50
  354.4 4.3 all_gather.61
  361.4 7.1 multiply_convert_fusion.4
  368.5 6.7 convolution_convert_fusion
  375.2 14.3 fusion.120
  389.4 33.8 %all-gather.19.cloned.1.call-done = bf16[8,768,1024]{2,1,0:T(8,128)(2,1)} async-done(((bf16[8,48,1024]{2,1,0:T(8,128)(2,1)}), bf16[8,768,1024]{2,1,0:T(8,128)(2,1)}) %all-gather.19.cloned.1.call-update) | async-done | bytes 12582928 | tf_op jit(solution)/shard_map/all_gather | solution.py:66
  423.2 13.8 fusion.25
  437.1 16.3 %fusion = f32[8,192,768,1]{2,1,0,3:T(8,128)} fusion(bf16[8,768,2,1024]{3,1,2,0:T(8,128)(2,1)} %all-gather.17.cloned.1.call-done, bf16[8,192,1,1024]{3,1,0,2:T(8,128)(2,1)} %get-tuple-element.184, bf16[8,192,1,1024]{3,1,0,2:T(8,128)(2,1)} %get-tuple-element.183), kind=kOutput, calls=%fused_computation.5 | convolution fusion | flops 4834983936 | bytes 36175872 | tf_op jit(solution)/shard_map/ecjf,edjf->ecd/dot_general | solution.py:266
  453.3 8.2 gather_fusion.4
  461.6 8.4 gather_fusion.3
  469.9 12.1 fusion.121
  482.0 8.2 gather_fusion.1
  490.2 8.2 gather_fusion.2
  498.4 6.8 fusion.15
  505.5 3.5 fusion.19
  509.8 2.7 multiply_reduce_fusion.2
  512.8 2.0 fusion.123
  514.8 18.9 %reduce-scatter.16.cloned.1.call-done = bf16[512,768]{1,0:T(8,128)(2,1)} async-done(((bf16[1024,768]{1,0:T(8,128)(2,1)}), bf16[512,768]{1,0:T(8,128)(2,1)}) %reduce-scatter.16.cloned.1.call-update) | async-done | bytes 786448 | tf_op jit(solution)/shard_map/reduce_scatter | solution.py:51
  533.8 4.4 multiply_reduce_fusion.6
  542.2 26.1 %all-gather.23.cloned.1.call-done = bf16[1024,768]{1,0:T(8,128)(2,1)} async-done(((bf16[512,768]{1,0:T(8,128)(2,1)}), bf16[1024,768]{1,0:T(8,128)(2,1)}) %all-gather.23.cloned.1.call-update) | async-done | bytes 1572880 | tf_op jit(solution)/shard_map/all_gather | solution.py:47
  568.3 2.5 convolution_convert_fusion.3
  571.7 5.2 fusion.59
  576.9 6.4 multiply_reduce_fusion.1
  583.3 6.5 multiply_convert_fusion.1
  589.8 3.3 fusion.62
  593.1 2.7 fusion.64
  595.8 9.1 multiply_reduce_fusion
  604.9 2.9 fusion.56
  607.9 7.0 multiply_convert_fusion
  614.9 2.0 fusion.63
  620.8 3.5 convolution_convert_fusion.2
  625.1 22.0 %fusion.4 = f32[8,768,2,1024]{3,1,2,0:T(8,128)} fusion(bf16[8,192,768,1]{2,1,3,0:T(8,128)(2,1)} %bitcast.222, bf16[8,192,1,1024]{3,1,0,2:T(8,128)(2,1)} %get-tuple-element.184, bf16[8,192,1,1024]{3,1,0,2:T(8,128)(2,1)} %get-tuple-element.183), kind=kOutput, calls=%fused_computation.18 | convolution fusion | flops 4834983936 | bytes 58982400 | tf_op jit(solution)/shard_map/ecd,ecjf->edjf/dot_general | solution.py:263
  647.1 3.7 fusion.124
  650.9 6.1 fusion.54
  657.1 14.5 fusion.127
  673.2 2.2 fusion.125
  676.6 1.9 fusion.37
  678.5 42.8 %all-reduce.21 = (f32[768]{0:T(1024)S(1)}, f32[768]{0:T(1024)S(1)}, f32[768,12]{0,1:T(8,128)S(1)}, f32[768,4]{0,1:T(4,128)S(1)}, f32[768,2]{0,1:T(2,128)S(1)}) all-reduce(f32[768]{0:T(1024)S(1)} %get-tuple-element.148, f32[768]{0:T(1024)} %get-tuple-element.146, ...), channel_id=6, replica_groups=mesh['fsdp'=16,'tp'=2] {'fsdp','tp'}, use_global_device_ids=true, to_apply=%region_35.37.clone | all-reduce | flops 15360 | bytes 122880
  725.1 6.1 fusion.47
  731.2 418.9 %reduce-scatter.24.cloned.1.call-done = f32[8,48,2,1024]{3,1,2,0:T(8,128)} async-done(((f32[8,768,2,1024]{3,1,2,0:T(8,128)}), f32[8,48,2,1024]{3,1,2,0:T(8,128)}) %reduce-scatter.24.cloned.1.call-update) | async-done | bytes 3145744 | tf_op jit(solution)/shard_map/reduce_scatter | solution.py:363
  1150.2 6.0 copy.156
  1156.1 56.9 %reduce-scatter.22.cloned.1.call-done = f32[48,384]{1,0:T(8,128)} async-done(((f32[768,384]{1,0:T(8,128)}), f32[48,384]{1,0:T(8,128)}) %reduce-scatter.22.cloned.1.call-update) | async-done | bytes 73744 | tf_op jit(solution)/shard_map/reduce_scatter | solution.py:360
  1213.1 70.9 %reduce-scatter.20.cloned.1.call-done = f32[48,3,384]{2,0,1:T(8,128)} async-done(((f32[768,3,384]{2,0,1:T(8,128)}), f32[48,3,384]{2,0,1:T(8,128)}) %reduce-scatter.20.cloned.1.call-update) | async-done | bytes 221200 | tf_op jit(solution)/shard_map/reduce_scatter | solution.py:359
  1284.0 246.2 %reduce-scatter.26.cloned.1.call-done = f32[8,48,1024]{2,1,0:T(8,128)} async-done(((f32[8,768,1024]{2,1,0:T(8,128)}), f32[8,48,1024]{2,1,0:T(8,128)}) %reduce-scatter.26.cloned.1.call-update) | async-done | bytes 1572880 | tf_op jit(solution)/shard_map/reduce_scatter | solution.py:364
  (321 shorter events, 42.5 us)
Async XLA Ops:
  7.2 50.1 %copy-start.59 = (bf16[48,384]{1,0:T(8,128)(2,1)S(1)}, bf16[48,384]{1,0:T(8,128)(2,1)}, u32[]{:S(2)}) copy-start(bf16[48,384]{1,0:T(8,128)(2,1)} %param.38) | copy-start | bytes 110596
  7.2 69.0 %all-gather.13.cloned.1.call-start = ((), (), s32[]{:S(2)}) async-start(), calls=%async_computation.9 | async-start | bytes 1880064 | tf_op jit(solution)/shard_map/all_gather | solution.py:58
  7.9 73.6 %all-gather.11.cloned.1.call-start = ((), (), s32[]{:S(2)}) async-start(), calls=%async_computation.8 | async-start | bytes 2359296 | tf_op jit(solution)/shard_map/all_gather | solution.py:47
  56.0 74.6 %reduce-scatter.12.cloned.1.call-start = ((), (), s32[]{:S(2)}) async-start(), calls=%async_computation.10 | async-start | bytes 2359296 | tf_op jit(solution)/shard_map/reduce_scatter | solution.py:51
  56.3 34.7 %copy-start.13 = (pred[512,512]{0,1:T(8,128)(4,1)}, pred[512,512]{0,1:T(8,128)(4,1)S(1)}, u32[]{:S(2)}) copy-start(pred[512,512]{0,1:T(8,128)(4,1)S(1)} %broadcast_compare_fusion.1) | copy-start | bytes 786436
  56.8 28.5 %copy-start.28 = (f32[1024,32]{0,1:T(8,128)}, f32[1024,32]{0,1:T(8,128)S(1)}, u32[]{:S(2)}) copy-start(f32[1024,32]{0,1:T(8,128)S(1)} %get-tuple-element.219) | copy-start | bytes 393220
  56.9 28.5 %copy-start.30 = (f32[1024,32]{0,1:T(8,128)}, f32[1024,32]{0,1:T(8,128)S(1)}, u32[]{:S(2)}) copy-start(f32[1024,32]{0,1:T(8,128)S(1)} %get-tuple-element.220) | copy-start | bytes 393220
  57.2 39.8 %copy-start.11 = (pred[512,1024]{1,0:T(8,128)(4,1)}, pred[512,1024]{1,0:T(8,128)(4,1)S(1)}, u32[]{:S(2)}) copy-start(pred[512,1024]{1,0:T(8,128)(4,1)S(1)} %broadcast_compare_fusion) | copy-start | bytes 1572868
  76.2 25.1 %copy-start.35 = (bf16[768,384]{1,0:T(8,128)(2,1)}, bf16[768,384]{1,0:T(8,128)(2,1)S(1)}, u32[]{:S(2)}) copy-start(bf16[768,384]{1,0:T(8,128)(2,1)S(1)} %all_gather.58) | copy-start | bytes 1769476
  79.0 5.9 copy-start.25
  85.0 12.1 copy-start.34
  89.7 7.4 copy-start
  89.7 7.4 copy-start.50
  101.2 29.4 %copy-start.2 = (bf16[512,768]{1,0:T(8,128)(2,1)S(1)}, bf16[512,768]{1,0:T(8,128)(2,1)}, u32[]{:S(2)}) copy-start(bf16[512,768]{1,0:T(8,128)(2,1)} %param.29) | copy-start | bytes 2359300
  104.4 257.1 %all-gather.21.cloned.1.call-start = ((), (), s32[]{:S(2)}) async-start(), calls=%async_computation.15 | async-start | bytes 2359296 | tf_op jit(solution)/shard_map/all_gather | solution.py:47
  104.9 263.6 %all-gather.15.cloned.1.call-start = ((), (), s32[]{:S(2)}) async-start(), calls=%async_computation.11 | async-start | bytes 2359296 | tf_op jit(solution)/shard_map/all_gather | solution.py:47
  105.0 29.5 %copy-start.48 = (f32[768]{0:T(1024)}, f32[768]{0:T(1024)S(1)}, u32[]{:S(2)}) copy-start(f32[768]{0:T(1024)S(1)} %convert_element_type.217) | copy-start | bytes 9220
  134.4 57.1 %copy-start.86 = (bf16[24,4]{0,1:T(4,128)(2,1)S(1)}, bf16[24,4]{0,1:T(4,128)(2,1)}, u32[]{:S(2)}) copy-start(bf16[24,4]{0,1:T(4,128)(2,1)} %param.40) | copy-start | bytes 580
  134.4 124.3 %copy-start.77 = (bf16[24,12]{0,1:T(8,128)(2,1)S(1)}, bf16[24,12]{0,1:T(8,128)(2,1)}, u32[]{:S(2)}) copy-start(bf16[24,12]{0,1:T(8,128)(2,1)} %param.39) | copy-start | bytes 1732
  134.5 189.4 %copy-start.45 = (s32[512,2]{0,1:T(2,128)S(1)}, s32[512,2]{0,1:T(2,128)}, u32[]{:S(2)}) copy-start(s32[512,2]{0,1:T(2,128)} %param.31) | copy-start | bytes 12292
  134.5 194.1 %copy-start.78 = (s32[512,2]{0,1:T(2,128)S(1)}, s32[512,2]{0,1:T(2,128)}, u32[]{:S(2)}) copy-start(s32[512,2]{0,1:T(2,128)} %param.32) | copy-start | bytes 12292
  134.5 198.4 %copy-start.79 = (s32[512,2]{0,1:T(2,128)S(1)}, s32[512,2]{0,1:T(2,128)}, u32[]{:S(2)}) copy-start(s32[512,2]{0,1:T(2,128)} %param.33) | copy-start | bytes 12292
  134.5 240.7 %all-gather.17.cloned.1.call-start = ((), (), s32[]{:S(2)}) async-start(), calls=%async_computation.12 | async-start | bytes 26738688 | tf_op jit(solution)/shard_map/all_gather | solution.py:65
  137.6 204.0 %copy-start.7 = (bf16[512,768]{1,0:T(8,128)(2,1)S(1)}, bf16[512,768]{1,0:T(8,128)(2,1)}, u32[]{:S(2)}) copy-start(bf16[512,768]{1,0:T(8,128)(2,1)} %get-tuple-element.181) | copy-start | bytes 2359300
  137.6 204.0 %copy-start.65 = (f32[512,12]{0,1:T(8,128)S(1)}, f32[512,12]{0,1:T(8,128)}, u32[]{:S(2)}) copy-start(f32[512,12]{0,1:T(8,128)} %param.30) | copy-start | bytes 73732
  137.6 285.6 %all-gather.19.cloned.1.call-start = ((), (), s32[]{:S(2)}) async-start(), calls=%async_computation.13 | async-start | bytes 13369344 | tf_op jit(solution)/shard_map/all_gather | solution.py:66
  138.4 395.4 %reduce-scatter.16.cloned.1.call-start = ((), (), s32[]{:S(2)}) async-start(), calls=%async_computation.16 | async-start | bytes 2359296 | tf_op jit(solution)/shard_map/reduce_scatter | solution.py:51
  258.7 82.0 %copy-start.56 = (bf16[768,4]{0,1:T(4,128)(2,1)}, bf16[768,4]{0,1:T(4,128)(2,1)S(1)}, u32[]{:S(2)}) copy-start(bf16[768,4]{0,1:T(4,128)(2,1)S(1)} %reshape.558) | copy-start | bytes 18436
  323.8 26.8 %copy-start.36 = (bf16[768,12]{0,1:T(8,128)(2,1)}, bf16[768,12]{0,1:T(8,128)(2,1)S(1)}, u32[]{:S(2)}) copy-start(bf16[768,12]{0,1:T(8,128)(2,1)S(1)} %reshape.556) | copy-start | bytes 55300
  328.5 22.1 %copy-start.43 = (s32[1024,2]{0,1:T(2,128)}, s32[1024,2]{0,1:T(2,128)S(1)}, u32[]{:S(2)}) copy-start(s32[1024,2]{0,1:T(2,128)S(1)} %all_gather.62) | copy-start | bytes 24580
  351.8 6.9 copy-start.80
  351.8 8.2 copy-start.81
  437.1 16.3 %copy-start.61 = (s32[1024]{0:T(1024)S(1)}, s32[1024]{0:T(1024)}, u32[]{:S(2)}) copy-start(s32[1024]{0:T(1024)} %fusion.81) | copy-start | bytes 12292
  453.3 8.2 copy-start.60
  490.2 8.2 copy-start.72
  490.2 8.2 copy-start.73
  498.4 6.9 copy-start.44
  498.4 7.0 copy-start.9
  498.4 7.0 copy-start.10
  498.4 7.0 copy-start.37
  509.0 59.4 %all-gather.23.cloned.1.call-start = ((), (), s32[]{:S(2)}) async-start(), calls=%async_computation.17 | async-start | bytes 2359296 | tf_op jit(solution)/shard_map/all_gather | solution.py:47
  509.0 24.8 %copy-start.67 = (f32[512,1]{0,1:T(1,128)}, f32[512,1]{0,1:T(1,128)S(1)}, u32[]{:S(2)}) copy-start(f32[512,1]{0,1:T(1,128)S(1)} %get-tuple-element.221) | copy-start | bytes 6148
  509.0 24.8 %copy-start.68 = (f32[512,1]{0,1:T(1,128)}, f32[512,1]{0,1:T(1,128)S(1)}, u32[]{:S(2)}) copy-start(f32[512,1]{0,1:T(1,128)S(1)} %get-tuple-element.222) | copy-start | bytes 6148
  509.8 24.0 %copy-start.3 = (bf16[512,768]{1,0:T(8,128)(2,1)S(1)}, bf16[512,768]{1,0:T(8,128)(2,1)}, u32[]{:S(2)}) copy-start(bf16[512,768]{1,0:T(8,128)(2,1)} %param.29) | copy-start | bytes 2359300
  509.8 24.0 %copy-start.49 = (f32[768]{0:T(1024)S(1)}, f32[768]{0:T(1024)}, u32[]{:S(2)}) copy-start(f32[768]{0:T(1024)} %copy-done.48) | copy-start | bytes 9220
  509.8 24.0 %copy-start.64 = (f32[512]{0:T(512)S(1)}, f32[512]{0:T(512)}, u32[]{:S(2)}) copy-start(f32[512]{0:T(512)} %copy-done.63) | copy-start | bytes 6148
  509.8 24.0 %copy-start.83 = (pred[512]{0:T(512)(128)(4,1)S(1)}, pred[512]{0:T(512)(128)(4,1)}, u32[]{:S(2)}) copy-start(pred[512]{0:T(512)(128)(4,1)} %get-tuple-element.158) | copy-start | bytes 1540
  509.8 24.0 %copy-start.85 = (pred[512]{0:T(512)(128)(4,1)S(1)}, pred[512]{0:T(512)(128)(4,1)}, u32[]{:S(2)}) copy-start(pred[512]{0:T(512)(128)(4,1)} %get-tuple-element.163) | copy-start | bytes 1540
  512.8 25.5 %copy-start.42 = (f32[512,12]{0,1:T(8,128)}, f32[512,12]{0,1:T(8,128)S(1)}, u32[]{:S(2)}) copy-start(f32[512,12]{0,1:T(8,128)S(1)} %fusion.76) | copy-start | bytes 73732
  533.8 5.6 copy-start.5
  538.3 32.5 %copy-start.66 = (f32[512]{0:T(512)}, f32[512]{0:T(512)S(1)}, u32[]{:S(2)}) copy-start(f32[512]{0:T(512)S(1)} %multiply_multiply_fusion.2) | copy-start | bytes 6148
  540.9 135.6 %reduce-scatter.18.cloned.1.call-start = ((), (), s32[]{:S(2)}) async-start(), calls=%async_computation.18 | async-start | bytes 2359296 | tf_op jit(solution)/shard_map/reduce_scatter | solution.py:51
  568.3 8.5 slice-start.3
  583.3 12.5 slice-start
  583.3 12.5 slice-start.1
  589.8 6.0 slice-start.2
  595.8 9.1 copy-start.88
  607.9 7.0 copy-start.22
  624.3 100.8 %reduce-scatter.14.cloned.1.call-start = ((), (), s32[]{:S(2)}) async-start(), calls=%async_computation.14 | async-start | bytes 2359296 | tf_op jit(solution)/shard_map/reduce_scatter | solution.py:51
  625.0 525.1 %reduce-scatter.24.cloned.1.call-start = ((), (), s32[]{:S(2)}) async-start(), calls=%async_computation.21 | async-start | bytes 53477376 | tf_op jit(solution)/shard_map/reduce_scatter | solution.py:363
  647.1 566.0 %reduce-scatter.22.cloned.1.call-start = ((), (), s32[]{:S(2)}) async-start(), calls=%async_computation.20 | async-start | bytes 1253376 | tf_op jit(solution)/shard_map/reduce_scatter | solution.py:360
  650.8 633.2 %reduce-scatter.20.cloned.1.call-start = ((), (), s32[]{:S(2)}) async-start(), calls=%async_computation.19 | async-start | bytes 3760128 | tf_op jit(solution)/shard_map/reduce_scatter | solution.py:359
  657.0 873.2 %reduce-scatter.26.cloned.1.call-start = ((), (), s32[]{:S(2)}) async-start(), calls=%async_computation.22 | async-start | bytes 26738688 | tf_op jit(solution)/shard_map/reduce_scatter | solution.py:364
  673.2 52.0 %copy-start.6 = (bf16[512,768]{1,0:T(8,128)(2,1)S(1)}, bf16[512,768]{1,0:T(8,128)(2,1)}, u32[]{:S(2)}) copy-start(bf16[512,768]{1,0:T(8,128)(2,1)} %reduce-scatter.12.cloned.1.call-done) | copy-start | bytes 2359300
  (45 other events, 118.0 us)
Sparse Core Ops, SparseCore 0:
  10.3 40.6 all-gather.12
  56.1 25.3 all-gather.10
  104.5 26.0 reduce-scatter.11
  132.1 27.3 all-gather.20
  161.5 27.2 all-gather.14
  190.9 129.4 all-gather.16
  322.9 100.2 all-gather.18
  509.1 24.6 reduce-scatter.15
  541.0 27.2 all-gather.22
  624.4 26.0 reduce-scatter.17
  652.9 26.0 reduce-scatter.13
  683.1 467.0 reduce-scatter.23
  1154.4 58.6 reduce-scatter.21
  1217.4 66.5 reduce-scatter.19
  1288.5 241.5 reduce-scatter.25
where the time goes:
time: 1540 us
  waiting for transfers between devices  903 us (59%)
  blocking collectives  305 us (20%)
  matrix products  186 us (12%)
  local copies, waits for them, and re-layouts  66.8 us (4%)
  other arithmetic  59.5 us (4%)
  between operations  15.7 us (1%)
    reduce_scatter x1, waiting for transfers between devices, shards(): lax.psum_scatter(grad_in_exp, 'fsdp', scatter_dimension=1, tiled=True)  419 us
    reduce_scatter x1, waiting for transfers between devices, shards(): lax.psum_scatter(grad_out_exp, 'fsdp', scatter_dimension=1, tiled=True)  246 us
    unnamed x2, blocking collectives  84.2 us
    reduce_scatter x1, waiting for transfers between devices, shards(): lax.psum_scatter(grad_qkv, 'fsdp', scatter_dimension=0, tiled=True)  70.9 us
    all_gather x1, blocking collectives, shards(): lax.all_gather(w_const_gate, ('fsdp', 'tp'), axis=0, tiled=True)  67.1 us
    all_gather x1, blocking collectives, shards(): lax.all_gather(w_router, ('fsdp', 'tp'), axis=0, tiled=True)  64.9 us
    reduce_scatter x1, waiting for transfers between devices, shards(): lax.psum_scatter(grad_attn_out, 'fsdp', scatter_dimension=0, tiled=True)  56.9 us
    all_gather x1, blocking collectives, shards(): lax.all_gather(w_const_value, ('fsdp', 'tp'), axis=0, tiled=True)  52.8 us
  transfers between devices with their start and end apart: 15, of which 9 were waited for; matrix products, arithmetic and copies ran while one was open for 9% of the time, Pallas kernels for 0%

commit v1 on v0

v1 whole, which is shorter than its diff:
```python
import jax
import jax.numpy as jnp
from jax import lax
from jax.experimental import pallas as pl
from jax.experimental.pallas import tpu as pltpu
from jax.sharding import PartitionSpec as P

HD = 64
BLOCK = 256


PRECISE = lax.Precision.HIGHEST
EPSILON = 1e-06
MASKED_SCORE = -1e30


def rms_norm(values, gain):
    return values * lax.rsqrt(jnp.mean(values * values, axis=-1, keepdims=True) + EPSILON) * gain


def rotate(heads):
    length, half_dim = (heads.shape[0], heads.shape[2] // 2)
    positions = jnp.arange(length).astype(jnp.float32)
    inverse = jnp.power(10000.0, -jnp.arange(half_dim).astype(jnp.float32) / half_dim)
    angles = positions[:, None] * inverse[None, :]
    cosine = jnp.cos(angles)[:, None, :]
    sine_part = jnp.sin(angles)[:, None, :]
    lower_half, upper_half = (heads[..., :half_dim], heads[..., half_dim:])
    return jnp.concatenate(
        [
            lower_half * cosine - upper_half * sine_part,
            upper_half * cosine + lower_half * sine_part,
        ],
        axis=-1,
    )


def soft_last(scores):
    highest = jnp.max(scores, axis=-1, keepdims=True)
    expanded = jnp.exp(scores - highest)
    return expanded / jnp.sum(expanded, axis=-1, keepdims=True)


def swiglu(gate_part, up_part):
    return gate_part / (1.0 + jnp.exp(-gate_part)) * up_part


FB = 512


def swap(values):
    return lax.ppermute(values, "tp", [(0, 1), (1, 0)])


def gather_rows(values):
    other = swap(values)
    first = lax.axis_index("tp") == 0
    return jnp.concatenate(
        [jnp.where(first, values, other), jnp.where(first, other, values)], axis=0
    )


def own_half(values):
    half = values.shape[0] // 2
    return lax.dynamic_slice_in_dim(values, lax.axis_index("tp") * half, half, 0)


def other_half(values):
    half = values.shape[0] // 2
    return lax.dynamic_slice_in_dim(values, (1 - lax.axis_index("tp")) * half, half, 0)


def sum_rows(values):
    values = values.astype(jnp.bfloat16)
    received = swap(other_half(values))
    return own_half(values).astype(jnp.float32) + received.astype(jnp.float32)


def member_groups(size, experts):
    span = 2 * experts
    starts = range(0, size, span)
    same_core = [[start + 2 * e + c for e in range(experts)] for start in starts for c in range(2)]
    cores = [[start + 2 * e, start + 2 * e + 1] for start in starts for e in range(experts)]
    whole = [[start + r for r in range(span)] for start in starts]
    across = [[start + r for start in starts] for r in range(span)]
    return same_core, cores, whole, across


def blocked_weights(w_expert_in, w_expert_out):
    experts, rows, _, hidden = w_expert_in.shape
    tiles = hidden // FB
    both = jnp.concatenate(
        [
            w_expert_in.reshape(experts, rows, 2, tiles, FB),
            w_expert_out.reshape(experts, rows, 1, tiles, FB),
        ],
        axis=2,
    )
    return both.transpose(0, 1, 3, 2, 4).reshape(experts, rows, 3 * hidden)


def split_grads(blocked):
    experts, rows, total = blocked.shape
    hidden = total // 3
    tiles = hidden // FB
    parts = blocked.reshape(experts, rows, tiles, 3, FB).transpose(0, 1, 3, 2, 4)
    return (
        parts[:, :, :2].reshape(experts, rows, 2, hidden),
        parts[:, :, 2].reshape(experts, rows, hidden),
    )


def fetch_expert(blocked):
    experts = blocked.shape[0]
    size = lax.axis_size("fsdp")
    same_core, cores, _, across = member_groups(size, experts)
    got = lax.all_to_all(blocked, "fsdp", 0, 0, axis_index_groups=same_core, tiled=True)
    got = lax.all_gather(got, "fsdp", axis=1, axis_index_groups=cores, tiled=True)
    got = got.reshape(-1, got.shape[-1])
    if size > 2 * experts:
        got = lax.all_gather(got, "fsdp", axis=0, axis_index_groups=across, tiled=True)
    return lax.all_gather(got, "tp", axis=0)


def return_grads(grads, experts):
    size = lax.axis_size("fsdp")
    same_core, cores, _, across = member_groups(size, experts)
    columns = grads.shape[-1]
    if size > 2 * experts:
        grads = lax.psum_scatter(
            grads, "fsdp", scatter_dimension=1, axis_index_groups=across, tiled=True
        )
    grads = grads.reshape(2, experts, -1, columns)
    grads = lax.psum_scatter(
        grads, "fsdp", scatter_dimension=2, axis_index_groups=cores, tiled=True
    )
    grads = lax.psum_scatter(grads, "tp", scatter_dimension=0)
    return lax.all_to_all(grads, "fsdp", 0, 0, axis_index_groups=same_core, tiled=True)


def exchange(values, experts):
    whole = member_groups(lax.axis_size("fsdp"), experts)[2]
    return lax.all_to_all(values, "fsdp", 0, 0, axis_index_groups=whole, tiled=True)


def nt_dot(left, right):
    return lax.dot_general(left, right, (((1,), (1,)), ((), ())), preferred_element_type=jnp.float32)


def nn_dot(left, right):
    return jnp.dot(left, right, preferred_element_type=jnp.float32)


def expert_kernel(x_ref, g_ref, w_ref, back_ref, grads_ref, xt_ref, gt_ref, res_ref, dx_ref):
    step = pl.program_id(0)

    @pl.when(step == 0)
    def _():
        xt_ref[...] = x_ref[...].T
        gt_ref[...] = g_ref[...].T
        res_ref[...] = jnp.zeros_like(res_ref)
        dx_ref[...] = jnp.zeros_like(dx_ref)

    w_gate = w_ref[0, :, :FB]
    w_up = w_ref[0, :, FB : 2 * FB]
    w_out = w_ref[0, :, 2 * FB :]
    gate = nn_dot(x_ref[...], w_gate)
    up = nn_dot(x_ref[...], w_up)
    sig = 1.0 / (1.0 + jnp.exp(-gate))
    silu = gate * sig
    act = (silu * up).astype(jnp.bfloat16)
    res_ref[...] += nt_dot(act, w_out)
    grads_ref[0, :, 2 * FB :] = nn_dot(gt_ref[...], act).astype(jnp.bfloat16)
    d_act = nn_dot(g_ref[...], w_out)
    d_up = (d_act * silu).astype(jnp.bfloat16)
    d_gate = (d_act * up * sig * (1.0 + gate * (1.0 - sig))).astype(jnp.bfloat16)
    dx_ref[...] += nt_dot(d_gate, w_gate) + nt_dot(d_up, w_up)
    grads_ref[0, :, :FB] = nn_dot(xt_ref[...], d_gate).astype(jnp.bfloat16)
    grads_ref[0, :, FB : 2 * FB] = nn_dot(xt_ref[...], d_up).astype(jnp.bfloat16)

    @pl.when(step == pl.num_programs(0) - 1)
    def _():
        width = res_ref.shape[1]
        back_ref[:, :width] = res_ref[...].astype(jnp.bfloat16)
        back_ref[:, width:] = dx_ref[...].astype(jnp.bfloat16)


def run_expert(arrived, weights):
    rows = arrived.shape[0]
    width = arrived.shape[1] // 2
    halves, _, total = weights.shape
    tiles = total // (3 * FB)
    whole = pl.BlockSpec((rows, width), lambda j: (0, 0))
    return pl.pallas_call(
        expert_kernel,
        grid=(halves * tiles,),
        in_specs=[
            pl.BlockSpec((rows, width), lambda j: (0, 0)),
            pl.BlockSpec((rows, width), lambda j: (0, 1)),
            pl.BlockSpec((1, width, 3 * FB), lambda j: (j // tiles, 0, j % tiles)),
        ],
        out_specs=[
            pl.BlockSpec((rows, 2 * width), lambda j: (0, 0)),
            pl.BlockSpec((1, width, 3 * FB), lambda j: (j // tiles, 0, j % tiles)),
        ],
        out_shape=[
            jax.ShapeDtypeStruct((rows, 2 * width), jnp.bfloat16),
            jax.ShapeDtypeStruct(weights.shape, jnp.bfloat16),
        ],
        scratch_shapes=[
            pltpu.VMEM((width, rows), jnp.bfloat16),
            pltpu.VMEM((width, rows), jnp.bfloat16),
            pltpu.VMEM((rows, width), jnp.float32),
            pltpu.VMEM((rows, width), jnp.float32),
        ],
        compiler_params=pltpu.CompilerParams(vmem_limit_bytes=60 << 20),
        cost_estimate=pl.CostEstimate(
            flops=18 * rows * width * total * halves // 3,
            bytes_accessed=4 * weights.size + 8 * rows * width,
            transcendentals=rows * total * halves // 3,
        ),
    )(arrived, arrived, weights)


def query_blocks(length):
    base_rows = BLOCK * max(1, 512 // BLOCK)
    block_count = max(1, min(8, length // base_rows))
    return (block_count, length // block_count)


def allowed_mask(row_start, row_count, key_stop):
    query_block = (row_start + jnp.arange(row_count)) // BLOCK
    key_block = jnp.arange(key_stop) // BLOCK
    return key_block[None, :] <= query_block[:, None]


def special_mix(normed, gate_matrix, value_table, gate_pair, routes, experts):
    const_weights = soft_last(jnp.dot(normed, gate_matrix, precision=PRECISE).reshape(-1, 2, 2))
    constants = (
        const_weights[:, :, 0:1] * normed[:, None, :]
        + const_weights[:, :, 1:2] * value_table.T[None, :, :]
    )
    mixture = jnp.zeros_like(normed)
    for member in range(2):
        route_col = routes[:, member][:, None]
        branch = jnp.where(route_col == experts + 1, normed, 0.0)
        branch = branch + jnp.where(route_col == experts + 2, constants[:, 0], 0.0)
        branch = branch + jnp.where(route_col == experts + 3, constants[:, 1], 0.0)
        mixture = mixture + gate_pair[:, member : member + 1] * branch
    return mixture


def shards(
    hidden,
    prev_logits,
    routes,
    slot_rank,
    dropped,
    cotangent,
    attn_norm,
    ffn_norm,
    w_qkv,
    w_attn_out,
    w_router,
    w_const_gate,
    w_const_value,
    w_expert_in,
    w_expert_out,
):
    own_rows = hidden.shape[0]
    width = hidden.shape[1]
    length = own_rows * lax.axis_size("tp")
    experts = w_expert_in.shape[0]
    route_count = w_router.shape[1]
    capacity = 9 * length // (4 * route_count)
    scaling = HD ** (-0.5)
    blocked = fetch_expert(blocked_weights(w_expert_in, w_expert_out))
    heads_width = w_attn_out.shape[1]
    small = jnp.concatenate(
        [attn_norm[:, None], ffn_norm[:, None], w_router, w_const_gate, w_const_value], axis=1
    )
    small = jnp.pad(small, ((0, 0), (0, 128 - small.shape[1])))
    small = lax.all_gather(small, "tp", axis=0, tiled=True)
    packed_weights = lax.all_gather(
        jnp.concatenate([w_qkv.reshape(-1, 3 * heads_width), w_attn_out, small], axis=1),
        "fsdp",
        axis=0,
        tiled=True,
    )
    qkv_flat = packed_weights[:, : 3 * heads_width]
    attn_full = packed_weights[:, 3 * heads_width : 4 * heads_width]
    small = packed_weights[:, 4 * heads_width :]
    gain_one = small[:, 0].astype(jnp.float32)
    gain_two = small[:, 1].astype(jnp.float32)
    router = small[:, 2 : 2 + route_count]
    router_wide = router.astype(jnp.float32)
    gate_matrix = small[:, 2 + route_count : 6 + route_count].astype(jnp.float32)
    value_table = small[:, 6 + route_count : 8 + route_count].astype(jnp.float32)
    grad_wide = cotangent.astype(jnp.float32)
    cot_other = swap(cotangent)
    kept_own = (routes < experts) & (dropped == 0)
    target_own = jnp.where(kept_own, routes * capacity + slot_rank, -1).T
    target_other = swap(target_own)
    hidden_wide = hidden.astype(jnp.float32)
    normed_one, back_one = jax.vjp(rms_norm, hidden_wide, gain_one)
    stream_one = gather_rows(normed_one.astype(jnp.bfloat16))
    local_heads = heads_width // HD
    projected = jnp.dot(
        stream_one, qkv_flat, preferred_element_type=jnp.float32
    ).reshape(length, 3, local_heads, HD)
    query_pre = projected[:, 0]
    key_pre = projected[:, 1]
    values_all = projected[:, 2].astype(jnp.bfloat16)
    queries = rotate(query_pre).astype(jnp.bfloat16)
    keys_rot = rotate(key_pre).astype(jnp.bfloat16)
    block_count, block_rows = query_blocks(length)
    mixed_parts = []
    log_sums = []
    for block_no in range(block_count):
        row_start = block_no * block_rows
        key_stop = row_start + block_rows
        allowed = allowed_mask(row_start, block_rows, key_stop)
        scores = (
            jnp.einsum(
                "qhd,khd->hqk",
                queries[row_start:key_stop],
                keys_rot[:key_stop],
                preferred_element_type=jnp.float32,
            )
            * scaling
        )
        scores = jnp.where(allowed[None], scores, MASKED_SCORE)
        highest = jnp.max(scores, axis=-1, keepdims=True)
        expanded = jnp.exp(scores - highest)
        totals = jnp.sum(expanded, axis=-1, keepdims=True)
        attn_probs = (expanded / totals).astype(jnp.bfloat16)
        mixed_parts.append(
            jnp.einsum(
                "hqk,khd->qhd",
                attn_probs,
                values_all[:key_stop],
                preferred_element_type=jnp.float32,
            ).astype(jnp.bfloat16)
        )
        log_sums.append(highest + jnp.log(totals))
    mixed = jnp.concatenate(mixed_parts, axis=0).reshape(length, -1)
    attended = sum_rows(
        jnp.einsum("tf,df->td", mixed, attn_full, preferred_element_type=jnp.float32)
    )
    residual_mid = hidden_wide + attended
    normed_two, back_two = jax.vjp(rms_norm, residual_mid, gain_two)
    stream_own = normed_two.astype(jnp.bfloat16)
    logits = jnp.dot(stream_own, router, preferred_element_type=jnp.float32) + prev_logits
    columns = jnp.arange(route_count)
    named = [routes[:, member][:, None] == columns[None, :] for member in range(2)]
    gates_own = soft_last(
        jnp.stack([jnp.sum(jnp.where(hit, logits, 0.0), axis=1) for hit in named], axis=1)
    )
    gates_line = gates_own.T
    gates_other = swap(gates_line)
    stream_other = swap(stream_own)
    half = capacity // 2
    slot = jnp.arange(experts * half)
    slot = (slot // half) * capacity + lax.axis_index("tp") * half + slot % half
    hits_own = [target_own[member][None, :] == slot[:, None] for member in range(2)]
    hits_other = [target_other[member][None, :] == slot[:, None] for member in range(2)]
    send_own = (hits_own[0] | hits_own[1]).astype(jnp.bfloat16)
    send_other = (hits_other[0] | hits_other[1]).astype(jnp.bfloat16)
    slot_gate = sum(
        jnp.sum(jnp.where(hits[member], line[member][None, :], 0.0), axis=1)
        for hits, line in ((hits_own, gates_line), (hits_other, gates_other))
        for member in range(2)
    )
    packed = (nn_dot(send_own, stream_own) + nn_dot(send_other, stream_other)).astype(jnp.bfloat16)
    gated = (
        (nn_dot(send_own, cotangent) + nn_dot(send_other, cot_other)) * slot_gate[:, None]
    ).astype(jnp.bfloat16)
    arrived = exchange(jnp.concatenate([packed, gated], axis=1), experts)
    answer, grads_exp = run_expert(arrived, blocked)
    answer = exchange(answer, experts)
    grads_exp = return_grads(grads_exp, experts)
    slot_result = answer[:, :width].astype(jnp.float32)
    slot_share = jnp.sum(slot_result * gated.astype(jnp.float32), axis=1)
    placed = jnp.concatenate(
        [(slot_result * slot_gate[:, None]).astype(jnp.bfloat16), answer[:, width:]], axis=1
    )

    def token_rows(send):
        return lax.dot_general(
            send, placed, (((0,), (0,)), ((), ())), preferred_element_type=jnp.float32
        )

    def token_share(hits):
        return jnp.stack(
            [jnp.sum(jnp.where(hit, slot_share[:, None], 0.0), axis=0) for hit in hits], axis=0
        )

    mixed_rows = token_rows(send_own) + swap(token_rows(send_other).astype(jnp.bfloat16)).astype(
        jnp.float32
    )
    share = (token_share(hits_own) + swap(token_share(hits_other))).T

    def local_mix(normed, gate_weights, value_weights, gate_pair):
        return special_mix(normed, gate_weights, value_weights, gate_pair, routes, experts)

    special, back_special = jax.vjp(local_mix, normed_two, gate_matrix, value_table, gates_own)
    output = (residual_mid + mixed_rows[:, :width] + special).astype(jnp.bfloat16)
    grad_normed_spec, grad_gate_matrix, grad_value_table, grad_gate_spec = back_special(grad_wide)
    share = share + gates_own * grad_gate_spec
    local_grad = share - gates_own * jnp.sum(share, axis=-1, keepdims=True)
    grad_logit = sum(jnp.where(named[member], local_grad[:, member : member + 1], 0.0) for member in range(2))
    grad_router = lax.dot_general(
        stream_own.astype(jnp.float32),
        grad_logit,
        (((0,), (0,)), ((), ())),
        precision=PRECISE,
        preferred_element_type=jnp.float32,
    )
    grad_normed_two = (
        mixed_rows[:, width:]
        + grad_normed_spec
        + jnp.dot(grad_logit, router_wide.T, precision=PRECISE)
    )
    grad_mid, grad_gain_two = back_two(grad_normed_two)
    grad_mid = grad_mid + grad_wide
    grad_attended = gather_rows(grad_mid.astype(jnp.bfloat16))
    grad_attn_out = jnp.einsum(
        "td,tf->df", grad_attended, mixed, preferred_element_type=jnp.float32
    )
    grad_mixed = (
        jnp.dot(grad_attended, attn_full, preferred_element_type=jnp.float32)
        .astype(jnp.bfloat16)
        .reshape(length, local_heads, HD)
    )
    grad_values = jnp.zeros((length, local_heads, HD), jnp.float32)
    grad_keys = jnp.zeros((length, local_heads, HD), jnp.float32)
    grad_query_parts = []
    for block_no in range(block_count):
        row_start = block_no * block_rows
        key_stop = row_start + block_rows
        allowed = allowed_mask(row_start, block_rows, key_stop)
        scores = (
            jnp.einsum(
                "qhd,khd->hqk",
                queries[row_start:key_stop],
                keys_rot[:key_stop],
                preferred_element_type=jnp.float32,
            )
            * scaling
        )
        recomputed = jnp.where(allowed[None], jnp.exp(scores - log_sums[block_no]), 0.0)
        grad_block = grad_mixed[row_start:key_stop]
        grad_probs = jnp.einsum(
            "qhd,khd->hqk", grad_block, values_all[:key_stop], preferred_element_type=jnp.float32
        )
        grad_values = grad_values.at[:key_stop].add(
            jnp.einsum(
                "hqk,qhd->khd",
                recomputed.astype(jnp.bfloat16),
                grad_block,
                preferred_element_type=jnp.float32,
            )
        )
        grad_scores = (
            recomputed * (grad_probs - jnp.sum(recomputed * grad_probs, axis=-1, keepdims=True))
        ).astype(jnp.bfloat16)
        grad_query_parts.append(
            jnp.einsum(
                "hqk,khd->qhd", grad_scores, keys_rot[:key_stop], preferred_element_type=jnp.float32
            )
            * scaling
        )
        grad_keys = grad_keys.at[:key_stop].add(
            jnp.einsum(
                "hqk,qhd->khd",
                grad_scores,
                queries[row_start:key_stop],
                preferred_element_type=jnp.float32,
            )
            * scaling
        )
    grad_query_pre = jax.vjp(rotate, query_pre)[1](jnp.concatenate(grad_query_parts, axis=0))[0]
    grad_key_pre = jax.vjp(rotate, key_pre)[1](grad_keys)[0]
    grad_projected = (
        jnp.stack([grad_query_pre, grad_key_pre, grad_values], axis=1)
        .astype(jnp.bfloat16)
        .reshape(length, -1)
    )
    grad_qkv = jnp.einsum(
        "td,tf->df", stream_one, grad_projected, preferred_element_type=jnp.float32
    )
    grad_stream_one = jnp.einsum(
        "tf,df->td", grad_projected, qkv_flat, preferred_element_type=jnp.float32
    )
    grad_hidden_one = back_one(sum_rows(grad_stream_one))[0]
    grad_hidden = grad_mid + grad_hidden_one
    grad_small = jnp.concatenate(
        [grad_gain_two[:, None], grad_router, grad_gate_matrix, grad_value_table], axis=1
    )
    grad_small = jnp.pad(grad_small, ((0, 0), (0, 128 - grad_small.shape[1])))
    reduced = lax.psum_scatter(
        jnp.concatenate([grad_qkv, grad_attn_out, grad_small], axis=1).astype(jnp.bfloat16),
        "fsdp",
        scatter_dimension=0,
        tiled=True,
    ).astype(jnp.float32)
    grad_qkv = reduced[:, : 3 * heads_width].reshape(w_qkv.shape)
    grad_attn_out = reduced[:, 3 * heads_width : 4 * heads_width]
    gain_share = jnp.sum(grad_qkv * w_qkv.astype(jnp.float32), axis=(1, 2))
    tail = jnp.concatenate([gain_share[:, None], reduced[:, 4 * heads_width :]], axis=1)
    tail = own_half(tail) + swap(other_half(tail))
    grad_gain_one = tail[:, 0] / attn_norm.astype(jnp.float32)
    grad_gain_two = tail[:, 1]
    grad_router = tail[:, 2 : 2 + route_count]
    grad_gate_matrix = tail[:, 2 + route_count : 6 + route_count]
    grad_value_table = tail[:, 6 + route_count : 8 + route_count]
    grad_in_exp, grad_out_exp = split_grads(grads_exp.astype(jnp.float32))
    return (
        output,
        grad_hidden,
        grad_gain_one,
        grad_gain_two,
        grad_qkv,
        grad_attn_out,
        grad_router,
        grad_gate_matrix,
        grad_value_table,
        grad_in_exp,
        grad_out_exp,
    )


def solution(mesh):
    in_specs = (
        P(("fsdp", "tp"), None),
        P(("fsdp", "tp"), None),
        P(("fsdp", "tp"), None),
        P(("fsdp", "tp"), None),
        P(("fsdp", "tp"), None),
        P(("fsdp", "tp"), None),
        P(("fsdp", "tp")),
        P(("fsdp", "tp")),
        P("fsdp", None, "tp"),
        P("fsdp", "tp"),
        P(("fsdp", "tp"), None),
        P(("fsdp", "tp"), None),
        P(("fsdp", "tp"), None),
        P(None, "fsdp", None, "tp"),
        P(None, "fsdp", "tp"),
    )
    out_specs = (
        P(("fsdp", "tp"), None),
        P(("fsdp", "tp"), None),
        P(("fsdp", "tp")),
        P(("fsdp", "tp")),
        P("fsdp", None, "tp"),
        P("fsdp", "tp"),
        P(("fsdp", "tp"), None),
        P(("fsdp", "tp"), None),
        P(("fsdp", "tp"), None),
        P(None, "fsdp", None, "tp"),
        P(None, "fsdp", "tp"),
    )
    return jax.shard_map(shards, mesh=mesh, in_specs=in_specs, out_specs=out_specs, check_vma=False)
```

time: 1540 us -> 658 us (0.43)
  waiting for transfers between devices: 903 us -> 259 us
  blocking collectives: 305 us -> 71 us
  matrix products: 186 us -> 82.5 us
  Pallas kernels: 0 us -> 30.8 us
  starting transfers between devices: 0.61 us -> 27.9 us
  local copies, waits for them, and re-layouts: 66.8 us -> 85.3 us
    reduce_scatter x8 -> x3, waiting for transfers between devices: 838 us -> 53.6 us  [the longest x1 53.5 us: shards(): lax.psum_scatter(jnp.concatenate([grad_qkv, grad_attn_out, grad_small], a...]
    all_gather x8 -> x1, blocking collectives: 221 us -> 4.36 us  [shards(): small = lax.all_gather(small, 'tp', axis=0, tiled=True)]
    ppermute x0 -> x11, waiting for transfers between devices: none -> 123 us  [swap(): return lax.ppermute(values, 'tp', [(0, 1), (1, 0)])]
    dot_general x15 -> x11, matrix products: 127 us -> 24.2 us  [the longest x4 7.47 us: nn_dot(): return jnp.dot(left, right, preferred_element_type=jnp.float32)]
    unnamed x2 -> x0, blocking collectives: 84.2 us -> none
    all_to_all x0 -> x1, blocking collectives: none -> 66.6 us  [exchange(): lax.all_to_all(values, 'fsdp', 0, 0, axis_index_groups=whole, tiled=True)]
    all_to_all x0 -> x3, waiting for transfers between devices: none -> 46.2 us  [the longest x1 28.5 us: exchange(): lax.all_to_all(values, 'fsdp', 0, 0, axis_index_groups=whole, tiled=True)]
    gather x9 -> x0, local copies, waits for them, and re-layouts: 42.3 us -> none  [the longest x2 16.6 us: shards(): jnp.take(grad_packed, safe_index[:, member], axis=0)]
  transfers between devices with their start and end apart: 15 -> 20, of which waited for: 9 -> 9; matrix products, arithmetic and copies ran while one was open for 9% -> 31% of each run, Pallas kernels for 0% -> 0%
where the time goes in v1:
time: 658 us; the launch traced here: 649 us
  waiting for transfers between devices  259 us (39%)
  local copies, waits for them, and re-layouts  85.3 us (13%)
  matrix products  82.5 us (13%)
  other arithmetic  74.6 us (11%)
  blocking collectives  71 us (11%)
  Pallas kernels  30.8 us (5%)
  starting transfers between devices  27.9 us (4%)
  between operations  17.9 us (3%)
    ppermute x11, waiting for transfers between devices, swap(): return lax.ppermute(values, 'tp', [(0, 1), (1, 0)])  123 us
    all_to_all x1, blocking collectives, exchange(): lax.all_to_all(values, 'fsdp', 0, 0, axis_index_groups=whole, tiled=True)  66.6 us
    reduce_scatter x1, waiting for transfers between devices, shards(): lax.psum_scatter(jnp.concatenate([grad_qkv, grad_attn_out, grad_small], a...  53.5 us
    all_gather x1, waiting for transfers between devices, shards(): lax.all_gather(jnp.concatenate([w_qkv.reshape(-1, 3 * heads_width), w_att...  36.1 us
    pallas_call x1, Pallas kernels, run_expert(): pl.pallas_call(expert_kernel, grid=(halves * tiles,), in_specs=[pl.BlockS...  30.8 us
    unnamed x292, local copies, waits for them, and re-layouts  29.1 us
    all_to_all x1, waiting for transfers between devices, exchange(): lax.all_to_all(values, 'fsdp', 0, 0, axis_index_groups=whole, tiled=True)  28.5 us
    all_to_all x1, waiting for transfers between devices, fetch_expert(): lax.all_to_all(blocked, 'fsdp', 0, 0, axis_index_groups=same_core, tiled=...  17.7 us
  transfers between devices with their start and end apart: 20, of which 9 were waited for; matrix products, arithmetic and copies ran while one was open for 31% of the time, Pallas kernels for 0%

profile of v1, /device:TPU:12, one launch (start us, length us, event | category | flops | bytes accessed | tf_op | source)
XLA Modules:
  0.0 648.7 jit_solution(9885549412317928091)
XLA Ops:
  12.0 4.4 all_gather.12
  18.7 4.5 reshape.535
  23.2 4.6 maximum_bitcast_fusion
  27.9 4.9 reshape.521
  32.7 6.4 all-to-all-start.1
  41.9 36.1 %all-gather.4.cloned.1.call-done = bf16[768,1664]{1,0:T(8,128)(2,1)} async-done(((bf16[48,1664]{1,0:T(8,128)(2,1)}), bf16[768,1664]{1,0:T(8,128)(2,1)}) %all-gather.4.cloned.1.call-update) | async-done | bytes 2555920 | tf_op jit(solution)/shard_map/all_gather | solution.py:284
  78.0 1.9 convert_reduce_fusion
  82.1 17.7 %all-to-all-done.1 = bf16[8,48,3072]{2,1,0:T(8,128)(2,1)} async-done(((bf16[8,48,3072]{2,1,0:T(8,128)(2,1)}), bf16[8,48,3072]{2,1,0:T(8,128)(2,1)}, u32[]{:S(2)}, u32[]{:S(2)}) %all-to-all-start.1) | async-done | bytes 2359328 | tf_op jit(solution)/shard_map/all_to_all | solution.py:117
  102.0 2.1 fusion.50
  106.7 3.1 copy-done.1
  111.2 2.4 select_reduce_fusion
  113.6 3.9 fusion
  118.3 4.0 fusion.66
  122.5 4.8 fusion.67
  127.4 2.3 convolution_convert_fusion.2
  130.4 3.5 fusion.68
  134.5 22.9 %collective-permute-done.1 = bf16[512,768]{0,1:T(8,128)(2,1)} collective-permute-done((bf16[512,768]{0,1:T(8,128)(2,1)S(1)}, bf16[512,768]{0,1:T(8,128)(2,1)}, u32[]{:S(2)}, u32[]{:S(2)}) %collective-permute-start.1) | collective-permute-done | bytes 786464 | tf_op jit(solution)/shard_map/ppermute | solution.py:52
  165.6 30.7 %collective-permute-done.5 = f32[2,512]{1,0:T(2,128)S(1)} collective-permute-done((f32[2,512]{1,0:T(2,128)S(1)}, f32[2,512]{1,0:T(2,128)S(1)}, u32[]{:S(2)}, u32[]{:S(2)}) %collective-permute-start.5) | collective-permute-done | bytes 4128 | tf_op jit(solution)/shard_map/ppermute | solution.py:52
  197.1 2.1 multiply_convert_fusion.2
  201.8 4.3 copy.171
  206.1 66.6 %all_to_all.33 = bf16[16,48,1536]{2,1,0:T(8,128)(2,1)} all-to-all(bf16[16,48,1536]{2,1,0:T(8,128)(2,1)} %bitcast.173), channel_id=1, replica_groups={{0,2,4,6,8,10,12,14,16,18,20,22,24,26,28,30},{1,3,5,7,9,11,13,15,17,19,..., dimensions={0} | all-to-all | bytes 4718592 | tf_op jit(solution)/shard_map/all_to_all | solution.py:143
  272.8 30.8 %shard_map.240 = (bf16[768,1536]{1,0:T(8,128)(2,1)}, bf16[2,768,3072]{2,1,0:T(8,128)(2,1)}) custom-call(bf16[768,1536]{1,0:T(8,128)(2,1)} %bitcast.180, bf16[768,1536]{1,0:T(8,128)(2,1)} %bitcast.181, bf16[2,768,3072]{2,1,0:T(8,128)(2,1)} %all-gather.8.cloned.1.call-done.w_ref), custom_call_target="tpu_custom_call" | custom-call | flops 21743271936 | bytes 23592960 | tf_op jit(solution)/shard_map/pallas_call | solution.py:194
  303.6 5.0 all-to-all-start.2
  308.6 2.5 copy.179
  312.4 1.9 convert_bitcast_fusion
  314.3 1.8 copy.178
  317.4 2.3 fusion.98
  321.3 1.8 fusion.29
  323.3 3.3 multiply_reduce_fusion.2
  328.5 3.0 fusion.44
  331.5 28.5 %all-to-all-done.2 = bf16[16,48,1536]{2,1,0:T(8,128)(2,1)} async-done(((bf16[16,48,1536]{2,1,0:T(8,128)(2,1)}), bf16[16,48,1536]{2,1,0:T(8,128)(2,1)}, u32[]{:S(2)}, u32[]{:S(2)}) %all-to-all-start.2) | async-done | bytes 2359328 | tf_op jit(solution)/shard_map/all_to_all | solution.py:143
  360.0 3.2 fusion.172
  363.2 2.4 copy.207
  365.6 2.4 copy.208
  368.0 2.2 fusion.15
  370.3 2.7 convolution_convert_fusion.1
  375.1 1.9 collective-permute-start.7
  378.3 31.4 %collective-permute-done.7 = f32[2,512]{1,0:T(2,128)} collective-permute-done((f32[2,512]{1,0:T(2,128)}, f32[2,512]{1,0:T(2,128)}, u32[]{:S(2)}, u32[]{:S(2)}) %collective-permute-start.7) | collective-permute-done | bytes 4128 | tf_op jit(solution)/shard_map/ppermute | solution.py:52
  411.8 1.8 fusion.100
  413.7 3.5 convert_add_fusion.1
  417.2 3.6 multiply_reduce_fusion.6
  422.6 2.0 convolution_convert_fusion.7
  427.4 22.9 %collective-permute-done.8 = bf16[512,768]{0,1:T(8,128)(2,1)} collective-permute-done((bf16[512,768]{0,1:T(8,128)(2,1)}, bf16[512,768]{0,1:T(8,128)(2,1)}, u32[]{:S(2)}, u32[]{:S(2)}) %collective-permute-start.8) | collective-permute-done | bytes 786464 | tf_op jit(solution)/shard_map/ppermute | solution.py:52
  451.8 2.4 convolution_convert_fusion.4
  454.4 5.9 multiply_reduce_fusion.1
  460.4 6.8 %multiply_convert_fusion.1 = bf16[6,512,512]{1,2,0:T(8,128)(2,1)} fusion(f32[6,512,512]{1,2,0:T(8,128)} %get-tuple-element.233, f32[6,512,512]{1,2,0:T(8,128)S(1)} %bitcast.167, f32[6,512]{1,0:T(8,128)S(1)} %get-tuple-element.232, f32[6,512]{1,0:T(8,128)S(1)} %copy-done.56, pred[512,512]{0,1:T(8,128)(4,1)S(1)} %broadcast_compare_fusion.1), kind=kLoop, calls=%fused_computation.8 | loop fusion | flops 9437184 | bytes 16015360 | tf_op jit(solution)/shard_map/convert_element_type | solution.py:466
  467.2 3.3 fusion.61
  470.5 2.6 fusion.63
  473.2 8.7 %multiply_reduce_fusion = (f32[6,512]{1,0:T(8,128)S(1)}, f32[6,512,1024]{2,1,0:T(8,128)}) fusion(f32[6,512,1024]{2,1,0:T(8,128)S(1)} %bitcast.165, f32[6,512]{1,0:T(8,128)S(1)} %log_add_fusion, pred[512,1024]{1,0:T(8,128)(4,1)S(1)} %copy-done.12, bf16[512,6,64]{0,2,1:T(8,128)(2,1)S(1)} %bitcast.184, bf16[1024,3,6,64]{0,3,2,1:T(8,128)(2,1)} %copy-done.25), kind=kOutput, calls=%fused_computation.1 | convolution fusion | flops 418378752 | bytes 26894336 | tf_op jit(solution)/shard_map/qhd,khd->hqk/dot_general | solution.py:453
  481.9 10.2 %multiply_convert_fusion = bf16[6,512,1024]{2,1,0:T(8,128)(2,1)} fusion(f32[6,512,1024]{2,1,0:T(8,128)} %get-tuple-element.231, f32[6,512,1024]{2,1,0:T(8,128)S(1)} %bitcast.165, f32[6,512]{1,0:T(8,128)S(1)} %get-tuple-element.230, f32[6,512]{1,0:T(8,128)S(1)} %log_add_fusion, pred[512,1024]{1,0:T(8,128)(4,1)S(1)} %copy-done.12), kind=kLoop, calls=%fused_computation | loop fusion | flops 18874368 | bytes 32006144 | tf_op jit(solution)/shard_map/convert_element_type | solution.py:466
  492.1 4.2 bitcast_add_fusion.1
  496.8 2.0 fusion.62
  501.8 2.9 fusion.55
  508.6 2.2 convolution_convert_fusion
  512.6 7.8 %all-to-all-start.3 = ((bf16[8,48,3072]{2,1,0:T(8,128)(2,1)}), bf16[8,48,3072]{2,1,0:T(8,128)(2,1)}, u32[]{:S(2)}, u32[]{:S(2)}) async-start(bf16[8,48,3072]{2,1,0:T(8,128)(2,1)} %bitcast.176), calls=%async_computation.6 | async-start | bytes 4718592 | tf_op jit(solution)/shard_map/all_to_all | solution.py:138
  520.4 3.7 convolution_convert_fusion.3
  526.4 14.8 %collective-permute-done.9 = bf16[512,768]{0,1:T(8,128)(2,1)} collective-permute-done((bf16[512,768]{0,1:T(8,128)(2,1)}, bf16[512,768]{0,1:T(8,128)(2,1)}, u32[]{:S(2)}, u32[]{:S(2)}) %collective-permute-start.9) | collective-permute-done | bytes 786464 | tf_op jit(solution)/shard_map/ppermute | solution.py:52
  543.0 53.5 %reduce-scatter.4.cloned.1.call-done = bf16[48,1664]{1,0:T(8,128)(2,1)} async-done(((bf16[768,1664]{1,0:T(8,128)(2,1)}), bf16[48,1664]{1,0:T(8,128)(2,1)}) %reduce-scatter.4.cloned.1.call-update) | async-done | bytes 159760 | tf_op jit(solution)/shard_map/reduce_scatter | solution.py:501
  601.2 4.9 fusion.31
  606.1 3.1 copy.190
  615.9 8.4 %reshape.534 = f32[8,48,2,3,512]{4,3,2,1,0:T(4,128)} reshape(bf16[8,48,3072]{2,1,0:T(8,128)(2,1)} %all-to-all-done.3) | data formatting | bytes 7077888 | tf_op jit(solution)/shard_map/transpose | solution.py:106
  624.3 8.2 %slice_reduce_fusion = f32[8,48,2,512]{3,2,1,0:T(2,128)S(1)} fusion(f32[8,48,3,2,512]{4,2,3,1,0:T(4,128)} %bitcast.168), kind=kLoop, calls=%fused_computation.98 | loop fusion | bytes 3145728 | tf_op jit(solution)/shard_map/slice | solution.py:109
  632.5 6.0 slice.366
  638.5 2.5 reshape_squeeze.3
  (421 shorter events, 72.6 us)
Async XLA Ops:
  8.0 69.9 %all-gather.4.cloned.1.call-start = ((), (), s32[]{:S(2)}) async-start(), calls=%async_computation.7 | async-start | bytes 2715648 | tf_op jit(solution)/shard_map/all_gather | solution.py:284
  32.7 6.4 copy-start.80
  32.7 6.4 copy-start.130
  32.7 6.4 copy-start.131
  32.7 8.5 %copy-start.43 = (bf16[512,768]{1,0:T(8,128)(2,1)S(1)}, bf16[512,768]{1,0:T(8,128)(2,1)}, u32[]{:S(2)}) copy-start(bf16[512,768]{1,0:T(8,128)(2,1)} %param.27) | copy-start | bytes 2359300
  32.7 67.0 %all-to-all-start.1 = ((bf16[8,48,3072]{2,1,0:T(8,128)(2,1)}), bf16[8,48,3072]{2,1,0:T(8,128)(2,1)}, u32[]{:S(2)}, u32[]{:S(2)}) async-start(bf16[8,48,3072]{2,1,0:T(8,128)(2,1)} %reshape.521), calls=%async_computation.1 | async-start | bytes 4718592 | tf_op jit(solution)/shard_map/all_to_all | solution.py:117
  39.1 83.2 %all-gather.6.cloned.1.call-start = ((), (), s32[]{:S(2)}) async-start(), calls=%async_computation.8 | async-start | bytes 7077888 | tf_op jit(solution)/shard_map/all_gather | solution.py:118
  39.2 95.3 %collective-permute-start.2 = (s32[2,512]{1,0:T(2,128)S(1)}, s32[2,512]{1,0:T(2,128)S(1)}, u32[]{:S(2)}, u32[]{:S(2)}) collective-permute-start(s32[2,512]{1,0:T(2,128)S(1)} %fusion.126), channel_id=1, source_target_pairs={{0,1},{1,0},{2,3},{3,2},{4,5},{5,4},{6,7},{7,6},{8,9},{9,8},{10,11... | collective-permute-start | bytes 12296 | tf_op jit(solution)/shard_map/ppermute | solution.py:52
  39.7 157.4 %collective-permute-start.4 = (bf16[512,768]{1,0:T(8,128)(2,1)}, bf16[512,768]{1,0:T(8,128)(2,1)}, u32[]{:S(2)}, u32[]{:S(2)}) collective-permute-start(bf16[512,768]{1,0:T(8,128)(2,1)} %param.32), channel_id=1, source_target_pairs={{0,1},{1,0},{2,3},{3,2},{4,5},{5,4},{6,7},{7,6},{8,9},{9,8},{10,11... | collective-permute-start | bytes 2359304 | tf_op jit(solution)/shard_map/ppermute | solution.py:52
  41.5 115.9 %copy-start.5 = (bf16[512,768]{0,1:T(8,128)(2,1)}, bf16[512,768]{0,1:T(8,128)(2,1)S(1)}, u32[]{:S(2)}) copy-start(bf16[512,768]{0,1:T(8,128)(2,1)S(1)} %copy.162) | copy-start | bytes 2359300
  41.8 58.0 %copy-start.103 = (f32[512]{0:T(512)}, f32[512]{0:T(512)S(1)}, u32[]{:S(2)}) copy-start(f32[512]{0:T(512)S(1)} %fusion.40) | copy-start | bytes 6148
  41.8 58.3 %copy-start.81 = (f32[512]{0:T(512)}, f32[512]{0:T(512)S(1)}, u32[]{:S(2)}) copy-start(f32[512]{0:T(512)S(1)} %fusion.140) | copy-start | bytes 6148
  41.8 88.6 %copy-start.107 = (s32[1,512]{1,0:T(1,128)}, s32[1,512]{1,0:T(1,128)S(1)}, u32[]{:S(2)}) copy-start(s32[1,512]{1,0:T(1,128)S(1)} %get-tuple-element.223) | copy-start | bytes 6148
  41.9 88.6 %copy-start.110 = (s32[1,512]{1,0:T(1,128)}, s32[1,512]{1,0:T(1,128)S(1)}, u32[]{:S(2)}) copy-start(s32[1,512]{1,0:T(1,128)S(1)} %get-tuple-element.224) | copy-start | bytes 6148
  79.8 20.2 %copy-start.57 = (f32[768]{0:T(1024)}, f32[768]{0:T(1024)S(1)}, u32[]{:S(2)}) copy-start(f32[768]{0:T(1024)S(1)} %get-tuple-element.141) | copy-start | bytes 9220
  80.1 20.0 %collective-permute-start = (bf16[512,768]{0,1:T(8,128)(2,1)S(1)}, bf16[512,768]{0,1:T(8,128)(2,1)}, u32[]{:S(2)}, u32[]{:S(2)}) collective-permute-start(bf16[512,768]{0,1:T(8,128)(2,1)S(1)} %fusion.42), channel_id=1, source_target_pairs={{0,1},{1,0},{2,3},{3,2},{4,5},{5,4},{6,7},{7,6},{8,9},{9,8},{10,11... | collective-permute-start | bytes 2359304 | tf_op jit(solution)/shard_map/ppermute | solution.py:52
  81.7 23.2 %copy-start.39 = (f32[1024,32]{0,1:T(8,128)}, f32[1024,32]{0,1:T(8,128)S(1)}, u32[]{:S(2)}) copy-start(f32[1024,32]{0,1:T(8,128)S(1)} %get-tuple-element.210) | copy-start | bytes 393220
  82.0 35.5 %copy-start.11 = (pred[512,1024]{1,0:T(8,128)(4,1)}, pred[512,1024]{1,0:T(8,128)(4,1)S(1)}, u32[]{:S(2)}) copy-start(pred[512,1024]{1,0:T(8,128)(4,1)S(1)} %broadcast_compare_fusion) | copy-start | bytes 1572868
  99.8 173.0 %all-gather.8.cloned.1.call-start = ((), (), s32[]{:S(2)}) async-start(), calls=%async_computation.9 | async-start | bytes 14155776 | tf_op jit(solution)/shard_map/all_gather | solution.py:122
  104.9 12.6 %copy-start.25 = (bf16[1024,3,6,64]{0,3,2,1:T(8,128)(2,1)}, bf16[1024,3,6,64]{0,3,2,1:T(8,128)(2,1)S(1)}, u32[]{:S(2)}) copy-start(bf16[1024,3,6,64]{0,3,2,1:T(8,128)(2,1)S(1)} %convert.55) | copy-start | bytes 7077892
  111.2 11.3 %copy-start.72 = (f32[6,512]{1,0:T(8,128)}, f32[6,512]{1,0:T(8,128)S(1)}, u32[]{:S(2)}) copy-start(f32[6,512]{1,0:T(8,128)S(1)} %fusion.7) | copy-start | bytes 36868
  122.4 302.2 %reduce-scatter.6.cloned.1.call-start = ((), (), s32[]{:S(2)}) async-start(), calls=%async_computation.11 | async-start | bytes 14155776 | tf_op jit(solution)/shard_map/reduce_scatter | solution.py:134
  129.8 27.6 %collective-permute-start.1 = (bf16[512,768]{0,1:T(8,128)(2,1)S(1)}, bf16[512,768]{0,1:T(8,128)(2,1)}, u32[]{:S(2)}, u32[]{:S(2)}) collective-permute-start(bf16[512,768]{0,1:T(8,128)(2,1)S(1)} %constant_dynamic-slice_fusion.1), channel_id=1, source_target_pairs={{0,1},{1,0},{2,3},{3,2},{4,5},{5,4},{6,7},{7,6},{8,9},{9,8},{10,11... | collective-permute-start | bytes 2359304 | tf_op jit(solution)/shard_map/ppermute | solution.py:52
  134.5 64.8 %copy-start.113 = (s32[1,512]{1,0:T(1,128)}, s32[1,512]{1,0:T(1,128)S(1)}, u32[]{:S(2)}) copy-start(s32[1,512]{1,0:T(1,128)S(1)} %get-tuple-element.217) | copy-start | bytes 6148
  134.5 64.8 %copy-start.115 = (s32[1,512]{1,0:T(1,128)}, s32[1,512]{1,0:T(1,128)S(1)}, u32[]{:S(2)}) copy-start(s32[1,512]{1,0:T(1,128)S(1)} %get-tuple-element.218) | copy-start | bytes 6148
  134.5 25.2 %copy-start.59 = (f32[768]{0:T(1024)S(1)}, f32[768]{0:T(1024)}, u32[]{:S(2)}) copy-start(f32[768]{0:T(1024)} %get-tuple-element.140) | copy-start | bytes 9220
  159.2 261.7 %copy-start.3 = (f32[512,768]{0,1:T(8,128)}, f32[512,768]{0,1:T(8,128)S(1)}, u32[]{:S(2)}) copy-start(f32[512,768]{0,1:T(8,128)S(1)} %get-tuple-element.173) | copy-start | bytes 4718596
  160.1 39.2 %collective-permute-start.3 = (bf16[512,768]{0,1:T(8,128)(2,1)S(1)}, bf16[512,768]{0,1:T(8,128)(2,1)S(1)}, u32[]{:S(2)}, u32[]{:S(2)}) collective-permute-start(bf16[512,768]{0,1:T(8,128)(2,1)S(1)} %get-tuple-element.170), channel_id=1, source_target_pairs={{0,1},{1,0},{2,3},{3,2},{4,5},{5,4},{6,7},{7,6},{8,9},{9,8},{10,11... | collective-permute-start | bytes 2359304 | tf_op jit(solution)/shard_map/ppermute | solution.py:52
  161.9 35.2 %copy-start.133 = (f32[768,768]{0,1:T(8,128)S(1)}, f32[768,768]{0,1:T(8,128)}, u32[]{:S(2)}) copy-start(f32[768,768]{0,1:T(8,128)} %fusion.68) | copy-start | bytes 7077892
  163.0 33.3 %collective-permute-start.5 = (f32[2,512]{1,0:T(2,128)S(1)}, f32[2,512]{1,0:T(2,128)S(1)}, u32[]{:S(2)}, u32[]{:S(2)}) collective-permute-start(f32[2,512]{1,0:T(2,128)S(1)} %fusion.204), channel_id=1, source_target_pairs={{0,1},{1,0},{2,3},{3,2},{4,5},{5,4},{6,7},{7,6},{8,9},{9,8},{10,11... | collective-permute-start | bytes 12296 | tf_op jit(solution)/shard_map/ppermute | solution.py:52
  303.6 56.5 %all-to-all-start.2 = ((bf16[16,48,1536]{2,1,0:T(8,128)(2,1)}), bf16[16,48,1536]{2,1,0:T(8,128)(2,1)}, u32[]{:S(2)}, u32[]{:S(2)}) async-start(bf16[16,48,1536]{2,1,0:T(8,128)(2,1)} %bitcast.177), calls=%async_computation.2 | async-start | bytes 4718592 | tf_op jit(solution)/shard_map/all_to_all | solution.py:143
  308.5 204.0 %reduce-scatter.8.cloned.1.call-start = ((), (), s32[]{:S(2)}) async-start(), calls=%async_computation.12 | async-start | bytes 7077888 | tf_op jit(solution)/shard_map/reduce_scatter | solution.py:137
  370.3 6.7 %copy-start.94 = (f32[512,2,2]{0,2,1:T(2,128)S(1)}, f32[512,2,2]{0,2,1:T(2,128)}, u32[]{:S(2)}) copy-start(f32[512,2,2]{0,2,1:T(2,128)} %get-tuple-element.165) | copy-start | bytes 24580
  373.0 40.6 %collective-permute-start.6 = (bf16[512,1536]{0,1:T(8,128)(2,1)}, bf16[512,1536]{0,1:T(8,128)(2,1)}, u32[]{:S(2)}, u32[]{:S(2)}) collective-permute-start(bf16[512,1536]{0,1:T(8,128)(2,1)} %convolution_convert_fusion.1), channel_id=1, source_target_pairs={{0,1},{1,0},{2,3},{3,2},{4,5},{5,4},{6,7},{7,6},{8,9},{9,8},{10,11... | collective-permute-start | bytes 4718600 | tf_op jit(solution)/shard_map/ppermute | solution.py:52
  375.1 34.7 %collective-permute-start.7 = (f32[2,512]{1,0:T(2,128)}, f32[2,512]{1,0:T(2,128)}, u32[]{:S(2)}, u32[]{:S(2)}) collective-permute-start(f32[2,512]{1,0:T(2,128)} %pad_maximum_fusion.26), channel_id=1, source_target_pairs={{0,1},{1,0},{2,3},{3,2},{4,5},{5,4},{6,7},{7,6},{8,9},{9,8},{10,11... | collective-permute-start | bytes 12296 | tf_op jit(solution)/shard_map/ppermute | solution.py:52
  378.3 38.8 %copy-start.65 = (f32[512,4]{0,1:T(4,128)}, f32[512,4]{0,1:T(4,128)S(1)}, u32[]{:S(2)}) copy-start(f32[512,4]{0,1:T(4,128)S(1)} %reshape.525) | copy-start | bytes 24580
  378.3 35.4 %copy-start.38 = (bf16[768,768]{0,1:T(8,128)(2,1)S(1)}, bf16[768,768]{0,1:T(8,128)(2,1)}, u32[]{:S(2)}) copy-start(bf16[768,768]{0,1:T(8,128)(2,1)} %copy-done.37) | copy-start | bytes 3538948
  422.3 28.0 %collective-permute-start.8 = (bf16[512,768]{0,1:T(8,128)(2,1)}, bf16[512,768]{0,1:T(8,128)(2,1)}, u32[]{:S(2)}, u32[]{:S(2)}) collective-permute-start(bf16[512,768]{0,1:T(8,128)(2,1)} %fusion.167), channel_id=1, source_target_pairs={{0,1},{1,0},{2,3},{3,2},{4,5},{5,4},{6,7},{7,6},{8,9},{9,8},{10,11... | collective-permute-start | bytes 2359304 | tf_op jit(solution)/shard_map/ppermute | solution.py:52
  424.7 29.7 %slice-start.3 = ((s8[6291456]{0:T(1024)(128)(4,1)}), s8[2097152]{0:T(1024)(128)(4,1)S(1)}, s32[]{:S(2)}) async-start(s8[6291456]{0:T(1024)(128)(4,1)} %bitcast.166), calls=%async_computation.16 | async-start | bytes 4194304
  424.7 171.8 %reduce-scatter.4.cloned.1.call-start = ((), (), s32[]{:S(2)}) async-start(), calls=%async_computation.10 | async-start | bytes 2715648 | tf_op jit(solution)/shard_map/reduce_scatter | solution.py:501
  427.4 27.0 %slice-start.4 = ((s8[6291456]{0:T(1024)(128)(4,1)}), s8[4194304]{0:T(1024)(128)(4,1)S(1)}, s32[]{:S(2)}) async-start(s8[6291456]{0:T(1024)(128)(4,1)} %bitcast.166), calls=%async_computation.17 | async-start | bytes 8388608
  454.4 18.7 %copy-start.33 = (bf16[512,384]{0,1:T(8,128)(2,1)}, bf16[512,384]{0,1:T(8,128)(2,1)S(1)}, u32[]{:S(2)}) copy-start(bf16[512,384]{0,1:T(8,128)(2,1)S(1)} %get-tuple-element.200) | copy-start | bytes 1179652
  460.3 6.8 %copy-start.16 = (bf16[1024,6,32]{0,2,1:T(8,128)(2,1)S(1)}, bf16[1024,6,32]{0,2,1:T(8,128)(2,1)}, u32[]{:S(2)}) copy-start(bf16[1024,6,32]{0,2,1:T(8,128)(2,1)} %copy-done.15) | copy-start | bytes 1179652
  460.3 6.8 %copy-start.18 = (bf16[1024,6,32]{0,2,1:T(8,128)(2,1)S(1)}, bf16[1024,6,32]{0,2,1:T(8,128)(2,1)}, u32[]{:S(2)}) copy-start(bf16[1024,6,32]{0,2,1:T(8,128)(2,1)} %copy-done.17) | copy-start | bytes 1179652
  460.3 10.1 %copy-start.22 = (bf16[1024,6,32]{0,2,1:T(8,128)(2,1)S(1)}, bf16[1024,6,32]{0,2,1:T(8,128)(2,1)}, u32[]{:S(2)}) copy-start(bf16[1024,6,32]{0,2,1:T(8,128)(2,1)} %copy-done.21) | copy-start | bytes 1179652
  460.3 12.8 %slice-start = ((s8[12582912]{0:T(1024)(128)(4,1)}), s8[4194304]{0:T(1024)(128)(4,1)S(1)}, s32[]{:S(2)}) async-start(s8[12582912]{0:T(1024)(128)(4,1)} %bitcast.164), calls=%async_computation.13 | async-start | bytes 8388608
  460.3 12.8 %slice-start.1 = ((s8[12582912]{0:T(1024)(128)(4,1)}), s8[4194304]{0:T(1024)(128)(4,1)S(1)}, s32[]{:S(2)}) async-start(s8[12582912]{0:T(1024)(128)(4,1)} %bitcast.164), calls=%async_computation.14 | async-start | bytes 8388608
  512.6 7.8 %copy-start.31 = (bf16[1024,3,6,64]{0,3,2,1:T(8,128)(2,1)S(1)}, bf16[1024,3,6,64]{0,3,2,1:T(8,128)(2,1)}, u32[]{:S(2)}) copy-start(bf16[1024,3,6,64]{0,3,2,1:T(8,128)(2,1)} %copy-done.30) | copy-start | bytes 7077892
  512.6 103.3 %all-to-all-start.3 = ((bf16[8,48,3072]{2,1,0:T(8,128)(2,1)}), bf16[8,48,3072]{2,1,0:T(8,128)(2,1)}, u32[]{:S(2)}, u32[]{:S(2)}) async-start(bf16[8,48,3072]{2,1,0:T(8,128)(2,1)} %bitcast.176), calls=%async_computation.6 | async-start | bytes 4718592 | tf_op jit(solution)/shard_map/all_to_all | solution.py:138
  520.4 20.8 %copy-start.58 = (f32[768]{0:T(1024)S(1)}, f32[768]{0:T(1024)}, u32[]{:S(2)}) copy-start(f32[768]{0:T(1024)} %copy-done.57) | copy-start | bytes 9220
  525.3 16.0 %copy-start.6 = (bf16[512,768]{0,1:T(8,128)(2,1)S(1)}, bf16[512,768]{0,1:T(8,128)(2,1)}, u32[]{:S(2)}) copy-start(bf16[512,768]{0,1:T(8,128)(2,1)} %copy-done.5) | copy-start | bytes 2359300
  525.3 17.7 %copy-start.104 = (f32[512]{0:T(512)S(1)}, f32[512]{0:T(512)}, u32[]{:S(2)}) copy-start(f32[512]{0:T(512)} %copy-done.103) | copy-start | bytes 6148
  526.3 72.0 %copy-start.55 = (bf16[48,3,384]{2,0,1:T(8,128)(2,1)S(1)}, bf16[48,3,384]{2,0,1:T(8,128)(2,1)}, u32[]{:S(2)}) copy-start(bf16[48,3,384]{2,0,1:T(8,128)(2,1)} %param.35) | copy-start | bytes 331780
  526.3 14.9 %collective-permute-start.9 = (bf16[512,768]{0,1:T(8,128)(2,1)}, bf16[512,768]{0,1:T(8,128)(2,1)}, u32[]{:S(2)}, u32[]{:S(2)}) collective-permute-start(bf16[512,768]{0,1:T(8,128)(2,1)} %constant_dynamic-slice_fusion), channel_id=1, source_target_pairs={{0,1},{1,0},{2,3},{3,2},{4,5},{5,4},{6,7},{7,6},{8,9},{9,8},{10,11... | collective-permute-start | bytes 2359304 | tf_op jit(solution)/shard_map/ppermute | solution.py:52
  526.3 74.8 %copy-start.4 = (f32[512,768]{0,1:T(8,128)S(1)}, f32[512,768]{0,1:T(8,128)}, u32[]{:S(2)}) copy-start(f32[512,768]{0,1:T(8,128)} %copy-done.3) | copy-start | bytes 4718596
  526.3 74.8 %copy-start.9 = (bf16[512,768]{0,1:T(8,128)(2,1)S(1)}, bf16[512,768]{0,1:T(8,128)(2,1)}, u32[]{:S(2)}) copy-start(bf16[512,768]{0,1:T(8,128)(2,1)} %copy.179) | copy-start | bytes 2359300
  526.3 74.8 %copy-start.61 = (f32[768]{0:T(1024)S(1)}, f32[768]{0:T(1024)}, u32[]{:S(2)}) copy-start(f32[768]{0:T(1024)} %get-tuple-element.140) | copy-start | bytes 9220
  526.3 74.8 %copy-start.75 = (f32[512]{0:T(512)S(1)}, f32[512]{0:T(512)}, u32[]{:S(2)}) copy-start(f32[512]{0:T(512)} %copy-done.73) | copy-start | bytes 6148
  526.3 74.8 %copy-start.82 = (f32[512]{0:T(512)S(1)}, f32[512]{0:T(512)}, u32[]{:S(2)}) copy-start(f32[512]{0:T(512)} %copy-done.81) | copy-start | bytes 6148
  526.4 74.8 %copy-start.85 = (f32[512,1]{0,1:T(1,128)S(1)}, f32[512,1]{0,1:T(1,128)}, u32[]{:S(2)}) copy-start(f32[512,1]{0,1:T(1,128)} %copy-done.83) | copy-start | bytes 6148
  526.4 74.8 %copy-start.88 = (f32[512,1]{0,1:T(1,128)S(1)}, f32[512,1]{0,1:T(1,128)}, u32[]{:S(2)}) copy-start(f32[512,1]{0,1:T(1,128)} %copy-done.86) | copy-start | bytes 6148
  526.4 74.8 %copy-start.98 = (f32[512]{0:T(512)S(1)}, f32[512]{0:T(512)}, u32[]{:S(2)}) copy-start(f32[512]{0:T(512)} %copy-done.97) | copy-start | bytes 6148
  600.5 11.9 %collective-permute-start.10 = (f32[24,129]{1,0:T(8,128)S(1)}, f32[24,129]{1,0:T(8,128)S(1)}, u32[]{:S(2)}, u32[]{:S(2)}) collective-permute-start(f32[24,129]{1,0:T(8,128)S(1)} %fusion.104), channel_id=1, source_target_pairs={{0,1},{1,0},{2,3},{3,2},{4,5},{5,4},{6,7},{7,6},{8,9},{9,8},{10,11... | collective-permute-start | bytes 37160 | tf_op jit(solution)/shard_map/ppermute | solution.py:52
  609.2 6.2 copy-start.132
  (95 other events, 265.9 us)
Sparse Core Ops, SparseCore 0:
  18.8 59.0 all-gather.3
Sparse Core Ops, SparseCore 1:
  99.9 15.7 all-gather.5
  122.5 145.1 all-gather.7
  303.7 17.7 reduce-scatter.5
  424.8 68.2 reduce-scatter.7
  512.6 83.9 reduce-scatter.3

commit v2 on v1

v2 whole, which is shorter than its diff:
```python
import jax
import jax.numpy as jnp
import numpy as np
from jax import lax
from jax.experimental import pallas as pl
from jax.experimental.pallas import tpu as pltpu
from jax.sharding import PartitionSpec as P

HD = 64
BLOCK = 256


EPSILON = 1e-06
MESH = pl.DeviceIdType.MESH
PAIR = 2 * HD
SCALING = HD ** (-0.5)
ROUTER = 2
MIXING = 14
VALUE = 18
ROUTE = 20
TARGET = 22
GATE = 24
COPY = 9


FB = 512


def swap(values):
    return lax.ppermute(values, "tp", [(0, 1), (1, 0)])


def gather_rows(values):
    other = swap(values)
    first = lax.axis_index("tp") == 0
    return jnp.concatenate(
        [jnp.where(first, values, other), jnp.where(first, other, values)], axis=0
    )


def own_half(values):
    half = values.shape[0] // 2
    return lax.dynamic_slice_in_dim(values, lax.axis_index("tp") * half, half, 0)


def other_half(values):
    half = values.shape[0] // 2
    return lax.dynamic_slice_in_dim(values, (1 - lax.axis_index("tp")) * half, half, 0)


def gather_columns(values):
    other = swap(values)
    first = lax.axis_index("tp") == 0
    return jnp.concatenate(
        [jnp.where(first, values, other), jnp.where(first, other, values)], axis=1
    )


def member_groups(size, experts):
    span = 2 * experts
    starts = range(0, size, span)
    same_core = [[start + 2 * e + c for e in range(experts)] for start in starts for c in range(2)]
    cores = [[start + 2 * e, start + 2 * e + 1] for start in starts for e in range(experts)]
    whole = [[start + r for r in range(span)] for start in starts]
    across = [[start + r for start in starts] for r in range(span)]
    return same_core, cores, whole, across


def blocked_weights(w_expert_in, w_expert_out):
    experts, rows, _, hidden = w_expert_in.shape
    tiles = hidden // FB
    both = jnp.concatenate(
        [
            w_expert_in.reshape(experts, rows, 2, tiles, FB),
            w_expert_out.reshape(experts, rows, 1, tiles, FB),
        ],
        axis=2,
    )
    return both.transpose(0, 1, 3, 2, 4).reshape(experts, rows, 3 * hidden)


def split_grads(blocked):
    experts, rows, total = blocked.shape
    hidden = total // 3
    tiles = hidden // FB
    parts = blocked.reshape(experts, rows, tiles, 3, FB).transpose(0, 1, 3, 2, 4)
    return (
        parts[:, :, :2].reshape(experts, rows, 2, hidden),
        parts[:, :, 2].reshape(experts, rows, hidden),
    )


def fetch_expert(blocked):
    experts = blocked.shape[0]
    size = lax.axis_size("fsdp")
    same_core, cores, _, across = member_groups(size, experts)
    got = lax.all_to_all(blocked, "fsdp", 0, 0, axis_index_groups=same_core, tiled=True)
    got = lax.all_gather(got, "fsdp", axis=1, axis_index_groups=cores, tiled=True)
    got = got.reshape(-1, got.shape[-1])
    if size > 2 * experts:
        got = lax.all_gather(got, "fsdp", axis=0, axis_index_groups=across, tiled=True)
    return lax.all_gather(got, "tp", axis=0)


def return_grads(grads, experts):
    size = lax.axis_size("fsdp")
    same_core, cores, _, across = member_groups(size, experts)
    columns = grads.shape[-1]
    if size > 2 * experts:
        grads = lax.psum_scatter(
            grads, "fsdp", scatter_dimension=1, axis_index_groups=across, tiled=True
        )
    grads = grads.reshape(2, experts, -1, columns)
    grads = lax.psum_scatter(
        grads, "fsdp", scatter_dimension=2, axis_index_groups=cores, tiled=True
    )
    grads = lax.psum_scatter(grads, "tp", scatter_dimension=0)
    return lax.all_to_all(grads, "fsdp", 0, 0, axis_index_groups=same_core, tiled=True)


def exchange(values, experts):
    whole = member_groups(lax.axis_size("fsdp"), experts)[2]
    return lax.all_to_all(values, "fsdp", 0, 0, axis_index_groups=whole, tiled=True)


def nt_dot(left, right):
    return lax.dot_general(left, right, (((1,), (1,)), ((), ())), preferred_element_type=jnp.float32)


def nn_dot(left, right):
    return jnp.dot(left, right, preferred_element_type=jnp.float32)


def expert_kernel(x_ref, g_ref, w_ref, back_ref, grads_ref, xt_ref, gt_ref, res_ref, dx_ref):
    step = pl.program_id(0)

    @pl.when(step == 0)
    def _():
        xt_ref[...] = x_ref[...].T
        gt_ref[...] = g_ref[...].T
        res_ref[...] = jnp.zeros_like(res_ref)
        dx_ref[...] = jnp.zeros_like(dx_ref)

    w_gate = w_ref[0, :, :FB]
    w_up = w_ref[0, :, FB : 2 * FB]
    w_out = w_ref[0, :, 2 * FB :]
    gate = nn_dot(x_ref[...], w_gate)
    up = nn_dot(x_ref[...], w_up)
    sig = 1.0 / (1.0 + jnp.exp(-gate))
    silu = gate * sig
    act = (silu * up).astype(jnp.bfloat16)
    res_ref[...] += nt_dot(act, w_out)
    grads_ref[0, :, 2 * FB :] = nn_dot(gt_ref[...], act).astype(jnp.bfloat16)
    d_act = nn_dot(g_ref[...], w_out)
    d_up = (d_act * silu).astype(jnp.bfloat16)
    d_gate = (d_act * up * sig * (1.0 + gate * (1.0 - sig))).astype(jnp.bfloat16)
    dx_ref[...] += nt_dot(d_gate, w_gate) + nt_dot(d_up, w_up)
    grads_ref[0, :, :FB] = nn_dot(xt_ref[...], d_gate).astype(jnp.bfloat16)
    grads_ref[0, :, FB : 2 * FB] = nn_dot(xt_ref[...], d_up).astype(jnp.bfloat16)

    @pl.when(step == pl.num_programs(0) - 1)
    def _():
        width = res_ref.shape[1]
        back_ref[:, :width] = res_ref[...].astype(jnp.bfloat16)
        back_ref[:, width:] = dx_ref[...].astype(jnp.bfloat16)


def run_expert(arrived, weights):
    rows = arrived.shape[0]
    width = arrived.shape[1] // 2
    halves, _, total = weights.shape
    tiles = total // (3 * FB)
    return pl.pallas_call(
        expert_kernel,
        grid=(halves * tiles,),
        in_specs=[
            pl.BlockSpec((rows, width), lambda j: (0, 0)),
            pl.BlockSpec((rows, width), lambda j: (0, 1)),
            pl.BlockSpec((1, width, 3 * FB), lambda j: (j // tiles, 0, j % tiles)),
        ],
        out_specs=[
            pl.BlockSpec((rows, 2 * width), lambda j: (0, 0)),
            pl.BlockSpec((1, width, 3 * FB), lambda j: (j // tiles, 0, j % tiles)),
        ],
        out_shape=[
            jax.ShapeDtypeStruct((rows, 2 * width), jnp.bfloat16),
            jax.ShapeDtypeStruct(weights.shape, jnp.bfloat16),
        ],
        scratch_shapes=[
            pltpu.VMEM((width, rows), jnp.bfloat16),
            pltpu.VMEM((width, rows), jnp.bfloat16),
            pltpu.VMEM((rows, width), jnp.float32),
            pltpu.VMEM((rows, width), jnp.float32),
        ],
        compiler_params=pltpu.CompilerParams(vmem_limit_bytes=60 << 20),
        cost_estimate=pl.CostEstimate(
            flops=18 * rows * width * total * halves // 3,
            bytes_accessed=4 * weights.size + 8 * rows * width,
            transcendentals=rows * total * halves // 3,
        ),
    )(arrived, arrived, weights)


def tn_dot(left, right):
    return lax.dot_general(left, right, (((0,), (0,)), ((), ())), preferred_element_type=jnp.float32)


def low(values):
    return values.astype(jnp.bfloat16)


def wide(values):
    return values.astype(jnp.float32)


def rotary_tables(length):
    half = HD // 2
    positions = np.arange(length, dtype=np.float32)
    inverse = np.power(np.float32(10000.0), -np.arange(half, dtype=np.float32) / np.float32(half))
    angles = (positions[:, None] * inverse[None, :].astype(np.float32)).astype(np.float32)
    cosine = np.cos(angles.astype(np.float64)).astype(np.float32)
    sine = np.sin(angles.astype(np.float64)).astype(np.float32)
    return (
        np.concatenate([cosine] * 4, axis=1),
        np.concatenate([-sine, sine, -sine, sine], axis=1),
    )


def turn(values, cosine, sine):
    lane = lax.broadcasted_iota(jnp.int32, values.shape, 1)
    upper = lax.rem(lane, HD) >= HD // 2
    partner = jnp.where(
        upper, pltpu.roll(values, HD // 2, 1), pltpu.roll(values, PAIR - HD // 2, 1)
    )
    return values * cosine + partner * sine


def head_lanes(shape, half, axis):
    return (lax.broadcasted_iota(jnp.int32, shape, axis) >= HD) == bool(half)


def mean_last(values):
    return jnp.mean(values, axis=-1, keepdims=True)


def greet_partner():
    partner = 1 - lax.axis_index("tp")
    barrier = pltpu.get_barrier_semaphore()
    pl.semaphore_signal(barrier, inc=1, device_id={"tp": partner}, device_id_type=MESH)
    pl.semaphore_wait(barrier, 1)


def to_partner(source, target, send_sem, recv_sem):
    return pltpu.make_async_remote_copy(
        src_ref=source,
        dst_ref=target,
        send_sem=send_sem,
        recv_sem=recv_sem,
        device_id={"tp": 1 - lax.axis_index("tp")},
        device_id_type=MESH,
    )


def block_rows(block):
    return slice(block * BLOCK, (block + 1) * BLOCK)


def column(values, index):
    return values[:, index : index + 1]


def lane_matrix(shape, columns):
    lane = lax.broadcasted_iota(jnp.int32, shape, 1)
    total = jnp.zeros(shape, jnp.float32)
    for index, values in columns:
        total = jnp.where(lane == index, values, total)
    return total


def forward_kernel(
    hid_ref,
    tok_in_ref,
    wqkv_ref,
    wout_ref,
    small_ref,
    rows_ref,
    cos_ref,
    sin_ref,
    s1_ref,
    qkv_ref,
    lse_ref,
    mixed_ref,
    mid_ref,
    s2_ref,
    tok_ref,
    vt_ref,
    send_ref,
    recv_ref,
    send_sem,
    recv_sem,
):
    greet_partner()
    blocks = hid_ref.shape[0] // BLOCK
    heads_width = wout_ref.shape[1]
    pairs = heads_width // PAIR
    gain_one = rows_ref[0:1, :]
    gain_two = rows_ref[1:2, :]
    copies = []
    lse_ref[...] = jnp.zeros_like(lse_ref)
    for block in range(blocks):
        rows = block_rows(block)
        keys = (block + 1) * BLOCK
        source = wide(hid_ref[rows, :])
        s1 = low(source * lax.rsqrt(mean_last(source * source) + EPSILON) * gain_one)
        s1_ref[rows, :] = s1
        cosine, sine = cos_ref[rows, :], sin_ref[rows, :]
        for part in range(3):
            projected = nn_dot(s1, wqkv_ref[:, part * heads_width : (part + 1) * heads_width])
            for pair in range(pairs):
                chunk = projected[:, pair * PAIR : (pair + 1) * PAIR]
                if part < 2:
                    chunk = turn(chunk, cosine, sine)
                else:
                    vt_ref[pair * PAIR : (pair + 1) * PAIR, rows] = low(chunk.T)
                start = part * heads_width + pair * PAIR
                qkv_ref[rows, start : start + PAIR] = low(chunk)
        for pair in range(pairs):
            lanes = slice(pair * PAIR, (pair + 1) * PAIR)
            query = qkv_ref[rows, lanes] * jnp.bfloat16(SCALING)
            key = qkv_ref[:keys, heads_width + pair * PAIR : heads_width + (pair + 1) * PAIR]
            value_t = vt_ref[lanes, :keys]
            gathered = None
            for half in range(2):
                masked = jnp.where(head_lanes(query.shape, half, 1), query, jnp.bfloat16(0))
                scores = nt_dot(key, masked)
                highest = jnp.max(scores, axis=0, keepdims=True)
                expanded = jnp.exp(scores - highest)
                totals = jnp.sum(expanded, axis=0, keepdims=True)
                probs = low(expanded * (1.0 / totals))
                lse_ref[2 * pair + half : 2 * pair + half + 1, rows] = highest + jnp.log(totals)
                found = nn_dot(value_t, probs)
                gathered = (
                    found
                    if half == 0
                    else jnp.where(head_lanes(found.shape, 1, 0), found, gathered)
                )
            mixed_ref[rows, lanes] = low(gathered.T)
        send_ref[block] = low(nt_dot(mixed_ref[rows, :], wout_ref[...]))
        copy = to_partner(
            send_ref.at[block], recv_ref.at[block], send_sem.at[block], recv_sem.at[block]
        )
        copy.start()
        copies.append(copy)
    for block in range(blocks):
        rows = block_rows(block)
        copies[block].wait()
        mid = wide(hid_ref[rows, :]) + (wide(send_ref[block]) + wide(recv_ref[block]))
        mid_ref[rows, :] = mid
        s2 = low(mid * lax.rsqrt(mean_last(mid * mid) + EPSILON) * gain_two)
        s2_ref[rows, :] = s2
        tok = tok_in_ref[rows, :]
        lane = lax.broadcasted_iota(jnp.int32, tok.shape, 1)
        logits = nn_dot(s2, small_ref[...]) + tok
        picked = [
            jnp.sum(
                jnp.where(wide(lane - ROUTER) == column(tok, ROUTE + member), logits, 0.0),
                axis=1,
                keepdims=True,
            )
            for member in range(2)
        ]
        gate = [
            1.0 / (1.0 + jnp.exp(picked[1 - member] - picked[member])) for member in range(2)
        ]
        tok_ref[rows, :] = jnp.where(
            lane == GATE, gate[0], jnp.where(lane == GATE + 1, gate[1], tok)
        )


def backward_kernel(
    dx_ref,
    pres_ref,
    slot_ref,
    tok_ref,
    cot_ref,
    mid_ref,
    s1_ref,
    qkv_ref,
    lse_ref,
    mixed_ref,
    wqkv_ref,
    wout_ref,
    small_ref,
    rows_ref,
    cos_ref,
    sin_ref,
    own_ref,
    grad_ref,
    base_ref,
    other_ref,
    big_ref,
    gsend_ref,
    grecv_ref,
    hsend_ref,
    hrecv_ref,
    gmid_ref,
    gown_ref,
    kt_ref,
    gm_ref,
    dqt_ref,
    dk_ref,
    dv_ref,
    gp_ref,
    acc_qkv_ref,
    acc_out_ref,
    acc_small_ref,
    acc_gain_ref,
    gsend_sem,
    grecv_sem,
    hsend_sem,
    hrecv_sem,
):
    greet_partner()
    tp = lax.axis_index("tp")
    width = dx_ref.shape[1]
    blocks = cot_ref.shape[0] // BLOCK
    heads_width = wout_ref.shape[1]
    pairs = heads_width // PAIR
    gain_one = rows_ref[0:1, :]
    gain_two = rows_ref[1:2, :]
    slot_row = slot_ref[1:2, :]
    share_row = slot_ref[0:1, :]
    order = list(reversed(range(blocks)))
    first = order[0]
    gcopies = {}
    for block in order:
        rows = block_rows(block)
        tok = tok_ref[rows, :]
        hits = [column(tok, TARGET + member) == slot_row for member in range(2)]
        onehot = low(jnp.where(hits[0] | hits[1], 1.0, 0.0))
        shares = [
            jnp.sum(jnp.where(hit, share_row, 0.0), axis=1, keepdims=True) for hit in hits
        ]
        high = [wide(low(share)) for share in shares]
        gsend_ref[block, :, :width] = low(nn_dot(onehot, dx_ref[...]))
        gsend_ref[block, :, width:] = low(
            lane_matrix(
                tok.shape,
                [
                    (0, high[0]),
                    (1, shares[0] - high[0]),
                    (2, high[1]),
                    (3, shares[1] - high[1]),
                ],
            )
        )
        copy = to_partner(
            gsend_ref.at[block], grecv_ref.at[block], gsend_sem.at[block], grecv_sem.at[block]
        )
        copy.start()
        gcopies[block] = copy
        placed = nn_dot(onehot, pres_ref[...])
        slab = slice((block % 2) * BLOCK, (block % 2 + 1) * BLOCK)

        @pl.when(tp == block // 2)
        def _():
            base_ref[slab, :] = placed

        @pl.when(tp != block // 2)
        def _():
            other_ref[slab, :] = low(placed)

    kt_ref[...] = qkv_ref[:, heads_width : 2 * heads_width].T
    for block in order:
        rows = block_rows(block)
        keys = (block + 1) * BLOCK
        slab = slice((block % 2) * BLOCK, (block % 2 + 1) * BLOCK)
        mine = tp == block // 2
        mine_f = jnp.where(mine, 1.0, 0.0)
        mid = mid_ref[rows, :]
        cot = cot_ref[rows, :]
        cot_wide = wide(cot)
        tok = tok_ref[rows, :]
        scale = lax.rsqrt(mean_last(mid * mid) + EPSILON)
        unit = mid * scale
        normed = unit * gain_two
        s2 = low(normed)
        small = small_ref[...]
        mixing = nn_dot(s2, small)
        value_dot = nn_dot(cot, small)
        normed_dot = jnp.sum(normed * cot_wide, axis=1, keepdims=True)
        route = [column(tok, ROUTE + member) for member in range(2)]
        gate = [column(tok, GATE + member) for member in range(2)]

        def weight_of(expert):
            return sum(jnp.where(route[m] == expert, gate[m], 0.0) for m in range(2))

        copy_weight = weight_of(COPY)
        copy_share = [jnp.where(route[m] == COPY, normed_dot, 0.0) for m in range(2)]
        alpha = copy_weight
        columns = []
        value_columns = []
        for c in range(2):
            weight = weight_of(COPY + 1 + c)
            left = column(mixing, MIXING + 2 * c)
            right = column(mixing, MIXING + 2 * c + 1)
            a0 = 1.0 / (1.0 + jnp.exp(right - left))
            a1 = 1.0 / (1.0 + jnp.exp(left - right))
            vd = column(value_dot, VALUE + c)
            alpha = alpha + weight * a0
            for m in range(2):
                copy_share[m] = copy_share[m] + jnp.where(
                    route[m] == COPY + 1 + c, a0 * normed_dot + a1 * vd, 0.0
                )
            slope = a0 * a1 * weight * (normed_dot - vd)
            columns.append((MIXING + 2 * c, slope))
            columns.append((MIXING + 2 * c + 1, -slope))
            value_columns.append((VALUE + c, weight * a1))
        value_matrix = lane_matrix(tok.shape, value_columns)
        base = mid + alpha * normed + nt_dot(low(value_matrix), small)

        @pl.when(mine)
        def _():
            base_ref[slab, :] += base

        gcopies[block].wait()
        extra = wide(gsend_ref[block, :, width:]) + wide(grecv_ref[block, :, width:])
        share = [
            column(extra, 2 * m) + column(extra, 2 * m + 1) + gate[m] * copy_share[m]
            for m in range(2)
        ]
        lane = lax.broadcasted_iota(jnp.int32, tok.shape, 1)
        slopes = lane_matrix(tok.shape, columns)
        for m in range(2):
            local = share[m] - gate[m] * (share[0] + share[1])
            slopes = slopes + jnp.where(wide(lane - ROUTER) == route[m], local, 0.0)
        slopes_low = low(slopes)
        grad_normed = (
            wide(gsend_ref[block, :, :width])
            + wide(grecv_ref[block, :, :width])
            + alpha * cot_wide
            + nt_dot(slopes_low, small)
        )
        small_grad = tn_dot(s2, low(slopes * mine_f)) + tn_dot(cot, low(value_matrix * mine_f))
        gain_grad = jnp.sum(unit * grad_normed, axis=0, keepdims=True) * mine_f
        scaled = grad_normed * gain_two
        grad_mid = cot_wide + scale * (scaled - unit * mean_last(scaled * unit))
        gmid_ref[rows, :] = grad_mid
        attended = low(grad_mid)
        out_grad = tn_dot(attended, mixed_ref[rows, :])
        gm_ref[...] = low(nn_dot(attended, wout_ref[...]))
        if block == first:
            acc_small_ref[...] = small_grad
            acc_gain_ref[...] = jnp.broadcast_to(gain_grad, acc_gain_ref.shape)
            acc_out_ref[...] = out_grad
        else:
            acc_small_ref[...] += small_grad
            acc_gain_ref[...] += jnp.broadcast_to(gain_grad, acc_gain_ref.shape)
            acc_out_ref[...] += out_grad
        cosine, sine = cos_ref[rows, :], sin_ref[rows, :]

        def one_pair(pair, carry):
            start = pl.multiple_of(pair * PAIR, PAIR)
            lanes = pl.ds(start, PAIR)
            key_lanes = pl.ds(pl.multiple_of(heads_width + start, PAIR), PAIR)
            value_lanes = pl.ds(pl.multiple_of(2 * heads_width + start, PAIR), PAIR)
            query = qkv_ref[rows, lanes] * jnp.bfloat16(SCALING)
            key = qkv_ref[:keys, key_lanes]
            value = qkv_ref[:keys, value_lanes]
            grad_out = gm_ref[:, lanes]
            key_t = kt_ref[lanes, :keys]
            grad_value = None
            for half in range(2):
                keep = head_lanes(query.shape, half, 1)
                q_half = jnp.where(keep, query, jnp.bfloat16(0))
                g_half = jnp.where(keep, grad_out, jnp.bfloat16(0))
                probs = jnp.exp(nt_dot(key, q_half) - lse_ref[pl.ds(2 * pair + half, 1), rows])
                grad_probs = nt_dot(value, g_half)
                inner = jnp.sum(probs * grad_probs, axis=0, keepdims=True)
                grad_scores = low(probs * (grad_probs - inner))
                value_part = nn_dot(low(probs), g_half)
                key_part = nn_dot(grad_scores, q_half)
                query_part = nn_dot(key_t, grad_scores)
                if half == 0:
                    grad_value, grad_key, grad_query = value_part, key_part, query_part
                else:
                    grad_value = grad_value + value_part
                    grad_key = grad_key + key_part
                    grad_query = jnp.where(
                        head_lanes(query_part.shape, 1, 0), query_part, grad_query
                    )
            if block == first:
                dv_ref[:keys, lanes] = grad_value
                dk_ref[:keys, lanes] = grad_key
            else:
                dv_ref[:keys, lanes] += grad_value
                dk_ref[:keys, lanes] += grad_key
            gp_ref[:, lanes] = low(turn(grad_query.T * SCALING, cosine, -sine))
            gp_ref[:, key_lanes] = low(turn(dk_ref[rows, lanes], cosine, -sine))
            gp_ref[:, value_lanes] = low(dv_ref[rows, lanes])
            return carry

        lax.fori_loop(0, pairs, one_pair, 0)
        gp = gp_ref[...]
        qkv_grad = tn_dot(s1_ref[rows, :], gp)
        if block == first:
            acc_qkv_ref[...] = qkv_grad
        else:
            acc_qkv_ref[...] += qkv_grad
        stream_grad = nt_dot(gp, wqkv_ref[...])

        @pl.when(mine)
        def _():
            gown_ref[block % 2] = stream_grad

        @pl.when(jnp.logical_not(mine))
        def _():
            hsend_ref[block % 2] = low(stream_grad)
            to_partner(
                hsend_ref.at[block % 2],
                hrecv_ref.at[block % 2],
                hsend_sem.at[block % 2],
                hrecv_sem.at[block % 2],
            ).start()

    big_ref[:, : 3 * heads_width] = low(acc_qkv_ref[...])
    big_ref[:, 3 * heads_width : 4 * heads_width] = low(acc_out_ref[...])
    gain_rows = acc_gain_ref[0:1, :]
    tall = jnp.where(
        lax.broadcasted_iota(jnp.int32, (PAIR, width), 0) == 1,
        jnp.broadcast_to(gain_rows, (PAIR, width)),
        0.0,
    )
    big_ref[:, 4 * heads_width :] = low(acc_small_ref[...] + tall.T)
    for slot in reversed(range(2)):
        slab = slice(slot * BLOCK, (slot + 1) * BLOCK)
        to_partner(
            hsend_ref.at[slot], hrecv_ref.at[slot], hsend_sem.at[slot], hrecv_sem.at[slot]
        ).wait()
        source = wide(own_ref[slab, :])
        scale = lax.rsqrt(mean_last(source * source) + EPSILON)
        unit = source * scale
        scaled = (gown_ref[slot] + wide(hrecv_ref[slot])) * gain_one
        mid_rows = pl.ds(pl.multiple_of(tp * 2 * BLOCK + slot * BLOCK, BLOCK), BLOCK)
        grad_ref[slab, :] = gmid_ref[mid_rows, :] + scale * (
            scaled - unit * mean_last(scaled * unit)
        )


def run_forward(hid, tok, wqkv, wout, small, rows, cosine, sine):
    length, width = hid.shape
    heads_width = wout.shape[1]
    blocks = length // BLOCK
    vmem = pl.BlockSpec(memory_space=pltpu.VMEM)
    low_t, wide_t = jnp.bfloat16, jnp.float32
    return pl.pallas_call(
        forward_kernel,
        in_specs=[vmem] * 8,
        out_specs=[vmem] * 7,
        out_shape=[
            jax.ShapeDtypeStruct((length, width), low_t),
            jax.ShapeDtypeStruct((length, 3 * heads_width), low_t),
            jax.ShapeDtypeStruct((8, length), wide_t),
            jax.ShapeDtypeStruct((length, heads_width), low_t),
            jax.ShapeDtypeStruct((length, width), wide_t),
            jax.ShapeDtypeStruct((length, width), low_t),
            jax.ShapeDtypeStruct((length, PAIR), wide_t),
        ],
        scratch_shapes=[
            pltpu.VMEM((heads_width, length), low_t),
            pltpu.VMEM((blocks, BLOCK, width), low_t),
            pltpu.VMEM((blocks, BLOCK, width), low_t),
            pltpu.SemaphoreType.DMA((blocks,)),
            pltpu.SemaphoreType.DMA((blocks,)),
        ],
        compiler_params=pltpu.CompilerParams(
            collective_id=0, has_side_effects=True, vmem_limit_bytes=60 << 20
        ),
    )(hid, tok, wqkv, wout, small, rows, cosine, sine)


def run_backward(*operands):
    dx, tok, cot, own, wout = operands[0], operands[3], operands[4], operands[16], operands[11]
    length, width = cot.shape
    heads_width = wout.shape[1]
    blocks = length // BLOCK
    own_rows = own.shape[0]
    vmem = pl.BlockSpec(memory_space=pltpu.VMEM)
    low_t, wide_t = jnp.bfloat16, jnp.float32
    dma = pltpu.SemaphoreType.DMA
    return pl.pallas_call(
        backward_kernel,
        in_specs=[vmem] * 17,
        out_specs=[vmem] * 4,
        out_shape=[
            jax.ShapeDtypeStruct((own_rows, width), wide_t),
            jax.ShapeDtypeStruct((own_rows, width), wide_t),
            jax.ShapeDtypeStruct((own_rows, width), low_t),
            jax.ShapeDtypeStruct((width, 4 * heads_width + PAIR), low_t),
        ],
        scratch_shapes=[
            pltpu.VMEM((blocks, BLOCK, width + PAIR), low_t),
            pltpu.VMEM((blocks, BLOCK, width + PAIR), low_t),
            pltpu.VMEM((2, BLOCK, width), low_t),
            pltpu.VMEM((2, BLOCK, width), low_t),
            pltpu.VMEM((length, width), wide_t),
            pltpu.VMEM((2, BLOCK, width), wide_t),
            pltpu.VMEM((heads_width, length), low_t),
            pltpu.VMEM((BLOCK, heads_width), low_t),
            pltpu.VMEM((PAIR, BLOCK), wide_t),
            pltpu.VMEM((length, heads_width), wide_t),
            pltpu.VMEM((length, heads_width), wide_t),
            pltpu.VMEM((BLOCK, 3 * heads_width), low_t),
            pltpu.VMEM((width, 3 * heads_width), wide_t),
            pltpu.VMEM((width, heads_width), wide_t),
            pltpu.VMEM((width, PAIR), wide_t),
            pltpu.VMEM((8, width), wide_t),
            dma((blocks,)),
            dma((blocks,)),
            dma((2,)),
            dma((2,)),
        ],
        compiler_params=pltpu.CompilerParams(
            collective_id=1, has_side_effects=True, vmem_limit_bytes=60 << 20
        ),
    )(*operands)


def shards(
    hidden,
    prev_logits,
    routes,
    slot_rank,
    dropped,
    cotangent,
    attn_norm,
    ffn_norm,
    w_qkv,
    w_attn_out,
    w_router,
    w_const_gate,
    w_const_value,
    w_expert_in,
    w_expert_out,
):
    own_rows, width = hidden.shape
    length = own_rows * lax.axis_size("tp")
    experts = w_expert_in.shape[0]
    route_count = w_router.shape[1]
    capacity = 9 * length // (4 * route_count)
    blocked = fetch_expert(blocked_weights(w_expert_in, w_expert_out))
    heads_width = w_attn_out.shape[1]
    small = jnp.concatenate(
        [attn_norm[:, None], ffn_norm[:, None], w_router, w_const_gate, w_const_value], axis=1
    )
    small = jnp.pad(small, ((0, 0), (0, PAIR - small.shape[1])))
    small = lax.all_gather(small, "tp", axis=0, tiled=True)
    packed_weights = lax.all_gather(
        jnp.concatenate([w_qkv.reshape(-1, 3 * heads_width), w_attn_out, small], axis=1),
        "fsdp",
        axis=0,
        tiled=True,
    )
    wqkv = packed_weights[:, : 3 * heads_width]
    wout = packed_weights[:, 3 * heads_width : 4 * heads_width]
    small = packed_weights[:, 4 * heads_width :]
    rows = small[:, :8].T.astype(jnp.float32)
    cosine, sine = (jnp.asarray(table) for table in rotary_tables(length))
    kept = (routes < experts) & (dropped == 0)
    target = jnp.where(kept, routes * capacity + slot_rank, -1)
    tok = jnp.concatenate(
        [prev_logits.T, wide(routes).T, wide(target).T], axis=0
    )
    tok = gather_columns(tok)
    tok = jnp.concatenate(
        [
            jnp.zeros((ROUTER, length), jnp.float32),
            tok[:route_count],
            jnp.zeros((ROUTE - ROUTER - route_count, length), jnp.float32),
            tok[route_count:],
            jnp.zeros((PAIR - ROUTE - 4, length), jnp.float32),
        ],
        axis=0,
    ).T
    hid = gather_rows(hidden)
    cot = gather_rows(cotangent)
    s1, qkv, lse, mixed, mid, s2, tok = run_forward(
        hid, tok, wqkv, wout, small, rows, cosine, sine
    )
    half = capacity // 2
    slot = jnp.arange(experts * half)
    slot = (slot // half) * capacity + lax.axis_index("tp") * half + slot % half
    lines = tok[:, TARGET : TARGET + 4].T
    hits = [lines[member][None, :] == wide(slot)[:, None] for member in range(2)]
    dispatch = low(hits[0] | hits[1])
    slot_gate = sum(
        jnp.sum(jnp.where(hits[member], lines[2 + member][None, :], 0.0), axis=1)
        for member in range(2)
    )
    packed = low(nn_dot(dispatch, s2))
    gated = low(nn_dot(dispatch, cot) * slot_gate[:, None])
    arrived = exchange(jnp.concatenate([packed, gated], axis=1), experts)
    answer, grads_exp = run_expert(arrived, blocked)
    answer = exchange(answer, experts)
    grads_exp = return_grads(grads_exp, experts)
    slot_result = wide(answer[:, :width])
    slot_share = jnp.sum(slot_result * wide(gated), axis=1)
    slot_rows = jnp.concatenate(
        [slot_share[None, :], wide(slot)[None, :], jnp.zeros((6, slot.shape[0]), jnp.float32)],
        axis=0,
    )
    grad_hidden, base, for_other, big = run_backward(
        answer[:, width:],
        low(slot_result * slot_gate[:, None]),
        slot_rows,
        tok,
        cot,
        mid,
        s1,
        qkv,
        lse,
        mixed,
        wqkv,
        wout,
        small,
        rows,
        cosine,
        sine,
        hidden,
    )
    output = low(base + wide(swap(for_other)))
    reduced = wide(lax.psum_scatter(big, "fsdp", scatter_dimension=0, tiled=True))
    grad_qkv = reduced[:, : 3 * heads_width].reshape(w_qkv.shape)
    grad_attn_out = reduced[:, 3 * heads_width : 4 * heads_width]
    gain_share = jnp.sum(grad_qkv * wide(w_qkv), axis=(1, 2))
    last = jnp.concatenate([gain_share[:, None], reduced[:, 4 * heads_width + 1 :]], axis=1)
    last = own_half(last) + swap(other_half(last))
    grad_in_exp, grad_out_exp = split_grads(wide(grads_exp))
    return (
        output,
        grad_hidden,
        last[:, 0] / wide(attn_norm),
        last[:, 1],
        grad_qkv,
        grad_attn_out,
        last[:, ROUTER:MIXING],
        last[:, MIXING:VALUE],
        last[:, VALUE : VALUE + 2],
        grad_in_exp,
        grad_out_exp,
    )


def solution(mesh):
    in_specs = (
        P(("fsdp", "tp"), None),
        P(("fsdp", "tp"), None),
        P(("fsdp", "tp"), None),
        P(("fsdp", "tp"), None),
        P(("fsdp", "tp"), None),
        P(("fsdp", "tp"), None),
        P(("fsdp", "tp")),
        P(("fsdp", "tp")),
        P("fsdp", None, "tp"),
        P("fsdp", "tp"),
        P(("fsdp", "tp"), None),
        P(("fsdp", "tp"), None),
        P(("fsdp", "tp"), None),
        P(None, "fsdp", None, "tp"),
        P(None, "fsdp", "tp"),
    )
    out_specs = (
        P(("fsdp", "tp"), None),
        P(("fsdp", "tp"), None),
        P(("fsdp", "tp")),
        P(("fsdp", "tp")),
        P("fsdp", None, "tp"),
        P("fsdp", "tp"),
        P(("fsdp", "tp"), None),
        P(("fsdp", "tp"), None),
        P(("fsdp", "tp"), None),
        P(None, "fsdp", None, "tp"),
        P(None, "fsdp", "tp"),
    )
    return jax.shard_map(shards, mesh=mesh, in_specs=in_specs, out_specs=out_specs, check_vma=False)
```

time: 658 us -> 607 us (0.922)
  Pallas kernels: 30.8 us -> 181 us
  matrix products: 82.5 us -> 3.1 us
  waiting for transfers between devices: 259 us -> 189 us
  other arithmetic: 74.6 us -> 18.8 us
  blocking collectives: 71 us -> 121 us
  local copies, waits for them, and re-layouts: 85.3 us -> 55.9 us
  starting transfers between devices: 27.9 us -> 16.9 us
    pallas_call x0 -> x2, Pallas kernels: none -> 150 us  [the longest x1 81.6 us: run_forward(): pl.pallas_call(forward_kernel, in_specs=[vmem] * 8, out_specs=[vmem] * 7,...]
    ppermute x11 -> x5, waiting for transfers between devices: 123 us -> 34.6 us  [swap(): return lax.ppermute(values, 'tp', [(0, 1), (1, 0)])]
    dot_general x26 -> x0, matrix products: 75.1 us -> none  [the longest x2 14.6 us: shards(): jnp.einsum('qhd,khd->hqk', grad_block, values_all[:key_stop], preferred_e...]
    all_to_all x0 -> x1, blocking collectives: none -> 59.3 us  [fetch_expert(): lax.all_to_all(blocked, 'fsdp', 0, 0, axis_index_groups=same_core, tiled=...]
    all_gather x1, waiting for transfers between devices: 36.1 us -> 2.43 us  [shards(): lax.all_gather(jnp.concatenate([w_qkv.reshape(-1, 3 * heads_width), w_att...]
    reduce_scatter x1, waiting for transfers between devices: 53.5 us -> 77.6 us  [shards(): lax.psum_scatter(big, 'fsdp', scatter_dimension=0, tiled=True)]
    unnamed x292 -> x42, local copies, waits for them, and re-layouts: 29.1 us -> 5.39 us
    reduce_sum x16 -> x3, other arithmetic: 23.6 us -> 2.86 us  [the longest x1 1.66 us: shards(): slot_share = jnp.sum(slot_result * wide(gated), axis=1)]
  transfers between devices with their start and end apart: 20 -> 13, of which waited for: 9 -> 6; matrix products, arithmetic and copies ran while one was open for 31% -> 6% of each run, Pallas kernels for 0% -> 25%
where the time goes in v2:
time: 607 us; the launch traced here: 600 us
  waiting for transfers between devices  189 us (31%)
  Pallas kernels  181 us (30%)
  blocking collectives  121 us (20%)
  local copies, waits for them, and re-layouts  55.9 us (9%)
  other arithmetic  18.8 us (3%)
  starting transfers between devices  16.9 us (3%)
  between operations  14.9 us (2%)
    pallas_call x1, Pallas kernels, run_forward(): pl.pallas_call(forward_kernel, in_specs=[vmem] * 8, out_specs=[vmem] * 7,...  81.6 us
    reduce_scatter x1, waiting for transfers between devices, shards(): lax.psum_scatter(big, 'fsdp', scatter_dimension=0, tiled=True)  77.6 us
    pallas_call x1, Pallas kernels, run_backward(): pl.pallas_call(backward_kernel, in_specs=[vmem] * 17, out_specs=[vmem] *...  68.2 us
    all_to_all x1, blocking collectives, fetch_expert(): lax.all_to_all(blocked, 'fsdp', 0, 0, axis_index_groups=same_core, tiled=...  59.3 us
    all_to_all x1, blocking collectives, exchange(): lax.all_to_all(values, 'fsdp', 0, 0, axis_index_groups=whole, tiled=True)  57.8 us
    all_to_all x1, waiting for transfers between devices, exchange(): lax.all_to_all(values, 'fsdp', 0, 0, axis_index_groups=whole, tiled=True)  48.7 us
    ppermute x5, waiting for transfers between devices, swap(): return lax.ppermute(values, 'tp', [(0, 1), (1, 0)])  34.6 us
    pallas_call x1, Pallas kernels, run_expert(): pl.pallas_call(expert_kernel, grid=(halves * tiles,), in_specs=[pl.BlockS...  30.8 us
  transfers between devices with their start and end apart: 13, of which 6 were waited for; matrix products, arithmetic and copies ran while one was open for 6% of the time, Pallas kernels for 25%

profile of v2, /device:TPU:12, one launch (start us, length us, event | category | flops | bytes accessed | tf_op | source)
XLA Modules:
  0.0 600.5 jit_solution(393017768053230271)
XLA Ops:
  7.2 4.5 reshape.144
  11.8 4.6 maximum_bitcast_fusion
  16.4 4.9 reshape.138
  21.2 59.3 %all_to_all.33 = bf16[8,48,3072]{2,1,0:T(8,128)(2,1)} all-to-all(bf16[8,48,3072]{2,1,0:T(8,128)(2,1)} %reshape.138), channel_id=1, replica_groups={{0,4,8,12,16,20,24,28},{2,6,10,14,18,22,26,30},{1,5,9,13,17,21,25,29},{..., dimensions={0} | all-to-all | bytes 4718592 | tf_op jit(solution)/shard_map/all_to_all | solution.py:97
  80.7 0.8 copy-done.4
  81.5 0.1 copy.125
  81.9 0.1 copy.129
  82.0 0.1 concatenate.37
  82.1 4.4 all_gather.12
  86.4 0.7 pad_maximum_fusion.3
  87.2 7.6 %all-gather.6.cloned.1.call-done = bf16[8,96,3072]{2,1,0:T(8,128)(2,1)} async-done(((bf16[8,48,3072]{2,1,0:T(8,128)(2,1)}), bf16[8,96,3072]{2,1,0:T(8,128)(2,1)}) %all-gather.6.cloned.1.call-update) | async-done | bytes 4718608 | tf_op jit(solution)/shard_map/all_gather | solution.py:98
  94.9 1.0 copy-done
  96.0 0.6 collective-permute-start
  96.5 1.5 collective-permute-start.2
  98.0 0.6 collective-permute-start.1
  98.7 34.6 %collective-permute-done.1 = f32[16,512]{1,0:T(8,128)S(1)} collective-permute-done((f32[16,512]{1,0:T(8,128)S(1)}, f32[16,512]{1,0:T(8,128)S(1)}, u32[]{:S(2)}, u32[]{:S(2)}) %collective-permute-start.1) | collective-permute-done | bytes 32800 | tf_op jit(solution)/shard_map/ppermute | solution.py:30
  133.3 0.2 copy.122
  133.5 0.2 copy.123
  133.9 1.7 concatenate.36
  135.7 1.8 broadcast_select_fusion.1
  137.5 1.3 pad_maximum_fusion.1.hid_ref
  138.8 2.4 all-gather.4.cloned.1.call-done
  141.3 0.9 slice.98
  142.3 2.9 slice.95.wqkv_ref
  145.2 1.9 slice.96.wout_ref
  147.1 1.7 slice.97.small_ref
  148.8 0.6 convert_bitcast_fusion.rows_ref
  149.4 81.6 %shard_map.248 = (bf16[1024,768]{1,0:T(8,128)(2,1)}, bf16[1024,1152]{1,0:T(8,128)(2,1)}, f32[8,1024]{1,0:T(8,128)}, bf16[1024,384]{1,0:T(8,128)(2,1)}, f32[1024,...) custom-call(bf16[1024,768]{1,0:T(8,128)(2,1)} %pad_maximum_fusion.1.hid_ref, f32[1024,128]{1,0:T(8,128)} %bitcast.44, ...), custom_call_target="tpu_custom_call" | custom-call | tf_op jit(solution)/shard_map/pallas_call | solution.py:656
  231.0 1.2 slice_bitcast_fusion
  232.3 1.0 slice_reduce_fusion.1
  233.3 0.8 fusion.1
  234.1 1.6 multiply_convert_fusion
  235.7 1.6 fusion.12
  237.2 0.2 pad_maximum_fusion
  237.4 57.8 %all_to_all.34 = bf16[16,48,1536]{2,1,0:T(8,128)(2,1)} all-to-all(bf16[16,48,1536]{2,1,0:T(8,128)(2,1)S(1)} %bitcast.37), channel_id=1, replica_groups={{0,2,4,6,8,10,12,14,16,18,20,22,24,26,28,30},{1,3,5,7,9,11,13,15,17,19,..., dimensions={0} | all-to-all | bytes 4718592 | tf_op jit(solution)/shard_map/all_to_all | solution.py:123
  295.2 30.8 %shard_map.249 = (bf16[768,1536]{1,0:T(8,128)(2,1)}, bf16[2,768,3072]{2,1,0:T(8,128)(2,1)}) custom-call(bf16[768,1536]{1,0:T(8,128)(2,1)} %bitcast.42, bf16[768,1536]{1,0:T(8,128)(2,1)} %bitcast.43, bf16[2,768,3072]{2,1,0:T(8,128)(2,1)} %all-gather.8.cloned.1.call-done.w_ref), custom_call_target="tpu_custom_call" | custom-call | flops 21743271936 | bytes 23592960 | tf_op jit(solution)/shard_map/pallas_call | solution.py:173
  326.1 17.6 %reduce-scatter.6.cloned.1.call-done = bf16[2,8,48,3072]{3,2,1,0:T(8,128)(2,1)} async-done(((bf16[2,8,96,3072]{3,2,1,0:T(8,128)(2,1)}), bf16[2,8,48,3072]{3,2,1,0:T(8,128)(2,1)}) %reduce-scatter.6.cloned.1.call-update) | async-done | bytes 4718608 | tf_op jit(solution)/shard_map/reduce_scatter | solution.py:114
  343.8 6.1 %all-to-all-start.2 = ((bf16[16,48,1536]{2,1,0:T(8,128)(2,1)}), bf16[16,48,1536]{2,1,0:T(8,128)(2,1)S(1)}, u32[]{:S(2)}, u32[]{:S(2)}) async-start(bf16[16,48,1536]{2,1,0:T(8,128)(2,1)} %bitcast.41), calls=%async_computation.2 | async-start | bytes 4718592 | tf_op jit(solution)/shard_map/all_to_all | solution.py:123
  350.0 2.6 pad_maximum_fusion.2.cot_ref
  352.6 48.7 %all-to-all-done.2 = bf16[16,48,1536]{2,1,0:T(8,128)(2,1)S(1)} async-done(((bf16[16,48,1536]{2,1,0:T(8,128)(2,1)}), bf16[16,48,1536]{2,1,0:T(8,128)(2,1)S(1)}, u32[]{:S(2)}, u32[]{:S(2)}) %all-to-all-start.2) | async-done | bytes 2359328 | tf_op jit(solution)/shard_map/all_to_all | solution.py:123
  401.3 1.1 slice.103.dx_ref
  402.4 1.7 fusion.5
  404.1 0.7 maximum_maximum_fusion.slot_ref
  404.8 68.2 %shard_map.250 = (f32[512,768]{1,0:T(8,128)}, f32[512,768]{1,0:T(8,128)}, bf16[512,768]{1,0:T(8,128)(2,1)}, bf16[768,1664]{1,0:T(8,128)(2,1)}) custom-call(bf16[768,768]{1,0:T(8,128)(2,1)} %slice.103.dx_ref, bf16[768,768]{1,0:T(8,128)(2,1)} %get-tuple-element.101.pres_ref, f32[8,768]{1,0:T(8,128)} %maximum_maximum_fusion.slot_ref, ...), custom_call_target="tpu_custom_call" | custom-call | tf_op jit(solution)/shard_map/pallas_call | solution.py:691
  473.0 6.9 %all-to-all-start.3 = ((bf16[8,48,3072]{2,1,0:T(8,128)(2,1)}), bf16[8,48,3072]{2,1,0:T(8,128)(2,1)S(1)}, u32[]{:S(2)}, u32[]{:S(2)}) async-start(bf16[8,48,3072]{2,1,0:T(8,128)(2,1)} %bitcast.40), calls=%async_computation.6 | async-start | bytes 4718592 | tf_op jit(solution)/shard_map/all_to_all | solution.py:118
  479.9 0.5 collective-permute-start.3
  480.4 77.6 %reduce-scatter.4.cloned.1.call-done = bf16[48,1664]{1,0:T(8,128)(2,1)} async-done(((bf16[768,1664]{1,0:T(8,128)(2,1)}), bf16[48,1664]{1,0:T(8,128)(2,1)}) %reduce-scatter.4.cloned.1.call-update) | async-done | bytes 159760 | tf_op jit(solution)/shard_map/reduce_scatter | solution.py:832
  558.0 0.9 slice.105
  559.0 0.4 multiply_reduce_fusion
  559.6 0.8 slice.106
  560.4 0.5 collective-permute-start.4
  561.0 2.6 add_convert_fusion
  563.6 0.7 copy.148
  564.3 1.4 slice.109
  566.0 0.7 copy.138
  566.7 0.7 copy.139
  567.3 0.6 copy.140
  568.0 0.7 slice_reduce_fusion.5
  568.7 0.5 convert_divide_fusion
  569.2 6.1 %reshape.143 = f32[8,48,2,3,512]{4,3,2,1,0:T(4,128)} reshape(bf16[8,48,3072]{2,1,0:T(8,128)(2,1)S(1)} %all-to-all-done.3) | data formatting | bytes 7077888 | tf_op jit(solution)/shard_map/transpose | solution.py:86
  575.3 6.0 slice.113
  581.3 8.2 %slice_reduce_fusion = f32[8,48,2,512]{3,2,1,0:T(2,128)S(1)} fusion(f32[8,48,3,2,512]{4,2,3,1,0:T(4,128)} %bitcast.33), kind=kLoop, calls=%fused_computation.14 | loop fusion | bytes 3145728 | tf_op jit(solution)/shard_map/slice | solution.py:89
  589.5 2.5 reshape_squeeze.3
  592.0 1.1 copy.150
  (78 shorter events, 1.7 us)
Async XLA Ops:
  7.2 87.7 %all-gather.6.cloned.1.call-start = ((), (), s32[]{:S(2)}) async-start(), calls=%async_computation.8 | async-start | bytes 7077888 | tf_op jit(solution)/shard_map/all_gather | solution.py:98
  80.5 0.9 copy-start.4
  80.5 0.9 copy-start.15
  80.5 1.0 copy-start.13
  80.5 1.1 copy-start.11
  80.5 1.2 copy-start.12
  80.6 1.3 copy-start.14
  80.6 5.9 copy-start.7
  80.6 60.7 %all-gather.4.cloned.1.call-start = ((), (), s32[]{:S(2)}) async-start(), calls=%async_computation.7 | async-start | bytes 2715648 | tf_op jit(solution)/shard_map/all_gather | solution.py:758
  87.1 208.1 %all-gather.8.cloned.1.call-start = ((), (), s32[]{:S(2)}) async-start(), calls=%async_computation.9 | async-start | bytes 14155776 | tf_op jit(solution)/shard_map/all_gather | solution.py:102
  94.8 1.1 copy-start
  94.8 3.2 copy-start.8
  94.8 3.2 copy-start.9
  94.8 3.2 copy-start.10
  94.8 3.2 copy-start.6
  94.9 248.9 %reduce-scatter.6.cloned.1.call-start = ((), (), s32[]{:S(2)}) async-start(), calls=%async_computation.11 | async-start | bytes 14155776 | tf_op jit(solution)/shard_map/reduce_scatter | solution.py:114
  96.0 39.7 %collective-permute-start = (bf16[512,768]{1,0:T(8,128)(2,1)S(1)}, bf16[512,768]{1,0:T(8,128)(2,1)}, u32[]{:S(2)}, u32[]{:S(2)}) collective-permute-start(bf16[512,768]{1,0:T(8,128)(2,1)S(1)} %copy-done), channel_id=1, source_target_pairs={{0,1},{1,0},{2,3},{3,2},{4,5},{5,4},{6,7},{7,6},{8,9},{9,8},{10,11... | collective-permute-start | bytes 2359304 | tf_op jit(solution)/shard_map/ppermute | solution.py:30
  96.5 39.1 %collective-permute-start.2 = (bf16[512,768]{1,0:T(8,128)(2,1)}, bf16[512,768]{1,0:T(8,128)(2,1)}, u32[]{:S(2)}, u32[]{:S(2)}) collective-permute-start(bf16[512,768]{1,0:T(8,128)(2,1)} %param.22), channel_id=1, source_target_pairs={{0,1},{1,0},{2,3},{3,2},{4,5},{5,4},{6,7},{7,6},{8,9},{9,8},{10,11... | collective-permute-start | bytes 2359304 | tf_op jit(solution)/shard_map/ppermute | solution.py:30
  98.0 35.2 %collective-permute-start.1 = (f32[16,512]{1,0:T(8,128)S(1)}, f32[16,512]{1,0:T(8,128)S(1)}, u32[]{:S(2)}, u32[]{:S(2)}) collective-permute-start(f32[16,512]{1,0:T(8,128)S(1)} %pad_maximum_fusion.4), channel_id=1, source_target_pairs={{0,1},{1,0},{2,3},{3,2},{4,5},{5,4},{6,7},{7,6},{8,9},{9,8},{10,11... | collective-permute-start | bytes 98312 | tf_op jit(solution)/shard_map/ppermute | solution.py:30
  137.5 96.6 %copy-start.1 = (bf16[512,768]{1,0:T(8,128)(2,1)}, bf16[512,768]{1,0:T(8,128)(2,1)S(1)}, u32[]{:S(2)}) copy-start(bf16[512,768]{1,0:T(8,128)(2,1)S(1)} %get-tuple-element.102) | copy-start | bytes 2359300
  137.5 96.6 %copy-start.2 = (bf16[512,768]{1,0:T(8,128)(2,1)}, bf16[512,768]{1,0:T(8,128)(2,1)S(1)}, u32[]{:S(2)}) copy-start(bf16[512,768]{1,0:T(8,128)(2,1)S(1)} %get-tuple-element.103) | copy-start | bytes 2359300
  234.1 1.6 copy-start.16
  326.0 146.9 %reduce-scatter.8.cloned.1.call-start = ((), (), s32[]{:S(2)}) async-start(), calls=%async_computation.12 | async-start | bytes 7077888 | tf_op jit(solution)/shard_map/reduce_scatter | solution.py:117
  343.8 57.6 %all-to-all-start.2 = ((bf16[16,48,1536]{2,1,0:T(8,128)(2,1)}), bf16[16,48,1536]{2,1,0:T(8,128)(2,1)S(1)}, u32[]{:S(2)}, u32[]{:S(2)}) async-start(bf16[16,48,1536]{2,1,0:T(8,128)(2,1)} %bitcast.41), calls=%async_computation.2 | async-start | bytes 4718592 | tf_op jit(solution)/shard_map/all_to_all | solution.py:123
  349.9 208.2 %reduce-scatter.4.cloned.1.call-start = ((), (), s32[]{:S(2)}) async-start(), calls=%async_computation.10 | async-start | bytes 2715648 | tf_op jit(solution)/shard_map/reduce_scatter | solution.py:832
  473.0 86.0 %copy-start.5 = (bf16[48,3,384]{2,0,1:T(8,128)(2,1)S(1)}, bf16[48,3,384]{2,0,1:T(8,128)(2,1)}, u32[]{:S(2)}) copy-start(bf16[48,3,384]{2,0,1:T(8,128)(2,1)} %param.25) | copy-start | bytes 331780
  473.0 96.2 %all-to-all-start.3 = ((bf16[8,48,3072]{2,1,0:T(8,128)(2,1)}), bf16[8,48,3072]{2,1,0:T(8,128)(2,1)S(1)}, u32[]{:S(2)}, u32[]{:S(2)}) async-start(bf16[8,48,3072]{2,1,0:T(8,128)(2,1)} %bitcast.40), calls=%async_computation.6 | async-start | bytes 4718592 | tf_op jit(solution)/shard_map/all_to_all | solution.py:118
  479.9 81.1 %collective-permute-start.3 = (bf16[512,768]{1,0:T(8,128)(2,1)}, bf16[512,768]{1,0:T(8,128)(2,1)}, u32[]{:S(2)}, u32[]{:S(2)}) collective-permute-start(bf16[512,768]{1,0:T(8,128)(2,1)} %get-tuple-element.33), channel_id=1, source_target_pairs={{0,1},{1,0},{2,3},{3,2},{4,5},{5,4},{6,7},{7,6},{8,9},{9,8},{10,11... | collective-permute-start | bytes 2359304 | tf_op jit(solution)/shard_map/ppermute | solution.py:30
  560.4 5.3 collective-permute-start.4
  589.5 2.5 copy-start.3
Sparse Core Ops, SparseCore 0:
  80.7 14.0 all-gather.5
  97.6 43.6 all-gather.3
  142.8 149.8 all-gather.7
  326.2 17.5 reduce-scatter.5
  345.9 59.9 reduce-scatter.7
  473.1 84.8 reduce-scatter.3

commit v3 on v2

--- a/solution.py
+++ b/solution.py
@@ -18,12 +18,12 @@
 MIXING = 14
 VALUE = 18
 ROUTE = 20
-TARGET = 22
-GATE = 24
+TARGET = 24
+GATE = 26
 COPY = 9
 
 
-FB = 512
+TILE = 256
 
 
 def swap(values):
@@ -48,79 +48,75 @@
     return lax.dynamic_slice_in_dim(values, (1 - lax.axis_index("tp")) * half, half, 0)
 
 
-def gather_columns(values):
-    other = swap(values)
-    first = lax.axis_index("tp") == 0
-    return jnp.concatenate(
-        [jnp.where(first, values, other), jnp.where(first, other, values)], axis=1
-    )
-
-
 def member_groups(size, experts):
     span = 2 * experts
     starts = range(0, size, span)
-    same_core = [[start + 2 * e + c for e in range(experts)] for start in starts for c in range(2)]
     cores = [[start + 2 * e, start + 2 * e + 1] for start in starts for e in range(experts)]
-    whole = [[start + r for r in range(span)] for start in starts]
     across = [[start + r for start in starts] for r in range(span)]
-    return same_core, cores, whole, across
-
-
-def blocked_weights(w_expert_in, w_expert_out):
-    experts, rows, _, hidden = w_expert_in.shape
-    tiles = hidden // FB
-    both = jnp.concatenate(
-        [
-            w_expert_in.reshape(experts, rows, 2, tiles, FB),
-            w_expert_out.reshape(experts, rows, 1, tiles, FB),
-        ],
-        axis=2,
-    )
-    return both.transpose(0, 1, 3, 2, 4).reshape(experts, rows, 3 * hidden)
-
-
-def split_grads(blocked):
-    experts, rows, total = blocked.shape
-    hidden = total // 3
-    tiles = hidden // FB
-    parts = blocked.reshape(experts, rows, tiles, 3, FB).transpose(0, 1, 3, 2, 4)
-    return (
-        parts[:, :, :2].reshape(experts, rows, 2, hidden),
-        parts[:, :, 2].reshape(experts, rows, hidden),
-    )
-
-
-def fetch_expert(blocked):
-    experts = blocked.shape[0]
+    return cores, across
+
+
+def own_core(values, rows):
+    parts = values.reshape(-1, 2, rows, values.shape[-1])
+    return lax.dynamic_index_in_dim(parts, lax.axis_index("fsdp") % 2, 1, keepdims=False)
+
+
+def join_weights(got, experts):
     size = lax.axis_size("fsdp")
-    same_core, cores, _, across = member_groups(size, experts)
-    got = lax.all_to_all(blocked, "fsdp", 0, 0, axis_index_groups=same_core, tiled=True)
+    if size == 2 * experts:
+        return got
+    cores, across = member_groups(size, experts)
     got = lax.all_gather(got, "fsdp", axis=1, axis_index_groups=cores, tiled=True)
     got = got.reshape(-1, got.shape[-1])
-    if size > 2 * experts:
-        got = lax.all_gather(got, "fsdp", axis=0, axis_index_groups=across, tiled=True)
-    return lax.all_gather(got, "tp", axis=0)
-
-
-def return_grads(grads, experts):
+    got = lax.all_gather(got, "fsdp", axis=0, axis_index_groups=across, tiled=True)
+    return own_core(got, got.shape[0] // (2 * experts))
+
+
+def split_grads(grads):
+    experts, _, columns = grads.shape
     size = lax.axis_size("fsdp")
-    same_core, cores, _, across = member_groups(size, experts)
-    columns = grads.shape[-1]
-    if size > 2 * experts:
-        grads = lax.psum_scatter(
-            grads, "fsdp", scatter_dimension=1, axis_index_groups=across, tiled=True
-        )
-    grads = grads.reshape(2, experts, -1, columns)
+    if size == 2 * experts:
+        return grads
+    cores, across = member_groups(size, experts)
+    grads = lax.all_gather(grads[:, None], "fsdp", axis=1, axis_index_groups=cores, tiled=True)
+    grads = grads.reshape(-1, columns)
     grads = lax.psum_scatter(
-        grads, "fsdp", scatter_dimension=2, axis_index_groups=cores, tiled=True
-    )
-    grads = lax.psum_scatter(grads, "tp", scatter_dimension=0)
-    return lax.all_to_all(grads, "fsdp", 0, 0, axis_index_groups=same_core, tiled=True)
-
-
-def exchange(values, experts):
-    whole = member_groups(lax.axis_size("fsdp"), experts)[2]
-    return lax.all_to_all(values, "fsdp", 0, 0, axis_index_groups=whole, tiled=True)
+        grads, "fsdp", scatter_dimension=0, axis_index_groups=across, tiled=True
+    )
+    return own_core(grads, grads.shape[0] // (2 * experts))
+
+
+def gather_plain(block, small, tok, hid, cot):
+    size = lax.axis_size("fsdp")
+    small = lax.all_gather(small, ("fsdp", "tp"), axis=0, tiled=True)
+    tok = lax.all_gather(tok, "tp", axis=1, tiled=True).T
+    return (
+        lax.all_gather(block, "fsdp", axis=0),
+        low(small),
+        small.T[:8],
+        tok,
+        gather_rows(hid),
+        gather_rows(cot),
+    )
+
+
+def finish_plain(big, wqkv, other, base, arrived):
+    heads_width = (big.shape[1] - PAIR) // 4
+    reduced = wide(lax.psum_scatter(big, "fsdp", scatter_dimension=0, tiled=True))
+    flat = reduced[:, : 3 * heads_width]
+    share = jnp.sum(flat * wide(wqkv), axis=1, keepdims=True)
+    last = jnp.concatenate([share, reduced[:, 4 * heads_width + 1 :]], axis=1)
+    experts, rows, columns = arrived.shape
+    hidden = columns // 3
+    wide_grads = wide(arrived)
+    return (
+        low(base + wide(swap(other))),
+        flat.reshape(-1, 3, heads_width),
+        reduced[:, 3 * heads_width : 4 * heads_width],
+        own_half(last) + swap(other_half(last)),
+        wide_grads[:, :, : 2 * hidden].reshape(experts, rows, 2, hidden),
+        wide_grads[:, :, 2 * hidden :],
+    )
 
 
 def nt_dot(left, right):
@@ -129,76 +125,6 @@
 
 def nn_dot(left, right):
     return jnp.dot(left, right, preferred_element_type=jnp.float32)
-
-
-def expert_kernel(x_ref, g_ref, w_ref, back_ref, grads_ref, xt_ref, gt_ref, res_ref, dx_ref):
-    step = pl.program_id(0)
-
-    @pl.when(step == 0)
-    def _():
-        xt_ref[...] = x_ref[...].T
-        gt_ref[...] = g_ref[...].T
-        res_ref[...] = jnp.zeros_like(res_ref)
-        dx_ref[...] = jnp.zeros_like(dx_ref)
-
-    w_gate = w_ref[0, :, :FB]
-    w_up = w_ref[0, :, FB : 2 * FB]
-    w_out = w_ref[0, :, 2 * FB :]
-    gate = nn_dot(x_ref[...], w_gate)
-    up = nn_dot(x_ref[...], w_up)
-    sig = 1.0 / (1.0 + jnp.exp(-gate))
-    silu = gate * sig
-    act = (silu * up).astype(jnp.bfloat16)
-    res_ref[...] += nt_dot(act, w_out)
-    grads_ref[0, :, 2 * FB :] = nn_dot(gt_ref[...], act).astype(jnp.bfloat16)
-    d_act = nn_dot(g_ref[...], w_out)
-    d_up = (d_act * silu).astype(jnp.bfloat16)
-    d_gate = (d_act * up * sig * (1.0 + gate * (1.0 - sig))).astype(jnp.bfloat16)
-    dx_ref[...] += nt_dot(d_gate, w_gate) + nt_dot(d_up, w_up)
-    grads_ref[0, :, :FB] = nn_dot(xt_ref[...], d_gate).astype(jnp.bfloat16)
-    grads_ref[0, :, FB : 2 * FB] = nn_dot(xt_ref[...], d_up).astype(jnp.bfloat16)
-
-    @pl.when(step == pl.num_programs(0) - 1)
-    def _():
-        width = res_ref.shape[1]
-        back_ref[:, :width] = res_ref[...].astype(jnp.bfloat16)
-        back_ref[:, width:] = dx_ref[...].astype(jnp.bfloat16)
-
-
-def run_expert(arrived, weights):
-    rows = arrived.shape[0]
-    width = arrived.shape[1] // 2
-    halves, _, total = weights.shape
-    tiles = total // (3 * FB)
-    return pl.pallas_call(
-        expert_kernel,
-        grid=(halves * tiles,),
-        in_specs=[
-            pl.BlockSpec((rows, width), lambda j: (0, 0)),
-            pl.BlockSpec((rows, width), lambda j: (0, 1)),
-            pl.BlockSpec((1, width, 3 * FB), lambda j: (j // tiles, 0, j % tiles)),
-        ],
-        out_specs=[
-            pl.BlockSpec((rows, 2 * width), lambda j: (0, 0)),
-            pl.BlockSpec((1, width, 3 * FB), lambda j: (j // tiles, 0, j % tiles)),
-        ],
-        out_shape=[
-            jax.ShapeDtypeStruct((rows, 2 * width), jnp.bfloat16),
-            jax.ShapeDtypeStruct(weights.shape, jnp.bfloat16),
-        ],
-        scratch_shapes=[
-            pltpu.VMEM((width, rows), jnp.bfloat16),
-            pltpu.VMEM((width, rows), jnp.bfloat16),
-            pltpu.VMEM((rows, width), jnp.float32),
-            pltpu.VMEM((rows, width), jnp.float32),
-        ],
-        compiler_params=pltpu.CompilerParams(vmem_limit_bytes=60 << 20),
-        cost_estimate=pl.CostEstimate(
-            flops=18 * rows * width * total * halves // 3,
-            bytes_accessed=4 * weights.size + 8 * rows * width,
-            transcendentals=rows * total * halves // 3,
-        ),
-    )(arrived, arrived, weights)
 
 
 def tn_dot(left, right):
@@ -243,13 +169,6 @@
     return jnp.mean(values, axis=-1, keepdims=True)
 
 
-def greet_partner():
-    partner = 1 - lax.axis_index("tp")
-    barrier = pltpu.get_barrier_semaphore()
-    pl.semaphore_signal(barrier, inc=1, device_id={"tp": partner}, device_id_type=MESH)
-    pl.semaphore_wait(barrier, 1)
-
-
 def to_partner(source, target, send_sem, recv_sem):
     return pltpu.make_async_remote_copy(
         src_ref=source,
@@ -275,6 +194,777 @@
     for index, values in columns:
         total = jnp.where(lane == index, values, total)
     return total
+
+
+def send_to(source, target, send_sem, recv_sem, device):
+    return pltpu.make_async_remote_copy(
+        src_ref=source,
+        dst_ref=target,
+        send_sem=send_sem,
+        recv_sem=recv_sem,
+        device_id=device,
+        device_id_type=MESH,
+    )
+
+
+def greet_group(peers):
+    me = lax.axis_index("fsdp")
+    rank = lax.rem(me, peers)
+    barrier = pltpu.get_barrier_semaphore()
+    for k in range(1, peers):
+        pl.semaphore_signal(
+            barrier,
+            inc=1,
+            device_id={"fsdp": me - rank + lax.rem(rank + k, peers)},
+            device_id_type=MESH,
+        )
+    pl.semaphore_signal(
+        barrier, inc=1, device_id={"tp": 1 - lax.axis_index("tp")}, device_id_type=MESH
+    )
+    pl.semaphore_wait(barrier, peers)
+
+
+def each(first, last, body):
+    def step(k, carry):
+        body(k)
+        return carry
+
+    lax.fori_loop(first, last, step, 0)
+
+
+class CoreExchange:
+    def __init__(self, source, target, send_sem, recv_sem):
+        experts = source.shape[0]
+        me = lax.axis_index("fsdp")
+        rank = lax.rem(me, 2 * experts)
+        core = lax.rem(rank, 2)
+        mine = rank // 2
+
+        def copy(k):
+            ahead = lax.rem(mine + k, experts)
+            return send_to(
+                source.at[ahead],
+                target.at[mine],
+                send_sem.at[k],
+                recv_sem.at[k],
+                {"fsdp": me - rank + 2 * ahead + core},
+            )
+
+        def arrival(k):
+            behind = lax.rem(mine + experts - k, experts)
+            return send_to(
+                source.at[behind],
+                target.at[behind],
+                send_sem.at[k],
+                recv_sem.at[k],
+                {"fsdp": me - rank + 2 * behind + core},
+            )
+
+        self.experts, self.copy, self.arrival = experts, copy, arrival
+        self.source, self.target, self.mine = source, target, mine
+
+    def start(self):
+        each(1, self.experts, lambda k: self.copy(k).start())
+        self.target[self.mine] = self.source[self.mine]
+
+    def wait(self):
+        each(1, self.experts, lambda k: self.copy(k).wait_send())
+        each(1, self.experts, lambda k: self.arrival(k).wait_recv())
+
+
+def gather_kernel(
+    block_ref,
+    small_ref,
+    tok_ref,
+    hid_ref,
+    cot_ref,
+    all_ref,
+    small_out_ref,
+    rows_out_ref,
+    tok_out_ref,
+    hid_out_ref,
+    cot_out_ref,
+    small_all_ref,
+    tok_all_ref,
+    y_send,
+    y_recv,
+    up_send,
+    up_recv,
+    down_send,
+    down_recv,
+    x_send,
+    x_recv,
+    core_send,
+    core_recv,
+):
+    size = all_ref.shape[0]
+    planes = size // 4
+    me = lax.axis_index("fsdp")
+    tp = lax.axis_index("tp")
+    z, x, core = me // 4, lax.rem(me // 2, 2), lax.rem(me, 2)
+    shard = small_ref.shape[0]
+    own_rows = hid_ref.shape[0]
+    greet_group(size)
+    partner = {"tp": 1 - tp}
+    small_all_ref[me, tp] = small_ref[...]
+    small_y = send_to(small_ref, small_all_ref.at[me, tp], y_send.at[0], y_recv.at[0], partner)
+    small_y.start()
+    all_ref[me] = block_ref[...]
+    mine = pl.ds(pl.multiple_of(tp * own_rows, own_rows), own_rows)
+    hid_y = send_to(hid_ref, hid_out_ref.at[mine], y_send.at[1], y_recv.at[1], partner)
+    tok_y = send_to(tok_ref, tok_all_ref.at[tp], y_send.at[2], y_recv.at[2], partner)
+    cot_y = send_to(cot_ref, cot_out_ref.at[mine], y_send.at[3], y_recv.at[3], partner)
+    hid_y.start()
+    tok_y.start()
+
+    def number(plane, line):
+        return plane * 4 + line * 2 + core
+
+    def pieces(number_of, send, recv, slot, device, source=None):
+        first = all_ref.at[number_of] if source is None else source
+        return (
+            send_to(first, all_ref.at[number_of], send.at[0, slot], recv.at[0, slot], device),
+            send_to(
+                small_all_ref.at[number_of],
+                small_all_ref.at[number_of],
+                send.at[1, slot],
+                recv.at[1, slot],
+                device,
+            ),
+        )
+
+    def up(step, plane):
+        return pieces(
+            number(plane, x),
+            up_send,
+            up_recv,
+            step,
+            {"fsdp": number(lax.min(z + 1, planes - 1), x)},
+        )
+
+    def down(step, plane):
+        return pieces(
+            number(plane, x), down_send, down_recv, step, {"fsdp": number(lax.max(z - 1, 0), x)}
+        )
+
+    def side(plane, line):
+        return pieces(number(plane, line), x_send, x_recv, plane, {"fsdp": number(z, 1 - x)})
+
+    def sibling(plane, line, parity):
+        return pieces(
+            plane * 4 + line * 2 + parity,
+            core_send,
+            core_recv,
+            plane * 2 + line,
+            {"fsdp": me + 1 - 2 * core},
+        )
+
+    def run(group, verb):
+        for item in group:
+            getattr(item, verb)()
+
+    def spread(step, plane):
+        run(side(plane, x), "start")
+        run(sibling(plane, x, core), "start")
+
+    small_y.wait()
+    hid_out_ref[mine, :] = hid_ref[...]
+
+    @pl.when(z < planes - 1)
+    def _():
+        run(up(0, z), "start")
+
+    @pl.when(z > 0)
+    def _():
+        run(down(0, z), "start")
+
+    spread(0, z)
+    cot_y.start()
+    tok_all_ref[tp] = tok_ref[...]
+    cot_out_ref[mine, :] = cot_ref[...]
+    for step in range(1, planes):
+
+        @pl.when(z >= step)
+        def _():
+            run(up(step - 1, z - step), "wait_recv")
+
+            @pl.when(z < planes - 1)
+            def _():
+                run(up(step, z - step), "start")
+
+            spread(step, z - step)
+
+        @pl.when(z + step < planes)
+        def _():
+            run(down(step - 1, z + step), "wait_recv")
+
+            @pl.when(z > 0)
+            def _():
+                run(down(step, z + step), "start")
+
+            spread(step, z + step)
+
+    for distance in range(planes):
+        plane = lax.rem(z + distance, planes)
+        run(side(plane, 1 - x), "wait_recv")
+        run(sibling(plane, 1 - x, core), "start")
+    for plane in range(planes):
+        for line in range(2):
+            run(sibling(plane, line, 1 - core), "wait_recv")
+    small_all = small_all_ref[...].reshape(size * 2 * shard, small_ref.shape[1])
+    small_out_ref[...] = low(small_all)
+    rows_out_ref[...] = small_all.T[:8, :]
+    tok_y.wait()
+    for part in range(2):
+        lanes = slice(part * own_rows, (part + 1) * own_rows)
+        tok_out_ref[lanes, :] = tok_all_ref[part].T
+    for step in range(planes):
+
+        @pl.when(jnp.logical_and(z >= step, z < planes - 1))
+        def _():
+            run(up(step, z - step), "wait_send")
+
+        @pl.when(jnp.logical_and(z + step < planes, z > 0))
+        def _():
+            run(down(step, z + step), "wait_send")
+
+    for plane in range(planes):
+        run(side(plane, x), "wait_send")
+        for line in range(2):
+            run(sibling(plane, line, core), "wait_send")
+    hid_y.wait()
+    cot_y.wait()
+
+
+def run_gather(block, small, tok, hid, cot):
+    size = lax.axis_size("fsdp")
+    own_rows, width = hid.shape
+    vmem = pl.BlockSpec(memory_space=pltpu.VMEM)
+    low_t, wide_t = jnp.bfloat16, jnp.float32
+    dma = pltpu.SemaphoreType.DMA
+    return pl.pallas_call(
+        gather_kernel,
+        in_specs=[vmem] * 5,
+        out_specs=[vmem] * 6,
+        out_shape=[
+            jax.ShapeDtypeStruct((size,) + block.shape, low_t),
+            jax.ShapeDtypeStruct((width, PAIR), low_t),
+            jax.ShapeDtypeStruct((8, width), wide_t),
+            jax.ShapeDtypeStruct((2 * own_rows, PAIR), wide_t),
+            jax.ShapeDtypeStruct((2 * own_rows, width), low_t),
+            jax.ShapeDtypeStruct((2 * own_rows, width), low_t),
+        ],
+        scratch_shapes=[
+            pltpu.VMEM((size, 2) + small.shape, wide_t),
+            pltpu.VMEM((2,) + tok.shape, wide_t),
+            dma((4,)),
+            dma((4,)),
+        ]
+        + [dma((2, size // 4))] * 6
+        + [dma((2, size // 2))] * 2,
+        compiler_params=pltpu.CompilerParams(
+            collective_id=3, has_side_effects=True, vmem_limit_bytes=60 << 20
+        ),
+    )(block, small, tok, hid, cot)
+
+
+def finish_kernel(
+    big_ref,
+    wqkv_ref,
+    other_ref,
+    base_ref,
+    expert_ref,
+    out_ref,
+    qkv_ref,
+    attn_ref,
+    tail_ref,
+    in_ref,
+    down_ref,
+    sum_ref,
+    core_ref,
+    side_ref,
+    acc_ref,
+    usend_ref,
+    urecv_ref,
+    dsend_ref,
+    drecv_ref,
+    y_ref,
+    tsend_ref,
+    trecv_ref,
+    core_send,
+    core_recv,
+    x_send,
+    x_recv,
+    up_send,
+    up_recv,
+    dn_send,
+    dn_recv,
+    y_send,
+    y_recv,
+):
+    size = big_ref.shape[0]
+    planes = size // 4
+    me = lax.axis_index("fsdp")
+    tp = lax.axis_index("tp")
+    z, x, core = me // 4, lax.rem(me // 2, 2), lax.rem(me, 2)
+    heads_width = attn_ref.shape[1]
+    greet_group(size)
+    partner = {"tp": 1 - tp}
+
+    def to_core(plane, line):
+        slot = plane * 2 + line
+        return send_to(
+            big_ref.at[plane * 4 + line * 2 + 1 - core],
+            core_ref.at[slot],
+            core_send.at[slot],
+            core_recv.at[slot],
+            {"fsdp": me + 1 - 2 * core},
+        )
+
+    def to_side(plane):
+        return send_to(
+            sum_ref.at[plane],
+            side_ref.at[plane],
+            x_send.at[plane],
+            x_recv.at[plane],
+            {"fsdp": z * 4 + (1 - x) * 2 + core},
+        )
+
+    def to_up(plane):
+        return send_to(
+            usend_ref.at[plane],
+            urecv_ref.at[plane],
+            up_send.at[plane],
+            up_recv.at[plane],
+            {"fsdp": lax.min(z + 1, planes - 1) * 4 + x * 2 + core},
+        )
+
+    def to_down(plane):
+        return send_to(
+            dsend_ref.at[plane],
+            drecv_ref.at[plane],
+            dn_send.at[plane],
+            dn_recv.at[plane],
+            {"fsdp": lax.max(z - 1, 0) * 4 + x * 2 + core},
+        )
+
+    for plane in range(planes):
+        to_core(plane, 1 - x).start()
+    for plane in range(planes):
+        to_core(plane, x).start()
+    out_y = send_to(other_ref, y_ref, y_send.at[0], y_recv.at[0], partner)
+    out_y.start()
+
+    def joined(plane, line):
+        to_core(plane, line).wait_recv()
+        return wide(big_ref[plane * 4 + line * 2 + core]) + wide(core_ref[plane * 2 + line])
+
+    for plane in range(planes):
+        sum_ref[plane] = low(joined(plane, 1 - x))
+        to_side(plane).start()
+    for plane in range(planes):
+        acc_ref[plane] = joined(plane, x)
+    experts, shard, total = expert_ref.shape
+    hidden = total // 3
+
+    def lay_out(e):
+        values = wide(expert_ref[e])
+        in_ref[e, :, 0, :] = values[:, :hidden]
+        in_ref[e, :, 1, :] = values[:, hidden : 2 * hidden]
+        down_ref[e] = values[:, 2 * hidden :]
+
+    each(0, experts, lay_out)
+    for plane in range(planes):
+        to_side(plane).wait_recv()
+        acc_ref[plane] += wide(side_ref[plane])
+
+    def rise(plane):
+        @pl.when(jnp.logical_and(z > 0, z <= plane))
+        def _():
+            to_up(plane).wait_recv()
+            acc_ref[plane] += wide(urecv_ref[plane])
+
+        @pl.when(z < plane)
+        def _():
+            usend_ref[plane] = low(acc_ref[plane])
+            to_up(plane).start()
+
+    def fall(plane):
+        @pl.when(jnp.logical_and(z < planes - 1, z >= plane))
+        def _():
+            to_down(plane).wait_recv()
+            acc_ref[plane] += wide(drecv_ref[plane])
+
+        @pl.when(z > plane)
+        def _():
+            dsend_ref[plane] = low(acc_ref[plane])
+            to_down(plane).start()
+
+    for step in range(planes):
+        rise(planes - 1 - step)
+        fall(step)
+    values = acc_ref[z]
+    flat = values[:, : 3 * heads_width]
+    for part in range(3):
+        qkv_ref[:, part, :] = flat[:, part * heads_width : (part + 1) * heads_width]
+    attn_ref[...] = values[:, 3 * heads_width : 4 * heads_width]
+    share = jnp.sum(flat * wide(wqkv_ref[...]), axis=1, keepdims=True)
+    last = values[:, 4 * heads_width :]
+    last = jnp.where(lax.broadcasted_iota(jnp.int32, last.shape, 1) == 0, share, last)
+    part_rows = tail_ref.shape[0]
+    tsend_ref[0] = last[:part_rows, :]
+    tsend_ref[1] = last[part_rows:, :]
+    tail_y = send_to(tsend_ref.at[1 - tp], trecv_ref, y_send.at[1], y_recv.at[1], partner)
+    tail_y.start()
+    out_y.wait()
+    out_ref[...] = low(base_ref[...] + wide(y_ref[...]))
+    tail_y.wait()
+    tail_ref[...] = tsend_ref[tp] + trecv_ref[...]
+    for plane in range(planes):
+        to_core(plane, 1 - x).wait_send()
+        to_core(plane, x).wait_send()
+        to_side(plane).wait_send()
+
+        @pl.when(z < plane)
+        def _():
+            to_up(plane).wait_send()
+
+        @pl.when(z > plane)
+        def _():
+            to_down(plane).wait_send()
+
+
+def run_finish(big, wqkv, other, base, arrived):
+    size = lax.axis_size("fsdp")
+    planes = size // 4
+    own_rows, width = base.shape
+    columns = big.shape[1]
+    heads_width = (columns - PAIR) // 4
+    shard = width // size
+    experts, _, total = arrived.shape
+    hidden = total // 3
+    vmem = pl.BlockSpec(memory_space=pltpu.VMEM)
+    low_t, wide_t = jnp.bfloat16, jnp.float32
+    dma = pltpu.SemaphoreType.DMA
+    line = (planes, shard, columns)
+    return pl.pallas_call(
+        finish_kernel,
+        in_specs=[vmem] * 5,
+        out_specs=[vmem] * 6,
+        out_shape=[
+            jax.ShapeDtypeStruct((own_rows, width), low_t),
+            jax.ShapeDtypeStruct((shard, 3, heads_width), wide_t),
+            jax.ShapeDtypeStruct((shard, heads_width), wide_t),
+            jax.ShapeDtypeStruct((shard // 2, PAIR), wide_t),
+            jax.ShapeDtypeStruct((experts, shard, 2, hidden), wide_t),
+            jax.ShapeDtypeStruct((experts, shard, hidden), wide_t),
+        ],
+        scratch_shapes=[
+            pltpu.VMEM(line, low_t),
+            pltpu.VMEM((2 * planes, shard, columns), low_t),
+            pltpu.VMEM(line, low_t),
+            pltpu.VMEM(line, wide_t),
+            pltpu.VMEM(line, low_t),
+            pltpu.VMEM(line, low_t),
+            pltpu.VMEM(line, low_t),
+            pltpu.VMEM(line, low_t),
+            pltpu.VMEM((own_rows, width), low_t),
+            pltpu.VMEM((2, shard // 2, PAIR), wide_t),
+            pltpu.VMEM((shard // 2, PAIR), wide_t),
+            dma((2 * planes,)),
+            dma((2 * planes,)),
+        ]
+        + [dma((planes,))] * 6
+        + [dma((2,))] * 2,
+        compiler_params=pltpu.CompilerParams(
+            collective_id=4, has_side_effects=True, vmem_limit_bytes=60 << 20
+        ),
+    )(big.reshape(size, shard, columns), wqkv, other, base, arrived)
+
+
+def expert_kernel(
+    s2_ref,
+    cot_ref,
+    line_ref,
+    slot_ref,
+    weight_ref,
+    res_out_ref,
+    dx_out_ref,
+    grads_out_ref,
+    xs_ref,
+    gs_ref,
+    x_ref,
+    g_ref,
+    w_ref,
+    gate_ref,
+    up_ref,
+    xt_ref,
+    gt_ref,
+    acc_ref,
+    grads_ref,
+    sibling_ref,
+    ysend_ref,
+    yrecv_ref,
+    w_sem,
+    grad_sem,
+    xs_sem,
+    xr_sem,
+    gs_sem,
+    gr_sem,
+    xfs_sem,
+    xfr_sem,
+    gfs_sem,
+    gfr_sem,
+    ys_sem,
+    yr_sem,
+    rs_sem,
+    rr_sem,
+    ds_sem,
+    dr_sem,
+):
+    peers, rows, width = xs_ref.shape
+    total = peers * rows
+    hidden = gate_ref.shape[1]
+    tiles = hidden // TILE
+    chunks = ysend_ref.shape[1]
+    chunk = total // chunks
+    group = peers // chunks
+    me = lax.axis_index("fsdp")
+    tp = lax.axis_index("tp")
+    rank = lax.rem(me, peers)
+    core = lax.rem(rank, 2)
+    start = me - rank
+
+    def ahead(k):
+        return start + lax.rem(rank + k, peers)
+
+    def behind(k):
+        return start + lax.rem(rank + peers - k, peers)
+
+    partner = {"tp": 1 - tp}
+    sibling = {"fsdp": start + rank + 1 - 2 * core}
+
+    def out_x(k):
+        return send_to(xs_ref.at[k], x_ref.at[0, k], xs_sem.at[k], xr_sem.at[k], {"fsdp": ahead(k)})
+
+    def out_g(k):
+        return send_to(gs_ref.at[k], g_ref.at[0, k], gs_sem.at[k], gr_sem.at[k], {"fsdp": ahead(k)})
+
+    def pass_x(k):
+        return send_to(x_ref.at[0, k], x_ref.at[1, k], xfs_sem.at[k], xfr_sem.at[k], partner)
+
+    def pass_g(k):
+        return send_to(g_ref.at[0, k], g_ref.at[1, k], gfs_sem.at[k], gfr_sem.at[k], partner)
+
+    def across(index, q):
+        return send_to(
+            ysend_ref.at[index, q],
+            yrecv_ref.at[index, q],
+            ys_sem.at[index, q],
+            yr_sem.at[index, q],
+            partner,
+        )
+
+    def back_res(k):
+        return send_to(
+            xs_ref.at[k], res_out_ref.at[k], rs_sem.at[k], rr_sem.at[k], {"fsdp": behind(k)}
+        )
+
+    def back_dx(k):
+        return send_to(
+            gs_ref.at[k], dx_out_ref.at[k], ds_sem.at[k], dr_sem.at[k], {"fsdp": behind(k)}
+        )
+
+    greet_group(peers)
+    here = pltpu.make_async_copy(weight_ref, w_ref.at[:, core], w_sem.at[0])
+    here.start()
+    there = send_to(weight_ref, w_ref.at[:, core], w_sem.at[1], w_sem.at[2], sibling)
+    there.start()
+
+    half = total // 2
+    halves = []
+    for part in range(2):
+        blocks = slice(part * peers // 2, (part + 1) * peers // 2)
+        ids = slot_ref[part * half : (part + 1) * half, 0:1]
+        hits = [line_ref[m : m + 1, :] == ids for m in range(2)]
+        gate = sum(
+            jnp.sum(jnp.where(hits[m], line_ref[2 + m : 3 + m, :], 0.0), axis=1, keepdims=True)
+            for m in range(2)
+        )
+        onehot = low(jnp.where(hits[0] | hits[1], 1.0, 0.0))
+        xs_ref[blocks] = low(nn_dot(onehot, s2_ref[...])).reshape(peers // 2, rows, width)
+        if part == 0:
+            x_ref[0, 0] = xs_ref[0]
+            pass_x(0).start()
+        each(max(1, part * peers // 2), (part + 1) * peers // 2, lambda k: out_x(k).start())
+        halves.append((blocks, onehot, gate))
+    for part in range(2):
+        blocks, onehot, gate = halves[part]
+        gs_ref[blocks] = low(nn_dot(onehot, cot_ref[...]) * gate).reshape(peers // 2, rows, width)
+        if part == 0:
+            g_ref[0, 0] = gs_ref[0]
+            pass_g(0).start()
+        each(max(1, part * peers // 2), (part + 1) * peers // 2, lambda k: out_g(k).start())
+
+    def forward_x(k):
+        out_x(k).wait_recv()
+        pass_x(k).start()
+
+    each(1, peers, forward_x)
+    here.wait()
+    send_to(weight_ref, w_ref.at[:, 1 - core], w_sem.at[1], w_sem.at[2], sibling).wait_recv()
+    there.wait_send()
+    each(0, peers, lambda k: pass_x(k).wait_recv())
+
+    def weights(which, lanes):
+        return w_ref[:, :, :, pl.ds(pl.multiple_of(which * hidden + lanes, TILE), TILE)].reshape(
+            width, TILE
+        )
+
+    acc_ref[...] = jnp.zeros_like(acc_ref)
+
+    def forward_tile(tile, carry):
+        lanes = pl.multiple_of(tile * TILE, TILE)
+        x = x_ref[...].reshape(2 * total, width)
+        gate = nn_dot(x, weights(0, lanes))
+        up = nn_dot(x, weights(1, lanes))
+        gate_ref[:, pl.ds(lanes, TILE)] = low(gate)
+        up_ref[:, pl.ds(lanes, TILE)] = low(up)
+        act = low(gate / (1.0 + jnp.exp(-gate)) * up)
+        acc_ref[...] += nt_dot(act, weights(2, lanes))
+
+        def forward_g(k):
+            @pl.when(k > 0)
+            def _():
+                out_g(k).wait_recv()
+                pass_g(k).start()
+
+        each(tile * (peers // tiles), (tile + 1) * (peers // tiles), forward_g)
+        return carry
+
+    lax.fori_loop(0, tiles, forward_tile, 0)
+    each(1, peers, lambda k: out_x(k).wait_send())
+    xs_ref[...] = low(acc_ref[:total, :]).reshape(peers, rows, width)
+    ysend_ref[0] = low(acc_ref[total:, :]).reshape(chunks, chunk, width)
+    for q in range(chunks):
+        across(0, q).start()
+    xt_ref[...] = x_ref[...].reshape(2 * total, width).T
+    acc_ref[...] = jnp.zeros_like(acc_ref)
+    each(0, peers, lambda k: pass_g(k).wait_recv())
+    gt_ref[...] = g_ref[...].reshape(2 * total, width).T
+
+    def backward_tile(tile, carry):
+        lanes = pl.multiple_of(tile * TILE, TILE)
+        gate = wide(gate_ref[:, pl.ds(lanes, TILE)])
+        up = wide(up_ref[:, pl.ds(lanes, TILE)])
+        sig = 1.0 / (1.0 + jnp.exp(-gate))
+        silu = gate * sig
+        act = low(silu * up)
+        d_act = nn_dot(g_ref[...].reshape(2 * total, width), weights(2, lanes))
+        d_up = low(d_act * silu)
+        d_gate = low(d_act * up * sig * (1.0 + gate * (1.0 - sig)))
+        acc_ref[...] += nt_dot(d_gate, weights(0, lanes)) + nt_dot(d_up, weights(1, lanes))
+
+        def keep(which, values):
+            grads_ref[
+                :, :, :, pl.ds(pl.multiple_of(which * hidden + lanes, TILE), TILE)
+            ] = low(values).reshape(peers // 2, 2, rows, TILE)
+
+        keep(0, nn_dot(xt_ref[...], d_gate))
+        keep(1, nn_dot(xt_ref[...], d_up))
+        keep(2, nn_dot(gt_ref[...], act))
+
+        @pl.when(tile == 1)
+        def _():
+            for q in range(chunks):
+                across(0, q).wait_recv()
+                part = slice(q * group, (q + 1) * group)
+                xs_ref[part] = low(
+                    wide(xs_ref[part]) + wide(yrecv_ref[0, q]).reshape(group, rows, width)
+                )
+            res_out_ref[0] = xs_ref[0]
+            each(1, peers, lambda k: back_res(k).start())
+
+        return carry
+
+    lax.fori_loop(0, tiles, backward_tile, 0)
+    for q in range(chunks):
+        ysend_ref[1, q] = low(acc_ref[total + q * chunk : total + (q + 1) * chunk, :])
+        across(1, q).start()
+    swap_grads = send_to(
+        grads_ref.at[:, 1 - core], sibling_ref, grad_sem.at[0], grad_sem.at[1], sibling
+    )
+    swap_grads.start()
+    each(1, peers, lambda k: out_g(k).wait_send())
+    for q in range(chunks):
+        across(1, q).wait_recv()
+        part = slice(q * group, (q + 1) * group)
+        gs_ref[part] = low(
+            acc_ref[q * chunk : (q + 1) * chunk, :] + wide(yrecv_ref[1, q])
+        ).reshape(group, rows, width)
+        if q == 0:
+            dx_out_ref[0] = gs_ref[0]
+        each(max(1, q * group), (q + 1) * group, lambda k: back_dx(k).start())
+    swap_grads.wait()
+    grads_out_ref[...] = low(wide(grads_ref[:, core]) + wide(sibling_ref[...]))
+    for q in range(chunks):
+        across(0, q).wait_send()
+        across(1, q).wait_send()
+    each(0, peers, lambda k: pass_x(k).wait_send())
+    each(0, peers, lambda k: pass_g(k).wait_send())
+    each(1, peers, lambda k: back_res(k).wait())
+    each(1, peers, lambda k: back_dx(k).wait())
+
+
+def run_expert(s2, cot, lines, slots, weights):
+    length, width = s2.shape
+    experts, shard, total = weights.shape
+    peers = 2 * experts
+    rows = slots.shape[0] // peers
+    hidden = total // 3
+    both = 2 * peers * rows
+    chunks = 4
+    vmem = pl.BlockSpec(memory_space=pltpu.VMEM)
+    low_t, wide_t = jnp.bfloat16, jnp.float32
+    dma = pltpu.SemaphoreType.DMA
+    block = (peers, rows, width)
+    return pl.pallas_call(
+        expert_kernel,
+        in_specs=[vmem] * 4 + [pl.BlockSpec(memory_space=pl.ANY)],
+        out_specs=[vmem] * 3,
+        out_shape=[
+            jax.ShapeDtypeStruct(block, low_t),
+            jax.ShapeDtypeStruct(block, low_t),
+            jax.ShapeDtypeStruct(weights.shape, low_t),
+        ],
+        scratch_shapes=[
+            pltpu.VMEM(block, low_t),
+            pltpu.VMEM(block, low_t),
+            pltpu.VMEM((2,) + block, low_t),
+            pltpu.VMEM((2,) + block, low_t),
+            pltpu.VMEM((experts, 2, shard, total), low_t),
+            pltpu.VMEM((both, hidden), low_t),
+            pltpu.VMEM((both, hidden), low_t),
+            pltpu.VMEM((width, both), low_t),
+            pltpu.VMEM((width, both), low_t),
+            pltpu.VMEM((both, width), wide_t),
+            pltpu.VMEM((experts, 2, shard, total), low_t),
+            pltpu.VMEM((experts, shard, total), low_t),
+            pltpu.VMEM((2, chunks, both // (2 * chunks), width), low_t),
+            pltpu.VMEM((2, chunks, both // (2 * chunks), width), low_t),
+            dma((3,)),
+            dma((2,)),
+        ]
+        + [dma((peers,))] * 8
+        + [dma((2, chunks))] * 2
+        + [dma((peers,))] * 4,
+            cost_estimate=pl.CostEstimate(
+            flops=36 * peers * rows * width * hidden, bytes_accessed=1 << 28, transcendentals=0
+        ),
+        compiler_params=pltpu.CompilerParams(
+            collective_id=2, has_side_effects=True, vmem_limit_bytes=67043328
+        ),
+    )(s2, cot, lines, slots, weights)
 
 
 def forward_kernel(
@@ -286,6 +976,7 @@
     rows_ref,
     cos_ref,
     sin_ref,
+    shard_ref,
     s1_ref,
     qkv_ref,
     lse_ref,
@@ -293,13 +984,19 @@
     mid_ref,
     s2_ref,
     tok_ref,
+    line_ref,
+    expert_ref,
     vt_ref,
     send_ref,
     recv_ref,
     send_sem,
     recv_sem,
+    wsend_sem,
+    wrecv_sem,
 ):
-    greet_partner()
+    greet_group(2 * shard_ref.shape[0])
+    experts = CoreExchange(shard_ref, expert_ref, wsend_sem, wrecv_sem)
+    experts.start()
     blocks = hid_ref.shape[0] // BLOCK
     heads_width = wout_ref.shape[1]
     pairs = heads_width // PAIR
@@ -372,14 +1069,15 @@
         gate = [
             1.0 / (1.0 + jnp.exp(picked[1 - member] - picked[member])) for member in range(2)
         ]
-        tok_ref[rows, :] = jnp.where(
-            lane == GATE, gate[0], jnp.where(lane == GATE + 1, gate[1], tok)
-        )
+        tok = jnp.where(lane == GATE, gate[0], jnp.where(lane == GATE + 1, gate[1], tok))
+        tok_ref[rows, :] = tok
+        line_ref[:, rows] = tok.T[TARGET : TARGET + 8, :]
+    experts.wait()
 
 
 def backward_kernel(
+    res_ref,
     dx_ref,
-    pres_ref,
     slot_ref,
     tok_ref,
     cot_ref,
@@ -395,10 +1093,12 @@
     cos_ref,
     sin_ref,
     own_ref,
+    egrad_ref,
     grad_ref,
     base_ref,
     other_ref,
     big_ref,
+    arrived_ref,
     gsend_ref,
     grecv_ref,
     hsend_ref,
@@ -419,8 +1119,12 @@
     grecv_sem,
     hsend_sem,
     hrecv_sem,
+    esend_sem,
+    erecv_sem,
 ):
-    greet_partner()
+    greet_group(2 * egrad_ref.shape[0])
+    experts = CoreExchange(egrad_ref, arrived_ref, esend_sem, erecv_sem)
+    experts.start()
     tp = lax.axis_index("tp")
     width = dx_ref.shape[1]
     blocks = cot_ref.shape[0] // BLOCK
@@ -428,21 +1132,24 @@
     pairs = heads_width // PAIR
     gain_one = rows_ref[0:1, :]
     gain_two = rows_ref[1:2, :]
-    slot_row = slot_ref[1:2, :]
-    share_row = slot_ref[0:1, :]
+    slot_row = slot_ref[0:1, :]
     order = list(reversed(range(blocks)))
     first = order[0]
     gcopies = {}
     for block in order:
         rows = block_rows(block)
         tok = tok_ref[rows, :]
-        hits = [column(tok, TARGET + member) == slot_row for member in range(2)]
-        onehot = low(jnp.where(hits[0] | hits[1], 1.0, 0.0))
+        onehots = [
+            low(jnp.where(column(tok, TARGET + m) == slot_row, 1.0, 0.0)) for m in range(2)
+        ]
+        placed = [nn_dot(onehot, res_ref[...]) for onehot in onehots]
+        cot_wide = wide(cot_ref[rows, :])
         shares = [
-            jnp.sum(jnp.where(hit, share_row, 0.0), axis=1, keepdims=True) for hit in hits
+            column(tok, GATE + m) * jnp.sum(placed[m] * cot_wide, axis=1, keepdims=True)
+            for m in range(2)
         ]
         high = [wide(low(share)) for share in shares]
-        gsend_ref[block, :, :width] = low(nn_dot(onehot, dx_ref[...]))
+        gsend_ref[block, :, :width] = low(nn_dot(onehots[0] + onehots[1], dx_ref[...]))
         gsend_ref[block, :, width:] = low(
             lane_matrix(
                 tok.shape,
@@ -459,7 +1166,7 @@
         )
         copy.start()
         gcopies[block] = copy
-        placed = nn_dot(onehot, pres_ref[...])
+        placed = column(tok, GATE) * placed[0] + column(tok, GATE + 1) * placed[1]
         slab = slice((block % 2) * BLOCK, (block % 2 + 1) * BLOCK)
 
         @pl.when(tp == block // 2)
@@ -645,9 +1352,10 @@
         grad_ref[slab, :] = gmid_ref[mid_rows, :] + scale * (
             scaled - unit * mean_last(scaled * unit)
         )
-
-
-def run_forward(hid, tok, wqkv, wout, small, rows, cosine, sine):
+    experts.wait()
+
+
+def run_forward(hid, tok, wqkv, wout, small, rows, cosine, sine, shard):
     length, width = hid.shape
     heads_width = wout.shape[1]
     blocks = length // BLOCK
@@ -655,8 +1363,8 @@
     low_t, wide_t = jnp.bfloat16, jnp.float32
     return pl.pallas_call(
         forward_kernel,
-        in_specs=[vmem] * 8,
-        out_specs=[vmem] * 7,
+        in_specs=[vmem] * 9,
+        out_specs=[vmem] * 9,
         out_shape=[
             jax.ShapeDtypeStruct((length, width), low_t),
             jax.ShapeDtypeStruct((length, 3 * heads_width), low_t),
@@ -665,6 +1373,8 @@
             jax.ShapeDtypeStruct((length, width), wide_t),
             jax.ShapeDtypeStruct((length, width), low_t),
             jax.ShapeDtypeStruct((length, PAIR), wide_t),
+            jax.ShapeDtypeStruct((8, length), wide_t),
+            jax.ShapeDtypeStruct(shard.shape, low_t),
         ],
         scratch_shapes=[
             pltpu.VMEM((heads_width, length), low_t),
@@ -672,15 +1382,20 @@
             pltpu.VMEM((blocks, BLOCK, width), low_t),
             pltpu.SemaphoreType.DMA((blocks,)),
             pltpu.SemaphoreType.DMA((blocks,)),
+            pltpu.SemaphoreType.DMA((shard.shape[0],)),
+            pltpu.SemaphoreType.DMA((shard.shape[0],)),
         ],
+        cost_estimate=pl.CostEstimate(
+            flops=16 * length * width * heads_width, bytes_accessed=1 << 27, transcendentals=0
+        ),
         compiler_params=pltpu.CompilerParams(
             collective_id=0, has_side_effects=True, vmem_limit_bytes=60 << 20
         ),
-    )(hid, tok, wqkv, wout, small, rows, cosine, sine)
+    )(hid, tok, wqkv, wout, small, rows, cosine, sine, shard)
 
 
 def run_backward(*operands):
-    dx, tok, cot, own, wout = operands[0], operands[3], operands[4], operands[16], operands[11]
+    cot, own, wout, egrads = operands[4], operands[16], operands[11], operands[17]
     length, width = cot.shape
     heads_width = wout.shape[1]
     blocks = length // BLOCK
@@ -690,13 +1405,14 @@
     dma = pltpu.SemaphoreType.DMA
     return pl.pallas_call(
         backward_kernel,
-        in_specs=[vmem] * 17,
-        out_specs=[vmem] * 4,
+        in_specs=[vmem] * 18,
+        out_specs=[vmem] * 5,
         out_shape=[
             jax.ShapeDtypeStruct((own_rows, width), wide_t),
             jax.ShapeDtypeStruct((own_rows, width), wide_t),
             jax.ShapeDtypeStruct((own_rows, width), low_t),
             jax.ShapeDtypeStruct((width, 4 * heads_width + PAIR), low_t),
+            jax.ShapeDtypeStruct(egrads.shape, low_t),
         ],
         scratch_shapes=[
             pltpu.VMEM((blocks, BLOCK, width + PAIR), low_t),
@@ -719,7 +1435,12 @@
             dma((blocks,)),
             dma((2,)),
             dma((2,)),
+            dma((egrads.shape[0],)),
+            dma((egrads.shape[0],)),
         ],
+        cost_estimate=pl.CostEstimate(
+            flops=32 * length * width * heads_width, bytes_accessed=1 << 27, transcendentals=0
+        ),
         compiler_params=pltpu.CompilerParams(
             collective_id=1, has_side_effects=True, vmem_limit_bytes=60 << 20
         ),
@@ -748,71 +1469,63 @@
     experts = w_expert_in.shape[0]
     route_count = w_router.shape[1]
     capacity = 9 * length // (4 * route_count)
-    blocked = fetch_expert(blocked_weights(w_expert_in, w_expert_out))
     heads_width = w_attn_out.shape[1]
+    planned = lax.axis_size("fsdp") == 16
     small = jnp.concatenate(
-        [attn_norm[:, None], ffn_norm[:, None], w_router, w_const_gate, w_const_value], axis=1
+        [
+            wide(values)
+            for values in (
+                attn_norm[:, None],
+                ffn_norm[:, None],
+                w_router,
+                w_const_gate,
+                w_const_value,
+            )
+        ],
+        axis=1,
     )
     small = jnp.pad(small, ((0, 0), (0, PAIR - small.shape[1])))
-    small = lax.all_gather(small, "tp", axis=0, tiled=True)
-    packed_weights = lax.all_gather(
-        jnp.concatenate([w_qkv.reshape(-1, 3 * heads_width), w_attn_out, small], axis=1),
-        "fsdp",
-        axis=0,
-        tiled=True,
-    )
-    wqkv = packed_weights[:, : 3 * heads_width]
-    wout = packed_weights[:, 3 * heads_width : 4 * heads_width]
-    small = packed_weights[:, 4 * heads_width :]
-    rows = small[:, :8].T.astype(jnp.float32)
-    cosine, sine = (jnp.asarray(table) for table in rotary_tables(length))
+    wqkv_own = w_qkv.reshape(-1, 3 * heads_width)
     kept = (routes < experts) & (dropped == 0)
     target = jnp.where(kept, routes * capacity + slot_rank, -1)
+    blank = jnp.zeros((own_rows, 2), jnp.float32)
     tok = jnp.concatenate(
-        [prev_logits.T, wide(routes).T, wide(target).T], axis=0
-    )
-    tok = gather_columns(tok)
-    tok = jnp.concatenate(
-        [
-            jnp.zeros((ROUTER, length), jnp.float32),
-            tok[:route_count],
-            jnp.zeros((ROUTE - ROUTER - route_count, length), jnp.float32),
-            tok[route_count:],
-            jnp.zeros((PAIR - ROUTE - 4, length), jnp.float32),
-        ],
-        axis=0,
-    ).T
-    hid = gather_rows(hidden)
-    cot = gather_rows(cotangent)
-    s1, qkv, lse, mixed, mid, s2, tok = run_forward(
-        hid, tok, wqkv, wout, small, rows, cosine, sine
-    )
+        [blank, prev_logits, blank, blank, blank, wide(routes), blank, wide(target)], axis=1
+    )
+    tok = jnp.pad(tok, ((0, 0), (0, PAIR - tok.shape[1]))).T
+    blocks, small, rows, tok, hid, cot = (run_gather if planned else gather_plain)(
+        jnp.concatenate([wqkv_own, w_attn_out], axis=1), small, tok, hidden, cotangent
+    )
+    blocks = blocks.reshape(width, -1)
+    wqkv = blocks[:, : 3 * heads_width]
+    wout = blocks[:, 3 * heads_width :]
+    cosine, sine = (jnp.asarray(table) for table in rotary_tables(length))
+    shard_rows, hidden_units = w_expert_out.shape[1:]
+    shard = jnp.concatenate(
+        [w_expert_in.reshape(experts, shard_rows, 2 * hidden_units), w_expert_out], axis=2
+    )
+    s1, qkv, lse, mixed, mid, s2, tok, lines, gathered = run_forward(
+        hid, tok, wqkv, wout, small, rows, cosine, sine, shard
+    )
+    expert_weights = join_weights(gathered, experts)
+    peers = 2 * experts
     half = capacity // 2
-    slot = jnp.arange(experts * half)
-    slot = (slot // half) * capacity + lax.axis_index("tp") * half + slot % half
-    lines = tok[:, TARGET : TARGET + 4].T
-    hits = [lines[member][None, :] == wide(slot)[:, None] for member in range(2)]
-    dispatch = low(hits[0] | hits[1])
-    slot_gate = sum(
-        jnp.sum(jnp.where(hits[member], lines[2 + member][None, :], 0.0), axis=1)
-        for member in range(2)
-    )
-    packed = low(nn_dot(dispatch, s2))
-    gated = low(nn_dot(dispatch, cot) * slot_gate[:, None])
-    arrived = exchange(jnp.concatenate([packed, gated], axis=1), experts)
-    answer, grads_exp = run_expert(arrived, blocked)
-    answer = exchange(answer, experts)
-    grads_exp = return_grads(grads_exp, experts)
-    slot_result = wide(answer[:, :width])
-    slot_share = jnp.sum(slot_result * wide(gated), axis=1)
-    slot_rows = jnp.concatenate(
-        [slot_share[None, :], wide(slot)[None, :], jnp.zeros((6, slot.shape[0]), jnp.float32)],
-        axis=0,
-    )
-    grad_hidden, base, for_other, big = run_backward(
-        answer[:, width:],
-        low(slot_result * slot_gate[:, None]),
-        slot_rows,
+    block = half // 2
+    place = jnp.arange(peers * block)
+    owner = (lax.axis_index("fsdp") + place // block) % peers
+    slot = wide(
+        (owner // 2) * capacity
+        + lax.axis_index("tp") * half
+        + (owner % 2) * block
+        + place % block
+    )
+    results, grad_rows, grads_exp = run_expert(
+        s2, cot, lines, jnp.broadcast_to(slot[:, None], (slot.shape[0], PAIR)), expert_weights
+    )
+    grad_hidden, base, for_other, big, arrived = run_backward(
+        results.reshape(-1, width),
+        grad_rows.reshape(-1, width),
+        jnp.broadcast_to(slot[None, :], (8, slot.shape[0])),
         tok,
         cot,
         mid,
@@ -827,15 +1540,12 @@
         cosine,
         sine,
         hidden,
-    )
-    output = low(base + wide(swap(for_other)))
-    reduced = wide(lax.psum_scatter(big, "fsdp", scatter_dimension=0, tiled=True))
-    grad_qkv = reduced[:, : 3 * heads_width].reshape(w_qkv.shape)
-    grad_attn_out = reduced[:, 3 * heads_width : 4 * heads_width]
-    gain_share = jnp.sum(grad_qkv * wide(w_qkv), axis=(1, 2))
-    last = jnp.concatenate([gain_share[:, None], reduced[:, 4 * heads_width + 1 :]], axis=1)
-    last = own_half(last) + swap(other_half(last))
-    grad_in_exp, grad_out_exp = split_grads(wide(grads_exp))
+        split_grads(grads_exp),
+    )
+    finish = run_finish if planned else finish_plain
+    output, grad_qkv, grad_attn_out, last, grad_in_exp, grad_out_exp = finish(
+        big, wqkv_own, for_other, base, arrived
+    )
     return (
         output,
         grad_hidden,

time: 607 us -> 451 us (0.74)
  Pallas kernels: 181 us -> 411 us
  waiting for transfers between devices: 189 us -> 0 us
  blocking collectives: 121 us -> 0 us
  local copies, waits for them, and re-layouts: 55.9 us -> 28.5 us
  starting transfers between devices: 16.9 us -> 0 us
  between operations: 14.9 us -> 0.94 us
  other arithmetic: 18.8 us -> 6.95 us
    pallas_call x3 -> x5, Pallas kernels: 181 us -> 411 us  [the longest x1 152 us: run_expert(): pl.pallas_call(expert_kernel, in_specs=[vmem] * 4 + [pl.BlockSpec(memory_...]
    all_to_all x2 -> x0, blocking collectives: 117 us -> none  [the longest x1 59.3 us: fetch_expert(): lax.all_to_all(blocked, 'fsdp', 0, 0, axis_index_groups=same_core, tiled=...]
    reduce_scatter x3 -> x0, waiting for transfers between devices: 95.3 us -> none  [the longest x1 77.6 us: shards(): lax.psum_scatter(big, 'fsdp', scatter_dimension=0, tiled=True)]
    all_to_all x2 -> x0, waiting for transfers between devices: 48.7 us -> none  [the longest x1 48.7 us: exchange(): lax.all_to_all(values, 'fsdp', 0, 0, axis_index_groups=whole, tiled=True)]
    ppermute x5 -> x0, waiting for transfers between devices: 34.6 us -> none  [swap(): return lax.ppermute(values, 'tp', [(0, 1), (1, 0)])]
    slice x13 -> x2, local copies, waits for them, and re-layouts: 27.3 us -> 4.79 us  [the longest x1 2.85 us: shards(): wqkv = blocks[:, :3 * heads_width]]
    all_to_all x2 -> x0, starting transfers between devices: 13 us -> none  [the longest x1 6.87 us: return_grads(): lax.all_to_all(grads, 'fsdp', 0, 0, axis_index_groups=same_core, tiled=True)]
    all_gather x3 -> x0, waiting for transfers between devices: 10.1 us -> none  [the longest x1 7.64 us: fetch_expert(): lax.all_gather(got, 'fsdp', axis=1, axis_index_groups=cores, tiled=True)]
  transfers between devices with their start and end apart: 13 -> 0, of which waited for: 6 -> 0; matrix products, arithmetic and copies ran while one was open for 6% -> 0% of each run, Pallas kernels for 25% -> 0%
where the time goes in v3:
time: 451 us; the launch traced here: 448 us
  Pallas kernels  411 us (91%)
  local copies, waits for them, and re-layouts  28.5 us (6%)
  other arithmetic  6.95 us (2%)
    pallas_call x1, Pallas kernels, run_expert(): pl.pallas_call(expert_kernel, in_specs=[vmem] * 4 + [pl.BlockSpec(memory_...  152 us
    pallas_call x1, Pallas kernels, run_backward(): pl.pallas_call(backward_kernel, in_specs=[vmem] * 18, out_specs=[vmem] *...  76.1 us
    pallas_call x1, Pallas kernels, run_finish(): pl.pallas_call(finish_kernel, in_specs=[vmem] * 5, out_specs=[vmem] * 6,...  72.5 us
    pallas_call x1, Pallas kernels, run_forward(): pl.pallas_call(forward_kernel, in_specs=[vmem] * 9, out_specs=[vmem] * 9,...  60.7 us
    pallas_call x1, Pallas kernels, run_gather(): pl.pallas_call(gather_kernel, in_specs=[vmem] * 5, out_specs=[vmem] * 6,...  49.5 us
    unnamed x23, local copies, waits for them, and re-layouts  11.3 us

profile of v3, /device:TPU:12, one launch (start us, length us, event | category | flops | bytes accessed | tf_op | source)
XLA Modules:
  0.0 447.6 jit_solution(7874557786730603898)
XLA Ops:
  0.6 0.0 copy-start.1
  0.7 0.8 bitcast_convert_fusion
  1.4 0.7 convert_bitcast_fusion
  2.1 0.8 fusion.14
  2.9 0.1 copy.49
  3.0 0.1 copy.50
  3.1 0.8 copy.51
  3.8 0.8 copy.52
  4.6 0.7 copy.53
  5.3 0.1 concatenate.16
  5.4 0.6 pad.8.small_ref
  6.0 0.6 broadcast_in_dim.24.slot_ref
  6.6 1.0 concatenate.18
  7.6 0.9 copy.58
  8.5 0.0 copy-start.4
  8.5 1.5 pad_maximum_fusion.1.block_ref
  10.0 0.7 pad_bitcast_fusion.tok_ref
  10.7 0.0 copy-done.4
  10.7 0.9 broadcast_in_dim.12.slot_ref
  11.7 0.0 copy-done.1
  11.7 1.2 reshape.167
  12.9 2.7 pad_maximum_fusion.shard_ref
  15.6 49.5 %shard_map.248 = (bf16[16,48,1536]{2,1,0:T(8,128)(2,1)}, bf16[768,128]{1,0:T(8,128)(2,1)}, f32[8,768]{1,0:T(8,128)}, f32[1024,128]{1,0:T(8,128)}, bf16[1024,768]{1,0:T(8,128)(2,1)}, /*index=5*/bf16[1024,768]{1,0:T(8,128)(2,1)}) custom-call(bf16[48,1536]{1,0:T(8,128)(2,1)} %pad_maximum_fusion.1.block_ref, f32[24,128]{1,0:T(8,128)} %pad.8.small_ref, ...), custom_call_target="tpu_custom_call" | custom-call | tf_op jit(solution)/shard_map/pallas_call | solution.py:445
  65.1 1.9 slice.29.wout_ref
  67.0 2.8 slice.28.wqkv_ref
  69.9 60.7 %shard_map.249 = (bf16[1024,768]{1,0:T(8,128)(2,1)}, bf16[1024,1152]{1,0:T(8,128)(2,1)}, f32[8,1024]{1,0:T(8,128)}, bf16[1024,384]{1,0:T(8,128)(2,1)}, f32[1024,...) custom-call(bf16[1024,768]{1,0:T(8,128)(2,1)} %get-tuple-element.40., ...), custom_call_target="tpu_custom_call" | custom-call | flops 4831838208 | bytes 134217728 | tf_op jit(solution)/shard_map/pallas_call | solution.py:1364
  130.6 152.5 %shard_map.250 = (bf16[16,48,768]{2,1,0:T(8,128)(2,1)}, bf16[16,48,768]{2,1,0:T(8,128)(2,1)}, bf16[8,48,3072]{2,1,0:T(8,128)(2,1)}) custom-call(bf16[1024,768]{1,0:T(8,128)(2,1)} %get-tuple-element.45.s2_ref, bf16[1024,768]{1,0:T(8,128)(2,1)} %get-tuple-element.46.cot_ref, f32[8,1024]{1,0:T(8,128)} %get-tuple-element.47.line_ref, ...), custom_call_target="tpu_custom_call" | custom-call | flops 21743271936 | bytes 268435456 | tf_op jit(solution)/shard_map/pallas_call | solution.py:931
  283.1 76.1 %shard_map.251 = (f32[512,768]{1,0:T(8,128)}, f32[512,768]{1,0:T(8,128)}, bf16[512,768]{1,0:T(8,128)(2,1)}, bf16[768,1664]{1,0:T(8,128)(2,1)}, bf16[8,48,3072]{2,1,0:T(8,128)(2,1)}) custom-call(bf16[768,768]{1,0:T(8,128)(2,1)} %bitcast.19, bf16[768,768]{1,0:T(8,128)(2,1)} %bitcast.20, f32[8,768]{1,0:T(8,128)} %broadcast_in_dim.24.slot_ref, ...), custom_call_target="tpu_custom_call" | custom-call | flops 9663676416 | bytes 134217728 | tf_op jit(solution)/shard_map/pallas_call | solution.py:1406
  359.2 0.0 copy-start.6
  359.2 72.5 %shard_map.252 = (bf16[512,768]{1,0:T(8,128)(2,1)}, f32[48,3,384]{2,1,0:T(4,128)}, f32[48,384]{1,0:T(8,128)}, f32[24,128]{1,0:T(8,128)}, f32[8,48,2,1024]{3,2,1,0:T(2,128)}, /*index=5*/f32[8,48,1024]{2,1,0:T(8,128)}) custom-call(bf16[16,48,1664]{2,1,0:T(8,128)(2,1)} %bitcast.13, bf16[48,1152]{1,0:T(8,128)(2,1)} %bitcast.17, ...), custom_call_target="tpu_custom_call" | custom-call | tf_op jit(solution)/shard_map/pallas_call | solution.py:650
  431.7 0.0 copy-start.2
  431.7 1.5 slice_reduce_fusion
  433.3 0.0 copy-done.6
  433.3 0.5 convert_divide_fusion
  433.8 0.8 slice.26
  434.6 0.7 copy.56
  435.2 0.8 slice.25
  436.0 0.7 copy.55
  436.7 0.8 slice.27
  437.5 0.6 copy.57
  438.1 1.7 copy.54
  439.8 0.0 copy-start.5
  439.8 0.0 copy-start
  439.8 2.2 copy.64
  442.0 0.0 copy-done.2
  442.0 1.1 copy.65
  443.1 0.0 copy-done.5
  443.1 0.6 copy.66
  443.8 0.0 copy-done
  443.8 0.0 copy-start.3
  443.8 1.7 copy.67
  445.4 0.9 copy-done.3
  446.3 1.1 copy.68
  (3 shorter events, 0.0 us)
Async XLA Ops:
  0.6 11.0 %copy-start.1 = (bf16[8,48,2,1024]{3,2,1,0:T(2,128)(2,1)S(1)}, bf16[8,48,2,1024]{3,2,1,0:T(2,128)(2,1)}, u32[]{:S(2)}) copy-start(bf16[8,48,2,1024]{3,2,1,0:T(2,128)(2,1)} %param.30) | copy-start | bytes 4718596
  8.5 2.2 copy-start.4
  359.2 74.1 %copy-start.6 = (bf16[24]{0:T(256)(128)(2,1)S(1)}, bf16[24]{0:T(256)(128)(2,1)}, u32[]{:S(2)}) copy-start(bf16[24]{0:T(256)(128)(2,1)} %param.23) | copy-start | bytes 148
  431.7 10.3 %copy-start.2 = (f32[512,768]{1,0:T(8,128)S(1)}, f32[512,768]{1,0:T(8,128)}, u32[]{:S(2)}) copy-start(f32[512,768]{1,0:T(8,128)} %get-tuple-element.118) | copy-start | bytes 4718596
  439.8 3.4 copy-start.5
  439.8 4.0 copy-start
  443.8 2.5 copy-start.3

commit v4 on v3

--- a/solution.py
+++ b/solution.py
@@ -86,17 +86,17 @@
     return own_core(grads, grads.shape[0] // (2 * experts))
 
 
-def gather_plain(block, small, tok, hid, cot):
+def gather_plain(block, small, tok, hid):
     size = lax.axis_size("fsdp")
     small = lax.all_gather(small, ("fsdp", "tp"), axis=0, tiled=True)
     tok = lax.all_gather(tok, "tp", axis=1, tiled=True).T
+    tok = jnp.pad(tok, ((0, 0), (0, PAIR - tok.shape[1])))
     return (
         lax.all_gather(block, "fsdp", axis=0),
         low(small),
         small.T[:8],
         tok,
         gather_rows(hid),
-        gather_rows(cot),
     )
 
 
@@ -277,13 +277,11 @@
     small_ref,
     tok_ref,
     hid_ref,
-    cot_ref,
     all_ref,
     small_out_ref,
     rows_out_ref,
     tok_out_ref,
     hid_out_ref,
-    cot_out_ref,
     small_all_ref,
     tok_all_ref,
     y_send,
@@ -306,52 +304,44 @@
     own_rows = hid_ref.shape[0]
     greet_group(size)
     partner = {"tp": 1 - tp}
-    small_all_ref[me, tp] = small_ref[...]
     small_y = send_to(small_ref, small_all_ref.at[me, tp], y_send.at[0], y_recv.at[0], partner)
     small_y.start()
     all_ref[me] = block_ref[...]
+    small_all_ref[me, tp] = small_ref[...]
     mine = pl.ds(pl.multiple_of(tp * own_rows, own_rows), own_rows)
     hid_y = send_to(hid_ref, hid_out_ref.at[mine], y_send.at[1], y_recv.at[1], partner)
     tok_y = send_to(tok_ref, tok_all_ref.at[tp], y_send.at[2], y_recv.at[2], partner)
-    cot_y = send_to(cot_ref, cot_out_ref.at[mine], y_send.at[3], y_recv.at[3], partner)
     hid_y.start()
     tok_y.start()
 
     def number(plane, line):
         return plane * 4 + line * 2 + core
 
-    def pieces(number_of, send, recv, slot, device, source=None):
-        first = all_ref.at[number_of] if source is None else source
-        return (
-            send_to(first, all_ref.at[number_of], send.at[0, slot], recv.at[0, slot], device),
-            send_to(
-                small_all_ref.at[number_of],
-                small_all_ref.at[number_of],
-                send.at[1, slot],
-                recv.at[1, slot],
-                device,
-            ),
+    def piece(kind, number_of, send, recv, slot, device):
+        array = small_all_ref if kind else all_ref
+        return send_to(
+            array.at[number_of],
+            array.at[number_of],
+            send.at[kind, slot],
+            recv.at[kind, slot],
+            device,
         )
 
-    def up(step, plane):
-        return pieces(
-            number(plane, x),
-            up_send,
-            up_recv,
-            step,
-            {"fsdp": number(lax.min(z + 1, planes - 1), x)},
-        )
-
-    def down(step, plane):
-        return pieces(
-            number(plane, x), down_send, down_recv, step, {"fsdp": number(lax.max(z - 1, 0), x)}
-        )
-
-    def side(plane, line):
-        return pieces(number(plane, line), x_send, x_recv, plane, {"fsdp": number(z, 1 - x)})
-
-    def sibling(plane, line, parity):
-        return pieces(
+    def up(kind, step, plane):
+        device = {"fsdp": number(lax.min(z + 1, planes - 1), x)}
+        return piece(kind, number(plane, x), up_send, up_recv, step, device)
+
+    def down(kind, step, plane):
+        device = {"fsdp": number(lax.max(z - 1, 0), x)}
+        return piece(kind, number(plane, x), down_send, down_recv, step, device)
+
+    def side(kind, plane, line):
+        device = {"fsdp": number(z, 1 - x)}
+        return piece(kind, number(plane, line), x_send, x_recv, plane, device)
+
+    def sibling(kind, plane, line, parity):
+        return piece(
+            kind,
             plane * 4 + line * 2 + parity,
             core_send,
             core_recv,
@@ -359,84 +349,94 @@
             {"fsdp": me + 1 - 2 * core},
         )
 
-    def run(group, verb):
-        for item in group:
-            getattr(item, verb)()
-
-    def spread(step, plane):
-        run(side(plane, x), "start")
-        run(sibling(plane, x, core), "start")
-
+    def launch(kind):
+        @pl.when(z < planes - 1)
+        def _():
+            up(kind, 0, z).start()
+
+        @pl.when(z > 0)
+        def _():
+            down(kind, 0, z).start()
+
+        side(kind, z, x).start()
+        sibling(kind, z, x, core).start()
+
+    launch(0)
+    hid_out_ref[mine, :] = hid_ref[...]
+    tok_all_ref[tp] = tok_ref[...]
     small_y.wait()
-    hid_out_ref[mine, :] = hid_ref[...]
-
-    @pl.when(z < planes - 1)
-    def _():
-        run(up(0, z), "start")
-
-    @pl.when(z > 0)
-    def _():
-        run(down(0, z), "start")
-
-    spread(0, z)
-    cot_y.start()
-    tok_all_ref[tp] = tok_ref[...]
-    cot_out_ref[mine, :] = cot_ref[...]
+    launch(1)
     for step in range(1, planes):
-
-        @pl.when(z >= step)
-        def _():
-            run(up(step - 1, z - step), "wait_recv")
-
-            @pl.when(z < planes - 1)
+        for kind in range(2):
+
+            @pl.when(z >= step)
             def _():
-                run(up(step, z - step), "start")
-
-            spread(step, z - step)
-
-        @pl.when(z + step < planes)
-        def _():
-            run(down(step - 1, z + step), "wait_recv")
-
-            @pl.when(z > 0)
+                up(kind, step - 1, z - step).wait_recv()
+
+                @pl.when(z < planes - 1)
+                def _():
+                    up(kind, step, z - step).start()
+
+                side(kind, z - step, x).start()
+                sibling(kind, z - step, x, core).start()
+
+            @pl.when(z + step < planes)
             def _():
-                run(down(step, z + step), "start")
-
-            spread(step, z + step)
-
-    for distance in range(planes):
-        plane = lax.rem(z + distance, planes)
-        run(side(plane, 1 - x), "wait_recv")
-        run(sibling(plane, 1 - x, core), "start")
+                down(kind, step - 1, z + step).wait_recv()
+
+                @pl.when(z > 0)
+                def _():
+                    down(kind, step, z + step).start()
+
+                side(kind, z + step, x).start()
+                sibling(kind, z + step, x, core).start()
+
+    for step in range(planes):
+        for kind in range(2):
+
+            @pl.when(z >= step)
+            def _():
+                side(kind, z - step, 1 - x).wait_recv()
+                sibling(kind, z - step, 1 - x, core).start()
+
+            if step > 0:
+
+                @pl.when(z + step < planes)
+                def _():
+                    side(kind, z + step, 1 - x).wait_recv()
+                    sibling(kind, z + step, 1 - x, core).start()
+
     for plane in range(planes):
         for line in range(2):
-            run(sibling(plane, line, 1 - core), "wait_recv")
+            for kind in range(2):
+                sibling(kind, plane, line, 1 - core).wait_recv()
     small_all = small_all_ref[...].reshape(size * 2 * shard, small_ref.shape[1])
     small_out_ref[...] = low(small_all)
     rows_out_ref[...] = small_all.T[:8, :]
     tok_y.wait()
     for part in range(2):
         lanes = slice(part * own_rows, (part + 1) * own_rows)
-        tok_out_ref[lanes, :] = tok_all_ref[part].T
-    for step in range(planes):
-
-        @pl.when(jnp.logical_and(z >= step, z < planes - 1))
-        def _():
-            run(up(step, z - step), "wait_send")
-
-        @pl.when(jnp.logical_and(z + step < planes, z > 0))
-        def _():
-            run(down(step, z + step), "wait_send")
-
-    for plane in range(planes):
-        run(side(plane, x), "wait_send")
-        for line in range(2):
-            run(sibling(plane, line, core), "wait_send")
+        tok_pad = jnp.zeros((PAIR - tok_ref.shape[0], own_rows), jnp.float32)
+        tok_out_ref[lanes, :] = jnp.concatenate([tok_all_ref[part], tok_pad], axis=0).T
+    for kind in range(2):
+        for step in range(planes):
+
+            @pl.when(jnp.logical_and(z >= step, z < planes - 1))
+            def _():
+                up(kind, step, z - step).wait_send()
+
+            @pl.when(jnp.logical_and(z + step < planes, z > 0))
+            def _():
+                down(kind, step, z + step).wait_send()
+
+        for plane in range(planes):
+            side(kind, plane, x).wait_send()
+            for line in range(2):
+                sibling(kind, plane, line, core).wait_send()
     hid_y.wait()
-    cot_y.wait()
-
-
-def run_gather(block, small, tok, hid, cot):
+
+
+def run_gather(block, small, tok, hid):
     size = lax.axis_size("fsdp")
     own_rows, width = hid.shape
     vmem = pl.BlockSpec(memory_space=pltpu.VMEM)
@@ -444,28 +444,27 @@
     dma = pltpu.SemaphoreType.DMA
     return pl.pallas_call(
         gather_kernel,
-        in_specs=[vmem] * 5,
-        out_specs=[vmem] * 6,
+        in_specs=[vmem] * 4,
+        out_specs=[vmem] * 5,
         out_shape=[
             jax.ShapeDtypeStruct((size,) + block.shape, low_t),
             jax.ShapeDtypeStruct((width, PAIR), low_t),
             jax.ShapeDtypeStruct((8, width), wide_t),
             jax.ShapeDtypeStruct((2 * own_rows, PAIR), wide_t),
             jax.ShapeDtypeStruct((2 * own_rows, width), low_t),
-            jax.ShapeDtypeStruct((2 * own_rows, width), low_t),
         ],
         scratch_shapes=[
             pltpu.VMEM((size, 2) + small.shape, wide_t),
             pltpu.VMEM((2,) + tok.shape, wide_t),
-            dma((4,)),
-            dma((4,)),
+            dma((3,)),
+            dma((3,)),
         ]
         + [dma((2, size // 4))] * 6
         + [dma((2, size // 2))] * 2,
         compiler_params=pltpu.CompilerParams(
             collective_id=3, has_side_effects=True, vmem_limit_bytes=60 << 20
         ),
-    )(block, small, tok, hid, cot)
+    )(block, small, tok, hid)
 
 
 def finish_kernel(
@@ -548,9 +547,10 @@
             {"fsdp": lax.max(z - 1, 0) * 4 + x * 2 + core},
         )
 
-    for plane in range(planes):
+    order = [planes - 1, 0, 2, 1]
+    for plane in order:
         to_core(plane, 1 - x).start()
-    for plane in range(planes):
+    for plane in order:
         to_core(plane, x).start()
     out_y = send_to(other_ref, y_ref, y_send.at[0], y_recv.at[0], partner)
     out_y.start()
@@ -559,10 +559,10 @@
         to_core(plane, line).wait_recv()
         return wide(big_ref[plane * 4 + line * 2 + core]) + wide(core_ref[plane * 2 + line])
 
-    for plane in range(planes):
+    for plane in order:
         sum_ref[plane] = low(joined(plane, 1 - x))
         to_side(plane).start()
-    for plane in range(planes):
+    for plane in order:
         acc_ref[plane] = joined(plane, x)
     experts, shard, total = expert_ref.shape
     hidden = total // 3
@@ -574,7 +574,8 @@
         down_ref[e] = values[:, 2 * hidden :]
 
     each(0, experts, lay_out)
-    for plane in range(planes):
+
+    def ready(plane):
         to_side(plane).wait_recv()
         acc_ref[plane] += wide(side_ref[plane])
 
@@ -600,9 +601,18 @@
             dsend_ref[plane] = low(acc_ref[plane])
             to_down(plane).start()
 
-    for step in range(planes):
-        rise(planes - 1 - step)
-        fall(step)
+    ready(3)
+    rise(3)
+    ready(0)
+    fall(0)
+    ready(2)
+    rise(2)
+    ready(1)
+    fall(1)
+    rise(1)
+    fall(2)
+    rise(0)
+    fall(3)
     values = acc_ref[z]
     flat = values[:, : 3 * heads_width]
     for part in range(3):
@@ -698,6 +708,7 @@
     w_ref,
     gate_ref,
     up_ref,
+    act_ref,
     xt_ref,
     gt_ref,
     acc_ref,
@@ -726,29 +737,29 @@
     total = peers * rows
     hidden = gate_ref.shape[1]
     tiles = hidden // TILE
-    chunks = ysend_ref.shape[1]
-    chunk = total // chunks
-    group = peers // chunks
     me = lax.axis_index("fsdp")
     tp = lax.axis_index("tp")
     rank = lax.rem(me, peers)
     core = lax.rem(rank, 2)
     start = me - rank
 
-    def ahead(k):
-        return start + lax.rem(rank + k, peers)
-
-    def behind(k):
-        return start + lax.rem(rank + peers - k, peers)
+    def peer(k):
+        other = start
+        bit = 1
+        while bit < peers:
+            ours, theirs = lax.rem(rank // bit, 2), lax.rem(k // bit, 2)
+            other = other + bit * (ours + theirs - 2 * ours * theirs)
+            bit *= 2
+        return {"fsdp": other}
 
     partner = {"tp": 1 - tp}
     sibling = {"fsdp": start + rank + 1 - 2 * core}
 
     def out_x(k):
-        return send_to(xs_ref.at[k], x_ref.at[0, k], xs_sem.at[k], xr_sem.at[k], {"fsdp": ahead(k)})
+        return send_to(xs_ref.at[k], x_ref.at[0, k], xs_sem.at[k], xr_sem.at[k], peer(k))
 
     def out_g(k):
-        return send_to(gs_ref.at[k], g_ref.at[0, k], gs_sem.at[k], gr_sem.at[k], {"fsdp": ahead(k)})
+        return send_to(gs_ref.at[k], g_ref.at[0, k], gs_sem.at[k], gr_sem.at[k], peer(k))
 
     def pass_x(k):
         return send_to(x_ref.at[0, k], x_ref.at[1, k], xfs_sem.at[k], xfr_sem.at[k], partner)
@@ -756,54 +767,76 @@
     def pass_g(k):
         return send_to(g_ref.at[0, k], g_ref.at[1, k], gfs_sem.at[k], gfr_sem.at[k], partner)
 
-    def across(index, q):
+    def across(index, k):
         return send_to(
-            ysend_ref.at[index, q],
-            yrecv_ref.at[index, q],
-            ys_sem.at[index, q],
-            yr_sem.at[index, q],
+            ysend_ref.at[index, k],
+            yrecv_ref.at[index, k],
+            ys_sem.at[index, k],
+            yr_sem.at[index, k],
             partner,
         )
 
-    def back_res(k):
-        return send_to(
-            xs_ref.at[k], res_out_ref.at[k], rs_sem.at[k], rr_sem.at[k], {"fsdp": behind(k)}
-        )
-
-    def back_dx(k):
-        return send_to(
-            gs_ref.at[k], dx_out_ref.at[k], ds_sem.at[k], dr_sem.at[k], {"fsdp": behind(k)}
-        )
+    def back(index, k):
+        if index == 0:
+            return send_to(xs_ref.at[k], res_out_ref.at[k], rs_sem.at[k], rr_sem.at[k], peer(k))
+        return send_to(gs_ref.at[k], dx_out_ref.at[k], ds_sem.at[k], dr_sem.at[k], peer(k))
+
+    def return_order(body):
+        def step(j, carry):
+            body(8 + 2 * j)
+            body(4 + j)
+            body(9 + 2 * j)
+            return carry
+
+        lax.fori_loop(0, 4, step, 0)
+        for k in (2, 3, 1, 0):
+            body(k)
+
+    def join(index, k):
+        across(index, k).wait_recv()
+        own = xs_ref if index == 0 else gs_ref
+        own[k] = low(wide(own[k]) + wide(yrecv_ref[index, k]))
+        back(index, k).start()
+
+    def join_some(index, tile):
+        join(index, 8 + 2 * tile)
+        join(index, 4 + tile)
+        join(index, 9 + 2 * tile)
+
+    def join_last(index):
+        for k in (2, 3, 1):
+            join(index, k)
+        across(index, 0).wait_recv()
+        own, target = (xs_ref, res_out_ref) if index == 0 else (gs_ref, dx_out_ref)
+        target[0] = low(wide(own[0]) + wide(yrecv_ref[index, 0]))
 
     greet_group(peers)
     here = pltpu.make_async_copy(weight_ref, w_ref.at[:, core], w_sem.at[0])
     here.start()
     there = send_to(weight_ref, w_ref.at[:, core], w_sem.at[1], w_sem.at[2], sibling)
-    there.start()
-
     half = total // 2
     halves = []
     for part in range(2):
         blocks = slice(part * peers // 2, (part + 1) * peers // 2)
         ids = slot_ref[part * half : (part + 1) * half, 0:1]
         hits = [line_ref[m : m + 1, :] == ids for m in range(2)]
-        gate = sum(
-            jnp.sum(jnp.where(hits[m], line_ref[2 + m : 3 + m, :], 0.0), axis=1, keepdims=True)
-            for m in range(2)
-        )
         onehot = low(jnp.where(hits[0] | hits[1], 1.0, 0.0))
         xs_ref[blocks] = low(nn_dot(onehot, s2_ref[...])).reshape(peers // 2, rows, width)
         if part == 0:
             x_ref[0, 0] = xs_ref[0]
             pass_x(0).start()
         each(max(1, part * peers // 2), (part + 1) * peers // 2, lambda k: out_x(k).start())
-        halves.append((blocks, onehot, gate))
+        halves.append((blocks, onehot, hits))
+    there.start()
     for part in range(2):
-        blocks, onehot, gate = halves[part]
+        blocks, onehot, hits = halves[part]
+        gate = sum(
+            jnp.sum(jnp.where(hits[m], line_ref[2 + m : 3 + m, :], 0.0), axis=1, keepdims=True)
+            for m in range(2)
+        )
         gs_ref[blocks] = low(nn_dot(onehot, cot_ref[...]) * gate).reshape(peers // 2, rows, width)
         if part == 0:
             g_ref[0, 0] = gs_ref[0]
-            pass_g(0).start()
         each(max(1, part * peers // 2), (part + 1) * peers // 2, lambda k: out_g(k).start())
 
     def forward_x(k):
@@ -811,6 +844,7 @@
         pass_x(k).start()
 
     each(1, peers, forward_x)
+    pass_g(0).start()
     here.wait()
     send_to(weight_ref, w_ref.at[:, 1 - core], w_sem.at[1], w_sem.at[2], sibling).wait_recv()
     there.wait_send()
@@ -825,12 +859,14 @@
 
     def forward_tile(tile, carry):
         lanes = pl.multiple_of(tile * TILE, TILE)
+        here_lanes = pl.ds(lanes, TILE)
         x = x_ref[...].reshape(2 * total, width)
         gate = nn_dot(x, weights(0, lanes))
         up = nn_dot(x, weights(1, lanes))
-        gate_ref[:, pl.ds(lanes, TILE)] = low(gate)
-        up_ref[:, pl.ds(lanes, TILE)] = low(up)
+        gate_ref[:, here_lanes] = low(gate)
+        up_ref[:, here_lanes] = low(up)
         act = low(gate / (1.0 + jnp.exp(-gate)) * up)
+        act_ref[:, here_lanes] = act
         acc_ref[...] += nt_dot(act, weights(2, lanes))
 
         def forward_g(k):
@@ -845,75 +881,65 @@
     lax.fori_loop(0, tiles, forward_tile, 0)
     each(1, peers, lambda k: out_x(k).wait_send())
     xs_ref[...] = low(acc_ref[:total, :]).reshape(peers, rows, width)
-    ysend_ref[0] = low(acc_ref[total:, :]).reshape(chunks, chunk, width)
-    for q in range(chunks):
-        across(0, q).start()
+    ysend_ref[0] = low(acc_ref[total:, :]).reshape(peers, rows, width)
+    return_order(lambda k: across(0, k).start())
     xt_ref[...] = x_ref[...].reshape(2 * total, width).T
     acc_ref[...] = jnp.zeros_like(acc_ref)
     each(0, peers, lambda k: pass_g(k).wait_recv())
+
+    def slope_tile(tile, carry):
+        lanes = pl.multiple_of(tile * TILE, TILE)
+        here_lanes = pl.ds(lanes, TILE)
+        gate = wide(gate_ref[:, here_lanes])
+        up = wide(up_ref[:, here_lanes])
+        sig = 1.0 / (1.0 + jnp.exp(-gate))
+        d_act = nn_dot(g_ref[...].reshape(2 * total, width), weights(2, lanes))
+        d_up = low(d_act * gate * sig)
+        d_gate = low(d_act * up * sig * (1.0 + gate * (1.0 - sig)))
+        gate_ref[:, here_lanes] = d_gate
+        up_ref[:, here_lanes] = d_up
+        acc_ref[...] += nt_dot(d_gate, weights(0, lanes)) + nt_dot(d_up, weights(1, lanes))
+        join_some(0, tile)
+        return carry
+
+    lax.fori_loop(0, tiles, slope_tile, 0)
+    join_last(0)
+    each(1, peers, lambda k: out_g(k).wait_send())
+    gs_ref[...] = low(acc_ref[:total, :]).reshape(peers, rows, width)
+    ysend_ref[1] = low(acc_ref[total:, :]).reshape(peers, rows, width)
+    return_order(lambda k: across(1, k).start())
     gt_ref[...] = g_ref[...].reshape(2 * total, width).T
 
-    def backward_tile(tile, carry):
+    def weight_tile(tile, carry):
         lanes = pl.multiple_of(tile * TILE, TILE)
-        gate = wide(gate_ref[:, pl.ds(lanes, TILE)])
-        up = wide(up_ref[:, pl.ds(lanes, TILE)])
-        sig = 1.0 / (1.0 + jnp.exp(-gate))
-        silu = gate * sig
-        act = low(silu * up)
-        d_act = nn_dot(g_ref[...].reshape(2 * total, width), weights(2, lanes))
-        d_up = low(d_act * silu)
-        d_gate = low(d_act * up * sig * (1.0 + gate * (1.0 - sig)))
-        acc_ref[...] += nt_dot(d_gate, weights(0, lanes)) + nt_dot(d_up, weights(1, lanes))
+        here_lanes = pl.ds(lanes, TILE)
 
         def keep(which, values):
             grads_ref[
                 :, :, :, pl.ds(pl.multiple_of(which * hidden + lanes, TILE), TILE)
             ] = low(values).reshape(peers // 2, 2, rows, TILE)
 
-        keep(0, nn_dot(xt_ref[...], d_gate))
-        keep(1, nn_dot(xt_ref[...], d_up))
-        keep(2, nn_dot(gt_ref[...], act))
-
-        @pl.when(tile == 1)
-        def _():
-            for q in range(chunks):
-                across(0, q).wait_recv()
-                part = slice(q * group, (q + 1) * group)
-                xs_ref[part] = low(
-                    wide(xs_ref[part]) + wide(yrecv_ref[0, q]).reshape(group, rows, width)
-                )
-            res_out_ref[0] = xs_ref[0]
-            each(1, peers, lambda k: back_res(k).start())
-
+        keep(0, nn_dot(xt_ref[...], gate_ref[:, here_lanes]))
+        keep(1, nn_dot(xt_ref[...], up_ref[:, here_lanes]))
+        keep(2, nn_dot(gt_ref[...], act_ref[:, here_lanes]))
+        join_some(1, tile)
         return carry
 
-    lax.fori_loop(0, tiles, backward_tile, 0)
-    for q in range(chunks):
-        ysend_ref[1, q] = low(acc_ref[total + q * chunk : total + (q + 1) * chunk, :])
-        across(1, q).start()
+    lax.fori_loop(0, tiles, weight_tile, 0)
+    join_last(1)
     swap_grads = send_to(
         grads_ref.at[:, 1 - core], sibling_ref, grad_sem.at[0], grad_sem.at[1], sibling
     )
     swap_grads.start()
-    each(1, peers, lambda k: out_g(k).wait_send())
-    for q in range(chunks):
-        across(1, q).wait_recv()
-        part = slice(q * group, (q + 1) * group)
-        gs_ref[part] = low(
-            acc_ref[q * chunk : (q + 1) * chunk, :] + wide(yrecv_ref[1, q])
-        ).reshape(group, rows, width)
-        if q == 0:
-            dx_out_ref[0] = gs_ref[0]
-        each(max(1, q * group), (q + 1) * group, lambda k: back_dx(k).start())
+    each(0, peers, lambda k: pass_x(k).wait_send())
+    each(0, peers, lambda k: pass_g(k).wait_send())
+    for index in range(2):
+        each(0, peers, lambda k: across(index, k).wait_send())
+        each(1, peers, lambda k: back(index, k).wait_send())
     swap_grads.wait()
     grads_out_ref[...] = low(wide(grads_ref[:, core]) + wide(sibling_ref[...]))
-    for q in range(chunks):
-        across(0, q).wait_send()
-        across(1, q).wait_send()
-    each(0, peers, lambda k: pass_x(k).wait_send())
-    each(0, peers, lambda k: pass_g(k).wait_send())
-    each(1, peers, lambda k: back_res(k).wait())
-    each(1, peers, lambda k: back_dx(k).wait())
+    for index in range(2):
+        each(1, peers, lambda k: back(index, k).wait_recv())
 
 
 def run_expert(s2, cot, lines, slots, weights):
@@ -923,7 +949,6 @@
     rows = slots.shape[0] // peers
     hidden = total // 3
     both = 2 * peers * rows
-    chunks = 4
     vmem = pl.BlockSpec(memory_space=pltpu.VMEM)
     low_t, wide_t = jnp.bfloat16, jnp.float32
     dma = pltpu.SemaphoreType.DMA
@@ -945,22 +970,20 @@
             pltpu.VMEM((experts, 2, shard, total), low_t),
             pltpu.VMEM((both, hidden), low_t),
             pltpu.VMEM((both, hidden), low_t),
+            pltpu.VMEM((both, hidden), low_t),
             pltpu.VMEM((width, both), low_t),
             pltpu.VMEM((width, both), low_t),
             pltpu.VMEM((both, width), wide_t),
             pltpu.VMEM((experts, 2, shard, total), low_t),
             pltpu.VMEM((experts, shard, total), low_t),
-            pltpu.VMEM((2, chunks, both // (2 * chunks), width), low_t),
-            pltpu.VMEM((2, chunks, both // (2 * chunks), width), low_t),
+            pltpu.VMEM((2,) + block, low_t),
+            pltpu.VMEM((2,) + block, low_t),
             dma((3,)),
             dma((2,)),
         ]
         + [dma((peers,))] * 8
-        + [dma((2, chunks))] * 2
+        + [dma((2, peers))] * 2
         + [dma((peers,))] * 4,
-            cost_estimate=pl.CostEstimate(
-            flops=36 * peers * rows * width * hidden, bytes_accessed=1 << 28, transcendentals=0
-        ),
         compiler_params=pltpu.CompilerParams(
             collective_id=2, has_side_effects=True, vmem_limit_bytes=67043328
         ),
@@ -977,6 +1000,7 @@
     cos_ref,
     sin_ref,
     shard_ref,
+    cot_ref,
     s1_ref,
     qkv_ref,
     lse_ref,
@@ -986,6 +1010,7 @@
     tok_ref,
     line_ref,
     expert_ref,
+    cot_all_ref,
     vt_ref,
     send_ref,
     recv_ref,
@@ -993,10 +1018,16 @@
     recv_sem,
     wsend_sem,
     wrecv_sem,
+    cot_sem,
 ):
     greet_group(2 * shard_ref.shape[0])
+    own_rows = cot_ref.shape[0]
+    mine = pl.ds(pl.multiple_of(lax.axis_index("tp") * own_rows, own_rows), own_rows)
+    cot_copy = to_partner(cot_ref, cot_all_ref.at[mine], cot_sem.at[0], cot_sem.at[1])
+    cot_copy.start()
     experts = CoreExchange(shard_ref, expert_ref, wsend_sem, wrecv_sem)
     experts.start()
+    cot_all_ref[mine, :] = cot_ref[...]
     blocks = hid_ref.shape[0] // BLOCK
     heads_width = wout_ref.shape[1]
     pairs = heads_width // PAIR
@@ -1072,6 +1103,7 @@
         tok = jnp.where(lane == GATE, gate[0], jnp.where(lane == GATE + 1, gate[1], tok))
         tok_ref[rows, :] = tok
         line_ref[:, rows] = tok.T[TARGET : TARGET + 8, :]
+    cot_copy.wait()
     experts.wait()
 
 
@@ -1355,7 +1387,7 @@
     experts.wait()
 
 
-def run_forward(hid, tok, wqkv, wout, small, rows, cosine, sine, shard):
+def run_forward(hid, tok, wqkv, wout, small, rows, cosine, sine, shard, cot):
     length, width = hid.shape
     heads_width = wout.shape[1]
     blocks = length // BLOCK
@@ -1363,8 +1395,8 @@
     low_t, wide_t = jnp.bfloat16, jnp.float32
     return pl.pallas_call(
         forward_kernel,
-        in_specs=[vmem] * 9,
-        out_specs=[vmem] * 9,
+        in_specs=[vmem] * 10,
+        out_specs=[vmem] * 10,
         out_shape=[
             jax.ShapeDtypeStruct((length, width), low_t),
             jax.ShapeDtypeStruct((length, 3 * heads_width), low_t),
@@ -1375,6 +1407,7 @@
             jax.ShapeDtypeStruct((length, PAIR), wide_t),
             jax.ShapeDtypeStruct((8, length), wide_t),
             jax.ShapeDtypeStruct(shard.shape, low_t),
+            jax.ShapeDtypeStruct((length, width), low_t),
         ],
         scratch_shapes=[
             pltpu.VMEM((heads_width, length), low_t),
@@ -1384,6 +1417,7 @@
             pltpu.SemaphoreType.DMA((blocks,)),
             pltpu.SemaphoreType.DMA((shard.shape[0],)),
             pltpu.SemaphoreType.DMA((shard.shape[0],)),
+            pltpu.SemaphoreType.DMA((2,)),
         ],
         cost_estimate=pl.CostEstimate(
             flops=16 * length * width * heads_width, bytes_accessed=1 << 27, transcendentals=0
@@ -1391,7 +1425,7 @@
         compiler_params=pltpu.CompilerParams(
             collective_id=0, has_side_effects=True, vmem_limit_bytes=60 << 20
         ),
-    )(hid, tok, wqkv, wout, small, rows, cosine, sine, shard)
+    )(hid, tok, wqkv, wout, small, rows, cosine, sine, shard, cot)
 
 
 def run_backward(*operands):
@@ -1492,9 +1526,9 @@
     tok = jnp.concatenate(
         [blank, prev_logits, blank, blank, blank, wide(routes), blank, wide(target)], axis=1
     )
-    tok = jnp.pad(tok, ((0, 0), (0, PAIR - tok.shape[1]))).T
-    blocks, small, rows, tok, hid, cot = (run_gather if planned else gather_plain)(
-        jnp.concatenate([wqkv_own, w_attn_out], axis=1), small, tok, hidden, cotangent
+    tok = jnp.pad(tok, ((0, 0), (0, 32 - tok.shape[1]))).T
+    blocks, small, rows, tok, hid = (run_gather if planned else gather_plain)(
+        jnp.concatenate([wqkv_own, w_attn_out], axis=1), small, tok, hidden
     )
     blocks = blocks.reshape(width, -1)
     wqkv = blocks[:, : 3 * heads_width]
@@ -1504,15 +1538,15 @@
     shard = jnp.concatenate(
         [w_expert_in.reshape(experts, shard_rows, 2 * hidden_units), w_expert_out], axis=2
     )
-    s1, qkv, lse, mixed, mid, s2, tok, lines, gathered = run_forward(
-        hid, tok, wqkv, wout, small, rows, cosine, sine, shard
+    s1, qkv, lse, mixed, mid, s2, tok, lines, gathered, cot = run_forward(
+        hid, tok, wqkv, wout, small, rows, cosine, sine, shard, cotangent
     )
     expert_weights = join_weights(gathered, experts)
     peers = 2 * experts
     half = capacity // 2
     block = half // 2
     place = jnp.arange(peers * block)
-    owner = (lax.axis_index("fsdp") + place // block) % peers
+    owner = (lax.axis_index("fsdp") % peers) ^ (place // block)
     slot = wide(
         (owner // 2) * capacity
         + lax.axis_index("tp") * half

time: 451 us -> 406 us (0.900)
  Pallas kernels: 411 us -> 366 us
    pallas_call x2, Pallas kernels: 110 us -> 91.9 us  [the longest x1 64 us: run_forward(): pl.pallas_call(forward_kernel, in_specs=[vmem] * 10, out_specs=[vmem] * 1...]
    pallas_call x1, Pallas kernels: 72.5 us -> 60.2 us  [run_finish(): pl.pallas_call(finish_kernel, in_specs=[vmem] * 5, out_specs=[vmem] * 6,...]
    pallas_call x1, Pallas kernels: 152 us -> 142 us  [run_expert(): pl.pallas_call(expert_kernel, in_specs=[vmem] * 4 + [pl.BlockSpec(memory_...]
    pallas_call x1, Pallas kernels: 76.1 us -> 71.2 us  [run_backward(): pl.pallas_call(backward_kernel, in_specs=[vmem] * 18, out_specs=[vmem] *...]
where the time goes in v4:
time: 406 us; the launch traced here: 402 us
  Pallas kernels  366 us (90%)
  local copies, waits for them, and re-layouts  30 us (7%)
  other arithmetic  5.79 us (1%)
    pallas_call x1, Pallas kernels, run_expert(): pl.pallas_call(expert_kernel, in_specs=[vmem] * 4 + [pl.BlockSpec(memory_...  142 us
    pallas_call x1, Pallas kernels, run_backward(): pl.pallas_call(backward_kernel, in_specs=[vmem] * 18, out_specs=[vmem] *...  71.2 us
    pallas_call x1, Pallas kernels, run_forward(): pl.pallas_call(forward_kernel, in_specs=[vmem] * 10, out_specs=[vmem] * 1...  64 us
    pallas_call x1, Pallas kernels, run_finish(): pl.pallas_call(finish_kernel, in_specs=[vmem] * 5, out_specs=[vmem] * 6,...  60.2 us
    pallas_call x1, Pallas kernels, run_gather(): pl.pallas_call(gather_kernel, in_specs=[vmem] * 4, out_specs=[vmem] * 5,...  28 us
    unnamed x23, local copies, waits for them, and re-layouts  11.3 us

profile of v4, /device:TPU:12, one launch (start us, length us, event | category | flops | bytes accessed | tf_op | source)
XLA Modules:
  0.0 402.3 jit_solution(5991980907359932942)
XLA Ops:
  0.6 0.0 copy-start.4
  0.7 0.7 bitcast_convert_fusion
  1.4 0.7 convert_bitcast_fusion
  2.1 0.8 fusion.13
  2.9 0.1 copy.49
  2.9 0.1 copy.50
  3.0 0.8 copy.51
  3.8 0.8 copy.52
  4.6 0.7 copy.53
  5.3 0.1 concatenate.16
  5.4 0.6 pad.8.small_ref
  6.0 0.6 broadcast_in_dim.24.slot_ref
  6.6 1.0 concatenate.18
  7.6 0.6 pad_bitcast_fusion.tok_ref
  8.2 0.9 copy.58
  9.1 0.0 copy-start.3
  9.1 1.5 pad_maximum_fusion.1.block_ref
  10.6 0.0 copy-done.3
  10.6 0.9 broadcast_in_dim.12.slot_ref
  11.5 2.9 reshape.145
  14.4 0.0 copy-done.4
  14.4 1.6 pad_maximum_fusion.shard_ref
  16.0 28.0 %shard_map.248 = (bf16[16,48,1536]{2,1,0:T(8,128)(2,1)}, bf16[768,128]{1,0:T(8,128)(2,1)}, f32[8,768]{1,0:T(8,128)}, f32[1024,128]{1,0:T(8,128)}, bf16[1024,768]{1,0:T(8,128)(2,1)}) custom-call(bf16[48,1536]{1,0:T(8,128)(2,1)} %pad_maximum_fusion.1.block_ref, f32[24,128]{1,0:T(8,128)} %pad.8.small_ref, f32[32,512]{1,0:T(8,128)} %pad_bitcast_fusion.tok_ref, ...), custom_call_target="tpu_custom_call" | custom-call | tf_op jit(solution)/shard_map/pallas_call | solution.py:445
  44.0 1.9 slice.29.wout_ref
  45.9 2.8 slice.28.wqkv_ref
  48.8 64.0 %shard_map.249 = (bf16[1024,768]{1,0:T(8,128)(2,1)}, bf16[1024,1152]{1,0:T(8,128)(2,1)}, f32[8,1024]{1,0:T(8,128)}, bf16[1024,384]{1,0:T(8,128)(2,1)}, f32[1024,...) custom-call(bf16[1024,768]{1,0:T(8,128)(2,1)} %get-tuple-element.40., ...), custom_call_target="tpu_custom_call" | custom-call | flops 4831838208 | bytes 134217728 | tf_op jit(solution)/shard_map/pallas_call | solution.py:1396
  112.8 142.1 %shard_map.250 = (bf16[16,48,768]{2,1,0:T(8,128)(2,1)}, bf16[16,48,768]{2,1,0:T(8,128)(2,1)}, bf16[8,48,3072]{2,1,0:T(8,128)(2,1)}) custom-call(bf16[1024,768]{1,0:T(8,128)(2,1)} %get-tuple-element.45.s2_ref, bf16[1024,768]{1,0:T(8,128)(2,1)} %get-tuple-element.46.cot_ref, f32[8,1024]{1,0:T(8,128)} %get-tuple-element.47.line_ref, ...), custom_call_target="tpu_custom_call" | custom-call | tf_op jit(solution)/shard_map/pallas_call | solution.py:956
  254.9 71.2 %shard_map.251 = (f32[512,768]{1,0:T(8,128)}, f32[512,768]{1,0:T(8,128)}, bf16[512,768]{1,0:T(8,128)(2,1)}, bf16[768,1664]{1,0:T(8,128)(2,1)}, bf16[8,48,3072]{2,1,0:T(8,128)(2,1)}) custom-call(bf16[768,768]{1,0:T(8,128)(2,1)} %bitcast.19, bf16[768,768]{1,0:T(8,128)(2,1)} %bitcast.20, f32[8,768]{1,0:T(8,128)} %broadcast_in_dim.24.slot_ref, ...), custom_call_target="tpu_custom_call" | custom-call | flops 9663676416 | bytes 134217728 | tf_op jit(solution)/shard_map/pallas_call | solution.py:1440
  326.2 0.0 copy-start.6
  326.2 60.2 %shard_map.252 = (bf16[512,768]{1,0:T(8,128)(2,1)}, f32[48,3,384]{2,1,0:T(4,128)}, f32[48,384]{1,0:T(8,128)}, f32[24,128]{1,0:T(8,128)}, f32[8,48,2,1024]{3,2,1,0:T(2,128)}, /*index=5*/f32[8,48,1024]{2,1,0:T(8,128)}) custom-call(bf16[16,48,1664]{2,1,0:T(8,128)(2,1)} %bitcast.13, bf16[48,1152]{1,0:T(8,128)(2,1)} %bitcast.17, ...), custom_call_target="tpu_custom_call" | custom-call | tf_op jit(solution)/shard_map/pallas_call | solution.py:660
  386.4 0.0 copy-start.1
  386.4 1.5 slice_reduce_fusion
  387.9 0.0 copy-done.6
  387.9 0.5 convert_divide_fusion
  388.5 0.8 slice.26
  389.2 0.7 copy.56
  389.9 0.8 slice.25
  390.7 0.7 copy.55
  391.4 0.8 slice.27
  392.1 0.6 copy.57
  392.8 1.7 copy.54
  394.4 0.0 copy-start.5
  394.4 0.0 copy-start
  394.4 2.2 copy.64
  396.6 0.0 copy-done.1
  396.7 1.1 copy.65
  397.8 0.0 copy-done.5
  397.8 0.6 copy.66
  398.4 0.0 copy-done
  398.4 0.0 copy-start.2
  398.4 1.7 copy.67
  400.1 0.9 copy-done.2
  401.0 1.1 copy.68
  (3 shorter events, 0.0 us)
Async XLA Ops:
  0.6 13.8 %copy-start.4 = (bf16[8,48,1024]{2,1,0:T(8,128)(2,1)S(1)}, bf16[8,48,1024]{2,1,0:T(8,128)(2,1)}, u32[]{:S(2)}) copy-start(bf16[8,48,1024]{2,1,0:T(8,128)(2,1)} %param.31) | copy-start | bytes 2359300
  9.1 1.5 copy-start.3
  326.2 61.8 %copy-start.6 = (bf16[24]{0:T(256)(128)(2,1)S(1)}, bf16[24]{0:T(256)(128)(2,1)}, u32[]{:S(2)}) copy-start(bf16[24]{0:T(256)(128)(2,1)} %param.23) | copy-start | bytes 148
  386.4 10.3 %copy-start.1 = (f32[512,768]{1,0:T(8,128)S(1)}, f32[512,768]{1,0:T(8,128)}, u32[]{:S(2)}) copy-start(f32[512,768]{1,0:T(8,128)} %get-tuple-element.118) | copy-start | bytes 4718596
  394.4 3.4 copy-start.5
  394.4 4.0 copy-start
  398.4 2.5 copy-start.2
